TPU v7x, 128 devices: a whole 4x4x4 slice. The times are simulated.
128 devices in a mesh: row: 8 (over y, z_lo), col: 16 (over x, z_hi, core).
Axes of the slice: x: 4, y: 4, z: 4 (z_hi: 2, z_lo: 2; z = z_hi * 2 + z_lo), core: 2. Of those that a mesh axis runs over, the one named last changes fastest.
Arguments:
- stream_in: bfloat16 [2048, 8192], P('col', 'row'), may hold values from -6 to 6
- grad_out: bfloat16 [2048, 8192], P('col', 'row'), may hold values from -6 to 6
- gate_pre: bfloat16 [2048, 14336], P('row', 'col'), may hold values from -6 to 6
- up_pre: bfloat16 [2048, 14336], P('row', 'col'), may hold values from -6 to 6
- keep_mask: int32 [2048, 14336], P('row', 'col'), may hold values 0 or 1
- segment_ids: int32 [2048], P('row'), may hold values from 0 to 15, never falling along the last dimension, each value on 1 to 256 neighbouring positions
- norm_gain: float32 [8192], P('row'), may hold values from 0.25 to 1.75
- w_gate: bfloat16 [8192, 14336], P('row', 'col'), may hold values from -0.0625 to 0.0625
- w_up: bfloat16 [8192, 14336], P('row', 'col'), may hold values from -0.0625 to 0.0625
- w_down: bfloat16 [14336, 8192], P('col', 'row'), may hold values from -0.046875 to 0.046875
Outputs:
- grad_in: bfloat16 [2048, 8192], P('col', 'row')
- grad_gate: bfloat16 [8192, 14336], P('row', 'col')
- grad_up: bfloat16 [8192, 14336], P('row', 'col')
- grad_down: bfloat16 [14336, 8192], P('col', 'row')
Inputs may be any that keep to these rules, and one draw needn't show every extreme that they name: `segment_ids`: never falls along the tokens; each of the 16 documents has 1 to 256 tokens, one exactly 256.
All inputs are finite; a program needn't handle non-finite values. No bound on the sum of `keep_mask` on one device may be relied on, other than what follows from the above.
Results may differ from a plain program's by a relative error of at most 0.0059.
Values may be sent and summed in bfloat16 or wider, within the bound.
A program may use at most 128 MiB of HBM per device.

v0:
```python
import jax
import jax.numpy as jnp
from jax import lax
from jax.sharding import PartitionSpec as P

D = 8192
SEGS = 16


eps = 1e-05
keep_scale = 1.0 / 0.9


def over_tokens(left, right):
    return lax.dot_general(
        left, right, (((0,), (0,)), ((), ())), preferred_element_type=jnp.float32
    )


def over_width(left, right):
    return lax.dot_general(
        left, right, (((1,), (1,)), ((), ())), preferred_element_type=jnp.float32
    )


def per_device(
    stream_in, grad_out, gate_pre, up_pre, keep_mask, segment_ids, norm_gain, w_gate, w_up, w_down
):
    n_row = lax.axis_size("row")
    n_col = lax.axis_size("col")
    tok_col, feat_loc = stream_in.shape
    total = tok_col * n_col
    xs = stream_in.astype(jnp.float32)
    onehot = (segment_ids[:, None] == jnp.arange(SEGS, dtype=jnp.int32)[None, :]).astype(
        jnp.float32
    )
    squares, counts = lax.psum((jnp.sum(xs * xs, axis=1), jnp.sum(onehot, axis=0)), "row")
    weights = jnp.sum(onehot * (total / (SEGS * counts))[None, :], axis=1)
    recip = lax.rsqrt(squares / D + eps)
    normed = (xs * recip[:, None] * norm_gain[None, :]).astype(jnp.bfloat16)
    gate_f = gate_pre.astype(jnp.float32)
    up_f = up_pre.astype(jnp.float32)
    sig = jax.nn.sigmoid(gate_f)
    keep_f = keep_mask.astype(jnp.float32) * keep_scale
    dropped = (gate_f * sig * up_f * keep_f * weights[:, None]).astype(jnp.bfloat16)
    cot_full, normed_full = (
        lax.all_gather(grad_out, "col", axis=0, tiled=True),
        lax.all_gather(normed, "col", axis=0, tiled=True),
    )
    back = lax.psum_scatter(over_width(cot_full, w_down), "row", scatter_dimension=0, tiled=True)
    grad_act = back * weights[:, None] * keep_f
    grad_gpre = (grad_act * up_f * sig * (1.0 + gate_f * (1.0 - sig))).astype(jnp.bfloat16)
    grad_upre = (grad_act * gate_f * sig).astype(jnp.bfloat16)
    dropped_full, gpre_full, upre_full = (
        lax.all_gather(dropped, "row", axis=0, tiled=True),
        lax.all_gather(grad_gpre, "row", axis=0, tiled=True),
        lax.all_gather(grad_upre, "row", axis=0, tiled=True),
    )
    grad_down = over_tokens(dropped_full, cot_full).astype(jnp.bfloat16)
    grad_gate = over_tokens(normed_full, gpre_full).astype(jnp.bfloat16)
    grad_up = over_tokens(normed_full, upre_full).astype(jnp.bfloat16)
    grad_normed = lax.psum_scatter(
        over_width(gpre_full, w_gate) + over_width(upre_full, w_up),
        "col",
        scatter_dimension=0,
        tiled=True,
    )
    scaled = grad_normed * norm_gain[None, :]
    per_dev = tok_col // n_row
    x_rows = lax.all_to_all(
        xs.reshape(n_row, per_dev, feat_loc), "row", split_axis=0, concat_axis=2, tiled=True
    )
    d_rows = lax.all_to_all(
        scaled.reshape(n_row, per_dev, feat_loc), "row", split_axis=0, concat_axis=2, tiled=True
    )
    row_recip = lax.rsqrt(jnp.mean(x_rows * x_rows, axis=2, keepdims=True) + eps)
    row_inner = jnp.mean(d_rows * x_rows, axis=2, keepdims=True)
    result = row_recip * (d_rows - x_rows * row_recip * row_recip * row_inner)
    moved = lax.all_to_all(result, "row", split_axis=2, concat_axis=0, tiled=True)
    branch = moved.reshape(tok_col, feat_loc)
    grad_in = (grad_out.astype(jnp.float32) + branch).astype(jnp.bfloat16)
    return (grad_in, grad_gate, grad_up, grad_down)


def solution(mesh):
    return jax.shard_map(
        per_device,
        mesh=mesh,
        in_specs=(
            P("col", "row"),
            P("col", "row"),
            P("row", "col"),
            P("row", "col"),
            P("row", "col"),
            P("row"),
            P("row"),
            P("row", "col"),
            P("row", "col"),
            P("col", "row"),
        ),
        out_specs=(P("col", "row"), P("row", "col"), P("row", "col"), P("col", "row")),
        check_vma=False,
    )
```

profile of v0, /device:TPU:64, one launch (start us, length us, event | category | flops | bytes accessed | tf_op | source)
XLA Modules:
  0.0 682.0 jit_solution(3972734062639505870)
XLA Ops:
  7.2 0.7 all-gather.6.cloned.1.call-update
  8.0 57.4 %all-gather.6.cloned.1.call-done = bf16[2048,1024]{1,0:T(8,128)(2,1)} async-done(((bf16[128,1024]{1,0:T(8,128)(2,1)}), bf16[2048,1024]{1,0:T(8,128)(2,1)}) %all-gather.6.cloned.1.call-update) | async-done | bytes 4194320 | tf_op jit(solution)/shard_map/all_gather | solution.py:47
  65.4 10.3 %fusion.15 = f32[2048,896]{1,0:T(8,128)} fusion(bf16[2048,1024]{1,0:T(8,128)(2,1)} %all-gather.6.cloned.1.call-done, bf16[896,1024]{1,0:T(8,128)(2,1)} %param.19), kind=kOutput, calls=%fused_computation.41 | convolution fusion | flops 3758096384 | bytes 13369344 | tf_op jit(solution)/shard_map/dot_general | solution.py:21
  75.7 0.6 copy-done.7
  76.7 25.4 %all-reduce = (f32[16]{0:T(128)S(1)}, f32[128]{0:T(128)S(1)}) all-reduce(f32[16]{0:T(128)S(1)} %convert_reduce_fusion, f32[128]{0:T(128)S(1)} %multiply_reduce_fusion), channel_id=1, replica_groups=mesh['row'=8,'col'=16] {'row'}, use_global_device_ids=true, to_apply=%region_3.0 | all-reduce | flops 144 | bytes 1152 | tf_op jit(solution)/shard_map/psum | solution.py:37
  102.3 124.5 %reduce-scatter.3.cloned.1.call-done = f32[256,896]{1,0:T(8,128)} async-done(((f32[2048,896]{1,0:T(8,128)}), f32[256,896]{1,0:T(8,128)}) %reduce-scatter.3.cloned.1.call-update) | async-done | bytes 917520 | tf_op jit(solution)/shard_map/reduce_scatter | solution.py:50
  226.8 3.1 fusion.11
  230.0 0.5 all-gather.10.cloned.1.call-update
  230.5 80.7 %all-gather.8.cloned.1.call-done = bf16[2048,896]{1,0:T(8,128)(2,1)} async-done(((bf16[256,896]{1,0:T(8,128)(2,1)}), bf16[2048,896]{1,0:T(8,128)(2,1)}) %all-gather.8.cloned.1.call-update) | async-done | bytes 3670032 | tf_op jit(solution)/shard_map/all_gather | solution.py:56
  311.3 8.8 %fusion.16 = f32[2048,1024]{1,0:T(8,128)} fusion(bf16[2048,896]{1,0:T(8,128)(2,1)} %all-gather.8.cloned.1.call-done, bf16[1024,896]{1,0:T(8,128)(2,1)S(1)} %copy-done), kind=kOutput, calls=%fused_computation.42 | convolution fusion | flops 3758096384 | bytes 13893632 | tf_op jit(solution)/shard_map/dot_general | solution.py:21
  320.1 74.2 %all-gather.10.cloned.1.call-done = bf16[2048,896]{1,0:T(8,128)(2,1)} async-done(((bf16[256,896]{1,0:T(8,128)(2,1)}), bf16[2048,896]{1,0:T(8,128)(2,1)}) %all-gather.10.cloned.1.call-update) | async-done | bytes 3670032 | tf_op jit(solution)/shard_map/all_gather | solution.py:57
  394.4 12.8 %convolution_add_fusion = f32[2048,1024]{1,0:T(8,128)} fusion(f32[2048,1024]{1,0:T(8,128)} %fusion.16, bf16[2048,896]{1,0:T(8,128)(2,1)} %all-gather.10.cloned.1.call-done, bf16[1024,896]{1,0:T(8,128)(2,1)} %param.18), kind=kOutput, calls=%fused_computation | convolution fusion | flops 3760193536 | bytes 22282240 | tf_op jit(solution)/shard_map/dot_general | solution.py:21
  407.4 0.3 all-gather.14.cloned.1.call-update
  407.8 100.2 %reduce-scatter.5.cloned.1.call-done = f32[128,1024]{1,0:T(8,128)} async-done(((f32[2048,1024]{1,0:T(8,128)}), f32[128,1024]{1,0:T(8,128)}) %reduce-scatter.5.cloned.1.call-update) | async-done | bytes 524304 | tf_op jit(solution)/shard_map/reduce_scatter | solution.py:62
  508.0 2.0 multiply_convert_fusion
  510.1 15.4 %all_to_all.51 = f32[8,16,1024]{2,1,0:T(8,128)S(1)} all-to-all(f32[8,16,1024]{2,1,0:T(8,128)S(1)} %convert), channel_id=1, replica_groups=mesh['row'=8,'col'=16] {'row'}, dimensions={0} | all-to-all | bytes 1048576 | tf_op jit(solution)/shard_map/all_to_all | solution.py:70
  525.5 7.4 %all-to-all-start.1 = ((f32[8,16,1024]{2,1,0:T(8,128)}), f32[8,16,1024]{2,1,0:T(8,128)S(1)}, u32[]{:S(2)}, u32[]{:S(2)}) async-start(f32[8,16,1024]{2,1,0:T(8,128)} %bitcast.3), calls=%async_computation.3 | async-start | bytes 1048576 | tf_op jit(solution)/shard_map/all_to_all | solution.py:73
  532.9 11.5 %all-to-all-done.1 = f32[8,16,1024]{2,1,0:T(8,128)S(1)} async-done(((f32[8,16,1024]{2,1,0:T(8,128)}), f32[8,16,1024]{2,1,0:T(8,128)S(1)}, u32[]{:S(2)}, u32[]{:S(2)}) %all-to-all-start.1) | async-done | bytes 524320 | tf_op jit(solution)/shard_map/all_to_all | solution.py:73
  544.9 6.5 copy.26
  551.4 0.5 broadcast.122
  551.9 38.4 %reduce.4 = f32[8192,16]{1,0:T(8,128)} reduce(f32[8192,1,16]{2,1,0:T(1,128)} %bitcast.41, f32[]{:T(128)} %broadcast.122), dimensions={1}, to_apply=%bitcast.26.reduce_sub_computation | reduce | bytes 1048580
  590.3 4.4 reshape.168
  594.6 3.7 all-to-all-start.2
  598.4 3.9 all-gather.14.cloned.1.call-done
  602.3 8.5 %convolution_convert_fusion = bf16[896,1024]{1,0:T(8,128)(2,1)} fusion(bf16[2048,896]{1,0:T(8,128)(2,1)} %all-gather.14.cloned.1.call-done, bf16[2048,1024]{1,0:T(8,128)(2,1)} %all-gather.6.cloned.1.call-done), kind=kOutput, calls=%fused_computation.1 | convolution fusion | flops 3759013888 | bytes 9699328 | tf_op jit(solution)/shard_map/dot_general | solution.py:15
  610.8 1.9 reduce.5
  612.7 10.2 %reshape.169 = f32[8192,1,16]{2,1,0:T(1,128)} reshape(f32[8,16384]{1,0:T(8,128)S(1)} %reduce.5) | data formatting | bytes 1048576
  622.9 3.2 copy.29
  626.5 0.8 fusion.12
  627.2 33.0 %all-gather.12.cloned.1.call-done = bf16[2048,1024]{1,0:T(8,128)(2,1)} async-done(((bf16[128,1024]{1,0:T(8,128)(2,1)}), bf16[2048,1024]{1,0:T(8,128)(2,1)}) %all-gather.12.cloned.1.call-update) | async-done | bytes 4194320 | tf_op jit(solution)/shard_map/all_gather | solution.py:48
  660.2 9.3 %convolution_convert_fusion.1 = bf16[1024,896]{1,0:T(8,128)(2,1)} fusion(bf16[2048,1024]{1,0:T(8,128)(2,1)} %all-gather.12.cloned.1.call-done, bf16[2048,896]{1,0:T(8,128)(2,1)} %all-gather.10.cloned.1.call-done), kind=kOutput, calls=%fused_computation.2 | convolution fusion | flops 3759013888 | bytes 9699328 | tf_op jit(solution)/shard_map/dot_general | solution.py:15
  669.4 5.7 convolution_convert_fusion.2
  (43 shorter events, 1.9 us)
Async XLA Ops:
  7.2 304.1 %copy-start = (bf16[1024,896]{1,0:T(8,128)(2,1)S(1)}, bf16[1024,896]{1,0:T(8,128)(2,1)}, u32[]{:S(2)}) copy-start(bf16[1024,896]{1,0:T(8,128)(2,1)} %param.17) | copy-start | bytes 5505028
  7.2 58.2 %all-gather.6.cloned.1.call-start = ((), (), s32[]{:S(2)}) async-start(), calls=%async_computation.5 | async-start | bytes 4456448 | tf_op jit(solution)/shard_map/all_gather | solution.py:47
  7.9 218.9 %reduce-scatter.3.cloned.1.call-start = ((), (), s32[]{:S(2)}) async-start(), calls=%async_computation.6 | async-start | bytes 8257536 | tf_op jit(solution)/shard_map/reduce_scatter | solution.py:50
  75.6 0.7 copy-start.7
  75.6 1.0 copy-start.2
  75.7 151.1 %copy-start.4 = (s32[256,896]{1,0:T(8,128)S(1)}, s32[256,896]{1,0:T(8,128)}, u32[]{:S(2)}) copy-start(s32[256,896]{1,0:T(8,128)} %param.14) | copy-start | bytes 2752516
  75.7 151.1 %copy-start.5 = (bf16[256,896]{1,0:T(8,128)(2,1)S(1)}, bf16[256,896]{1,0:T(8,128)(2,1)}, u32[]{:S(2)}) copy-start(bf16[256,896]{1,0:T(8,128)(2,1)} %param.12) | copy-start | bytes 1376260
  75.7 235.6 %all-gather.8.cloned.1.call-start = ((), (), s32[]{:S(2)}) async-start(), calls=%async_computation.7 | async-start | bytes 4128768 | tf_op jit(solution)/shard_map/all_gather | solution.py:56
  229.9 164.4 %all-gather.10.cloned.1.call-start = ((), (), s32[]{:S(2)}) async-start(), calls=%async_computation.8 | async-start | bytes 4128768 | tf_op jit(solution)/shard_map/all_gather | solution.py:57
  230.5 277.5 %reduce-scatter.5.cloned.1.call-start = ((), (), s32[]{:S(2)}) async-start(), calls=%async_computation.9 | async-start | bytes 8912896 | tf_op jit(solution)/shard_map/reduce_scatter | solution.py:62
  407.2 100.8 %copy-start.6 = (f32[1024]{0:T(1024)S(1)}, f32[1024]{0:T(1024)}, u32[]{:S(2)}) copy-start(f32[1024]{0:T(1024)} %param.16) | copy-start | bytes 12292
  407.2 195.1 %all-gather.14.cloned.1.call-start = ((), (), s32[]{:S(2)}) async-start(), calls=%async_computation.11 | async-start | bytes 4128768 | tf_op jit(solution)/shard_map/all_gather | solution.py:55
  407.8 252.4 %all-gather.12.cloned.1.call-start = ((), (), s32[]{:S(2)}) async-start(), calls=%async_computation.10 | async-start | bytes 4456448 | tf_op jit(solution)/shard_map/all_gather | solution.py:48
  525.5 18.9 %all-to-all-start.1 = ((f32[8,16,1024]{2,1,0:T(8,128)}), f32[8,16,1024]{2,1,0:T(8,128)S(1)}, u32[]{:S(2)}, u32[]{:S(2)}) async-start(f32[8,16,1024]{2,1,0:T(8,128)} %bitcast.3), calls=%async_computation.3 | async-start | bytes 1048576 | tf_op jit(solution)/shard_map/all_to_all | solution.py:73
  594.6 16.2 %all-to-all-start.2 = ((f32[8,1,16384]{2,1,0:T(1,128)}), f32[8,1,16384]{2,1,0:T(1,128)S(1)}, u32[]{:S(2)}, u32[]{:S(2)}) async-start(f32[8,1,16384]{2,1,0:T(1,128)} %reshape.168), calls=%async_computation.4 | async-start | bytes 1048576 | tf_op jit(solution)/shard_map/all_to_all | solution.py:79
  622.9 3.5 copy-start.3
  660.2 9.3 %copy-start.8 = (bf16[2048,1024]{1,0:T(8,128)(2,1)S(1)}, bf16[2048,1024]{1,0:T(8,128)(2,1)}, u32[]{:S(2)}) copy-start(bf16[2048,1024]{1,0:T(8,128)(2,1)} %all-gather.12.cloned.1.call-done) | copy-start | bytes 12582916
  660.2 9.3 %copy-start.9 = (bf16[2048,896]{1,0:T(8,128)(2,1)S(1)}, bf16[2048,896]{1,0:T(8,128)(2,1)}, u32[]{:S(2)}) copy-start(bf16[2048,896]{1,0:T(8,128)(2,1)} %all-gather.8.cloned.1.call-done) | copy-start | bytes 11010052
  660.2 14.9 %copy-start.1 = (bf16[1024,896]{1,0:T(8,128)(2,1)S(1)}, bf16[1024,896]{1,0:T(8,128)(2,1)}, u32[]{:S(2)}) copy-start(bf16[1024,896]{1,0:T(8,128)(2,1)} %param.17) | copy-start | bytes 5505028
Sparse Core Ops, SparseCore 0:
  10.4 54.9 all-gather.5
  75.8 150.9 reduce-scatter.2
  230.0 81.2 all-gather.7
  313.3 80.9 all-gather.9
  407.3 100.6 reduce-scatter.4
  510.1 92.1 all-gather.13
  604.7 55.4 all-gather.11
where the time goes:
time: 687 us; the launch traced here: 682 us
  waiting for transfers between devices  487 us (71%)
  matrix products  55.4 us (8%)
  other arithmetic  46.9 us (7%)
  blocking collectives  40.8 us (6%)
  local copies, waits for them, and re-layouts  26 us (4%)
  between operations  14.2 us (2%)
  starting transfers between devices  11.6 us (2%)
    reduce_scatter x1, waiting for transfers between devices, per_device(): lax.psum_scatter(over_width(cot_full, w_down), 'row', scatter_dimension=0...  125 us
    reduce_scatter x1, waiting for transfers between devices, per_device(): lax.psum_scatter(over_width(gpre_full, w_gate) + over_width(upre_full, w_...  100 us
    all_gather x1, waiting for transfers between devices, per_device(): lax.all_gather(grad_gpre, 'row', axis=0, tiled=True)  80.7 us
    all_gather x1, waiting for transfers between devices, per_device(): lax.all_gather(grad_upre, 'row', axis=0, tiled=True)  74.2 us
    all_gather x1, waiting for transfers between devices, per_device(): lax.all_gather(grad_out, 'col', axis=0, tiled=True)  57.4 us
    unnamed x1, other arithmetic  38.4 us
    all_gather x1, waiting for transfers between devices, per_device(): lax.all_gather(normed, 'col', axis=0, tiled=True)  33 us
    dot_general x3, matrix products, over_width(): lax.dot_general(left, right, (((1,), (1,)), ((), ())), preferred_element_...  31.9 us
  transfers between devices with their start and end apart: 9, of which 8 were waited for; matrix products, arithmetic and copies ran while one was open for 13% of the time, Pallas kernels for 0%

commit v1 on v0

--- a/solution.py
+++ b/solution.py
@@ -66,18 +66,8 @@
         tiled=True,
     )
     scaled = grad_normed * norm_gain[None, :]
-    per_dev = tok_col // n_row
-    x_rows = lax.all_to_all(
-        xs.reshape(n_row, per_dev, feat_loc), "row", split_axis=0, concat_axis=2, tiled=True
-    )
-    d_rows = lax.all_to_all(
-        scaled.reshape(n_row, per_dev, feat_loc), "row", split_axis=0, concat_axis=2, tiled=True
-    )
-    row_recip = lax.rsqrt(jnp.mean(x_rows * x_rows, axis=2, keepdims=True) + eps)
-    row_inner = jnp.mean(d_rows * x_rows, axis=2, keepdims=True)
-    result = row_recip * (d_rows - x_rows * row_recip * row_recip * row_inner)
-    moved = lax.all_to_all(result, "row", split_axis=2, concat_axis=0, tiled=True)
-    branch = moved.reshape(tok_col, feat_loc)
+    inner = lax.psum(jnp.sum(scaled * xs, axis=1), "row") / D
+    branch = recip[:, None] * (scaled - xs * (recip * recip * inner)[:, None])
     grad_in = (grad_out.astype(jnp.float32) + branch).astype(jnp.bfloat16)
     return (grad_in, grad_gate, grad_up, grad_down)
 

time: 687 us -> 676 us (0.984)
  waiting for transfers between devices: 487 us -> 545 us
  other arithmetic: 46.9 us -> 6.63 us
  local copies, waits for them, and re-layouts: 26 us -> 0.64 us
  starting transfers between devices: 11.6 us -> 0.46 us
  blocking collectives: 40.8 us -> 47.9 us
    all_gather x1, waiting for transfers between devices: 3.92 us -> 58.3 us  [per_device(): lax.all_gather(dropped, 'row', axis=0, tiled=True)]
    unnamed x1 -> x0, other arithmetic: 38.4 us -> none
    psum x0 -> x1, blocking collectives: none -> 22.2 us  [per_device(): inner = lax.psum(jnp.sum(scaled * xs, axis=1), 'row') / D]
    all_gather x1, waiting for transfers between devices: 33 us -> 48.5 us  [per_device(): lax.all_gather(normed, 'col', axis=0, tiled=True)]
    all_to_all x1 -> x0, blocking collectives: 15.4 us -> none  [per_device(): lax.all_to_all(xs.reshape(n_row, per_dev, feat_loc), 'row', split_axis=0,...]
    unnamed x23 -> x18, local copies, waits for them, and re-layouts: 15.9 us -> 0.64 us
    all_to_all x2 -> x0, waiting for transfers between devices: 11.5 us -> none  [the longest x1 11.5 us: per_device(): lax.all_to_all(scaled.reshape(n_row, per_dev, feat_loc), 'row', split_axi...]
    all_to_all x2 -> x0, starting transfers between devices: 11.1 us -> none  [the longest x1 7.41 us: per_device(): lax.all_to_all(scaled.reshape(n_row, per_dev, feat_loc), 'row', split_axi...]
  transfers between devices with their start and end apart: 9 -> 7, of which waited for: 8 -> 7; matrix products, arithmetic and copies ran while one was open for 13% -> 3% of each run, Pallas kernels for 0% -> 0%
where the time goes in v1:
time: 676 us; the launch traced here: 671 us
  waiting for transfers between devices  545 us (81%)
  matrix products  55.5 us (8%)
  blocking collectives  47.9 us (7%)
  between operations  14.1 us (2%)
    reduce_scatter x1, waiting for transfers between devices, per_device(): lax.psum_scatter(over_width(cot_full, w_down), 'row', scatter_dimension=0...  124 us
    reduce_scatter x1, waiting for transfers between devices, per_device(): lax.psum_scatter(over_width(gpre_full, w_gate) + over_width(upre_full, w_...  100 us
    all_gather x1, waiting for transfers between devices, per_device(): lax.all_gather(grad_gpre, 'row', axis=0, tiled=True)  80.8 us
    all_gather x1, waiting for transfers between devices, per_device(): lax.all_gather(grad_upre, 'row', axis=0, tiled=True)  74.2 us
    all_gather x1, waiting for transfers between devices, per_device(): lax.all_gather(dropped, 'row', axis=0, tiled=True)  58.3 us
    all_gather x1, waiting for transfers between devices, per_device(): lax.all_gather(grad_out, 'col', axis=0, tiled=True)  57.4 us
    all_gather x1, waiting for transfers between devices, per_device(): lax.all_gather(normed, 'col', axis=0, tiled=True)  48.5 us
    dot_general x3, matrix products, over_width(): lax.dot_general(left, right, (((1,), (1,)), ((), ())), preferred_element_...  32 us
  transfers between devices with their start and end apart: 7, of which 7 were waited for; matrix products, arithmetic and copies ran while one was open for 3% of the time, Pallas kernels for 0%

profile of v1, /device:TPU:64, one launch (start us, length us, event | category | flops | bytes accessed | tf_op | source)
XLA Modules:
  0.0 670.6 jit_solution(16865181960123287659)
XLA Ops:
  7.2 0.0 all-gather.6.cloned.1.call-start
  7.2 0.7 all-gather.6.cloned.1.call-update
  7.9 0.0 reduce-scatter.3.cloned.1.call-start
  8.0 57.4 %all-gather.6.cloned.1.call-done = bf16[2048,1024]{1,0:T(8,128)(2,1)} async-done(((bf16[128,1024]{1,0:T(8,128)(2,1)}), bf16[2048,1024]{1,0:T(8,128)(2,1)}) %all-gather.6.cloned.1.call-update) | async-done | bytes 4194320 | tf_op jit(solution)/shard_map/all_gather | solution.py:47
  65.4 10.3 %fusion.20 = f32[2048,896]{1,0:T(8,128)} fusion(bf16[2048,1024]{1,0:T(8,128)(2,1)} %all-gather.6.cloned.1.call-done, bf16[896,1024]{1,0:T(8,128)(2,1)} %param.19), kind=kOutput, calls=%fused_computation.42 | convolution fusion | flops 3758096384 | bytes 13369344 | tf_op jit(solution)/shard_map/dot_general | solution.py:21
  75.7 0.0 reduce-scatter.3.cloned.1.call-update
  75.7 0.0 all-gather.8.cloned.1.call-start
  75.7 0.6 copy-done.6
  76.3 0.1 convert_reduce_fusion
  76.5 25.7 %psum.22 = f32[16]{0:T(128)S(1)} all-reduce(f32[16]{0:T(128)S(1)} %convert_reduce_fusion), channel_id=1, replica_groups=mesh['row'=8,'col'=16] {'row'}, use_global_device_ids=true, to_apply=%region_4.0 | all-reduce | flops 16 | bytes 128 | tf_op jit(solution)/shard_map/psum | solution.py:37
  102.2 0.1 select_reduce_fusion
  102.3 124.5 %reduce-scatter.3.cloned.1.call-done = f32[256,896]{1,0:T(8,128)} async-done(((f32[2048,896]{1,0:T(8,128)}), f32[256,896]{1,0:T(8,128)}) %reduce-scatter.3.cloned.1.call-update) | async-done | bytes 917520 | tf_op jit(solution)/shard_map/reduce_scatter | solution.py:50
  226.8 3.1 fusion.11
  229.9 0.0 all-gather.10.cloned.1.call-start
  229.9 0.5 all-gather.10.cloned.1.call-update
  230.5 0.0 reduce-scatter.5.cloned.1.call-start
  230.5 80.8 %all-gather.8.cloned.1.call-done = bf16[2048,896]{1,0:T(8,128)(2,1)} async-done(((bf16[256,896]{1,0:T(8,128)(2,1)}), bf16[2048,896]{1,0:T(8,128)(2,1)}) %all-gather.8.cloned.1.call-update) | async-done | bytes 3670032 | tf_op jit(solution)/shard_map/all_gather | solution.py:56
  311.3 8.9 %fusion.21 = f32[2048,1024]{1,0:T(8,128)} fusion(bf16[2048,896]{1,0:T(8,128)(2,1)} %all-gather.8.cloned.1.call-done, bf16[1024,896]{1,0:T(8,128)(2,1)S(1)} %copy-done), kind=kOutput, calls=%fused_computation.43 | convolution fusion | flops 3758096384 | bytes 13893632 | tf_op jit(solution)/shard_map/dot_general | solution.py:21
  320.2 74.2 %all-gather.10.cloned.1.call-done = bf16[2048,896]{1,0:T(8,128)(2,1)} async-done(((bf16[256,896]{1,0:T(8,128)(2,1)}), bf16[2048,896]{1,0:T(8,128)(2,1)}) %all-gather.10.cloned.1.call-update) | async-done | bytes 3670032 | tf_op jit(solution)/shard_map/all_gather | solution.py:57
  394.4 12.8 %convolution_add_fusion = f32[2048,1024]{1,0:T(8,128)} fusion(f32[2048,1024]{1,0:T(8,128)} %fusion.21, bf16[2048,896]{1,0:T(8,128)(2,1)} %all-gather.10.cloned.1.call-done, bf16[1024,896]{1,0:T(8,128)(2,1)} %param.18), kind=kOutput, calls=%fused_computation | convolution fusion | flops 3760193536 | bytes 22282240 | tf_op jit(solution)/shard_map/dot_general | solution.py:21
  407.2 0.0 all-gather.14.cloned.1.call-start
  407.2 0.5 all-gather.14.cloned.1.call-update
  407.8 0.2 all-gather.12.cloned.1.call-start
  408.0 100.0 %reduce-scatter.5.cloned.1.call-done = f32[128,1024]{1,0:T(8,128)} async-done(((f32[2048,1024]{1,0:T(8,128)}), f32[128,1024]{1,0:T(8,128)}) %reduce-scatter.5.cloned.1.call-update) | async-done | bytes 524304 | tf_op jit(solution)/shard_map/reduce_scatter | solution.py:62
  508.0 1.2 fusion.12
  509.2 22.2 %all-reduce = (f32[128]{0:T(128)S(1)}, f32[128]{0:T(128)S(1)}) all-reduce(f32[128]{0:T(128)S(1)} %get-tuple-element.5, f32[128]{0:T(128)S(1)} %get-tuple-element.4), channel_id=1, replica_groups=mesh['row'=8,'col'=16] {'row'}, use_global_device_ids=true, to_apply=%region_8.0 | all-reduce | flops 256 | bytes 2048 | tf_op jit(solution)/shard_map/psum | solution.py:69
  531.4 2.1 fusion.19
  533.5 58.3 %all-gather.14.cloned.1.call-done = bf16[2048,896]{1,0:T(8,128)(2,1)} async-done(((bf16[256,896]{1,0:T(8,128)(2,1)}), bf16[2048,896]{1,0:T(8,128)(2,1)}) %all-gather.14.cloned.1.call-update) | async-done | bytes 3670032 | tf_op jit(solution)/shard_map/all_gather | solution.py:55
  591.8 8.5 %convolution_convert_fusion = bf16[896,1024]{1,0:T(8,128)(2,1)} fusion(bf16[2048,896]{1,0:T(8,128)(2,1)} %all-gather.14.cloned.1.call-done, bf16[2048,1024]{1,0:T(8,128)(2,1)} %all-gather.6.cloned.1.call-done), kind=kOutput, calls=%fused_computation.1 | convolution fusion | flops 3759013888 | bytes 9699328 | tf_op jit(solution)/shard_map/dot_general | solution.py:15
  600.4 48.5 %all-gather.12.cloned.1.call-done = bf16[2048,1024]{1,0:T(8,128)(2,1)} async-done(((bf16[128,1024]{1,0:T(8,128)(2,1)}), bf16[2048,1024]{1,0:T(8,128)(2,1)}) %all-gather.12.cloned.1.call-update) | async-done | bytes 4194320 | tf_op jit(solution)/shard_map/all_gather | solution.py:48
  648.8 9.3 %convolution_convert_fusion.1 = bf16[1024,896]{1,0:T(8,128)(2,1)} fusion(bf16[2048,1024]{1,0:T(8,128)(2,1)} %all-gather.12.cloned.1.call-done, bf16[2048,896]{1,0:T(8,128)(2,1)} %all-gather.10.cloned.1.call-done), kind=kOutput, calls=%fused_computation.2 | convolution fusion | flops 3759013888 | bytes 9699328 | tf_op jit(solution)/shard_map/dot_general | solution.py:15
  658.1 5.7 convolution_convert_fusion.2
  (22 shorter events, 0.1 us)
Async XLA Ops:
  7.2 304.1 %copy-start = (bf16[1024,896]{1,0:T(8,128)(2,1)S(1)}, bf16[1024,896]{1,0:T(8,128)(2,1)}, u32[]{:S(2)}) copy-start(bf16[1024,896]{1,0:T(8,128)(2,1)} %param.17) | copy-start | bytes 5505028
  7.2 58.2 %all-gather.6.cloned.1.call-start = ((), (), s32[]{:S(2)}) async-start(), calls=%async_computation.2 | async-start | bytes 4456448 | tf_op jit(solution)/shard_map/all_gather | solution.py:47
  7.9 218.8 %reduce-scatter.3.cloned.1.call-start = ((), (), s32[]{:S(2)}) async-start(), calls=%async_computation.3 | async-start | bytes 8257536 | tf_op jit(solution)/shard_map/reduce_scatter | solution.py:50
  75.7 0.7 copy-start.6
  75.7 151.1 %copy-start.3 = (s32[256,896]{1,0:T(8,128)S(1)}, s32[256,896]{1,0:T(8,128)}, u32[]{:S(2)}) copy-start(s32[256,896]{1,0:T(8,128)} %param.14) | copy-start | bytes 2752516
  75.7 151.1 %copy-start.4 = (bf16[256,896]{1,0:T(8,128)(2,1)S(1)}, bf16[256,896]{1,0:T(8,128)(2,1)}, u32[]{:S(2)}) copy-start(bf16[256,896]{1,0:T(8,128)(2,1)} %param.12) | copy-start | bytes 1376260
  75.7 235.6 %all-gather.8.cloned.1.call-start = ((), (), s32[]{:S(2)}) async-start(), calls=%async_computation.4 | async-start | bytes 4128768 | tf_op jit(solution)/shard_map/all_gather | solution.py:56
  229.9 164.5 %all-gather.10.cloned.1.call-start = ((), (), s32[]{:S(2)}) async-start(), calls=%async_computation.5 | async-start | bytes 4128768 | tf_op jit(solution)/shard_map/all_gather | solution.py:57
  230.5 277.5 %reduce-scatter.5.cloned.1.call-start = ((), (), s32[]{:S(2)}) async-start(), calls=%async_computation.6 | async-start | bytes 8912896 | tf_op jit(solution)/shard_map/reduce_scatter | solution.py:62
  407.2 100.8 %copy-start.1 = (bf16[128,1024]{1,0:T(8,128)(2,1)S(1)}, bf16[128,1024]{1,0:T(8,128)(2,1)}, u32[]{:S(2)}) copy-start(bf16[128,1024]{1,0:T(8,128)(2,1)} %param.10) | copy-start | bytes 786436
  407.2 100.8 %copy-start.5 = (f32[1024]{0:T(1024)S(1)}, f32[1024]{0:T(1024)}, u32[]{:S(2)}) copy-start(f32[1024]{0:T(1024)} %param.16) | copy-start | bytes 12292
  407.2 124.3 %copy-start.2 = (bf16[128,1024]{1,0:T(8,128)(2,1)S(1)}, bf16[128,1024]{1,0:T(8,128)(2,1)}, u32[]{:S(2)}) copy-start(bf16[128,1024]{1,0:T(8,128)(2,1)} %param.11) | copy-start | bytes 786436
  407.2 184.6 %all-gather.14.cloned.1.call-start = ((), (), s32[]{:S(2)}) async-start(), calls=%async_computation.8 | async-start | bytes 4128768 | tf_op jit(solution)/shard_map/all_gather | solution.py:55
  407.8 241.1 %all-gather.12.cloned.1.call-start = ((), (), s32[]{:S(2)}) async-start(), calls=%async_computation.7 | async-start | bytes 4456448 | tf_op jit(solution)/shard_map/all_gather | solution.py:48
  648.8 9.3 %copy-start.7 = (bf16[2048,1024]{1,0:T(8,128)(2,1)S(1)}, bf16[2048,1024]{1,0:T(8,128)(2,1)}, u32[]{:S(2)}) copy-start(bf16[2048,1024]{1,0:T(8,128)(2,1)} %all-gather.12.cloned.1.call-done) | copy-start | bytes 12582916
  648.8 9.3 %copy-start.8 = (bf16[2048,896]{1,0:T(8,128)(2,1)S(1)}, bf16[2048,896]{1,0:T(8,128)(2,1)}, u32[]{:S(2)}) copy-start(bf16[2048,896]{1,0:T(8,128)(2,1)} %all-gather.8.cloned.1.call-done) | copy-start | bytes 11010052
Sparse Core Ops, SparseCore 0:
  10.4 54.9 all-gather.5
  75.8 150.8 reduce-scatter.2
  230.0 81.2 all-gather.7
  313.3 80.9 all-gather.9
  407.3 100.6 reduce-scatter.4
  510.0 81.7 all-gather.13
  594.8 54.0 all-gather.11

commit v2 on v1

v2 whole, which is shorter than its diff:
```python
import functools

import jax
import jax.numpy as jnp
from jax import lax
from jax.experimental import pallas as pl
from jax.experimental.pallas import tpu as pltpu
from jax.sharding import PartitionSpec as P

D = 8192
SEGS = 16
AXES = ("row", "col")

eps = 1e-05
keep_scale = 1.0 / 0.9


def over_tokens(left, right):
    return lax.dot_general(
        left, right, (((0,), (0,)), ((), ())), preferred_element_type=jnp.float32
    )


def over_width(left, right):
    return lax.dot_general(
        left, right, (((1,), (1,)), ((), ())), preferred_element_type=jnp.float32
    )


def _dev(axis, idx):
    return tuple(idx if a == axis else lax.axis_index(a) for a in AXES)


def _barrier(axes):
    barrier = pltpu.get_barrier_semaphore()
    count = 0
    for axis in sorted(set(axes)):
        k = lax.axis_size(axis)
        me = lax.axis_index(axis)
        for d in range(1, k):
            pl.semaphore_signal(
                barrier, inc=1, device_id=_dev(axis, (me + d) % k),
                device_id_type=pl.DeviceIdType.MESH,
            )
        count += k - 1
    pl.semaphore_wait(barrier, count)


def _exchange_kernel(modes, axes, *refs):
    n = len(modes)
    ins, outs = refs[:n], refs[n:2 * n]
    send_sem, recv_sem, local_sem = refs[2 * n:]
    _barrier(axes)
    sends = []
    for i, (mode, axis) in enumerate(zip(modes, axes)):
        k = lax.axis_size(axis)
        me = lax.axis_index(axis)
        m = outs[i].shape[1]
        for d in range(1, k):
            tgt = (me + d) % k
            src = ins[i] if mode == "gather" else ins[i].at[pl.ds(tgt * m, m)]
            c = pltpu.make_async_remote_copy(
                src, outs[i].at[me], send_sem.at[i, d], recv_sem.at[i, me],
                device_id=_dev(axis, tgt), device_id_type=pl.DeviceIdType.MESH,
            )
            c.start()
            sends.append(c)
        src = ins[i] if mode == "gather" else ins[i].at[pl.ds(me * m, m)]
        loc = pltpu.make_async_copy(src, outs[i].at[me], local_sem.at[i])
        loc.start()
        sends.append(loc)
    for c in sends:
        if c.is_remote:
            c.wait_send()
        else:
            c.wait()
    for i, (mode, axis) in enumerate(zip(modes, axes)):
        k = lax.axis_size(axis)
        me = lax.axis_index(axis)
        m = outs[i].shape[1]
        for d in range(1, k):
            srcdev = (me + k - d) % k
            src = ins[i] if mode == "gather" else ins[i].at[pl.ds(0, m)]
            pltpu.make_async_remote_copy(
                src, outs[i].at[srcdev], send_sem.at[i, d], recv_sem.at[i, srcdev],
                device_id=_dev(axis, srcdev), device_id_type=pl.DeviceIdType.MESH,
            ).wait_recv()


def exchange(items, cid):
    modes = tuple(mode for _, _, mode in items)
    axes = tuple(axis for _, axis, _ in items)
    out_shapes = []
    kmax = 1
    for x, axis, mode in items:
        k = lax.axis_size(axis)
        kmax = max(kmax, k)
        if mode == "gather":
            out_shapes.append(jax.ShapeDtypeStruct((k,) + x.shape, x.dtype))
        else:
            out_shapes.append(
                jax.ShapeDtypeStruct((k, x.shape[0] // k) + x.shape[1:], x.dtype)
            )
    n = len(items)
    return pl.pallas_call(
        functools.partial(_exchange_kernel, modes, axes),
        out_shape=tuple(out_shapes),
        in_specs=[pl.BlockSpec(memory_space=pl.ANY)] * n,
        out_specs=tuple(pl.BlockSpec(memory_space=pl.ANY) for _ in range(n)),
        scratch_shapes=[
            pltpu.SemaphoreType.DMA((n, kmax)),
            pltpu.SemaphoreType.DMA((n, kmax)),
            pltpu.SemaphoreType.DMA((n,)),
        ],
        compiler_params=pltpu.CompilerParams(collective_id=cid, has_side_effects=True),
    )(*[x for x, _, _ in items])


def per_device(
    stream_in, grad_out, gate_pre, up_pre, keep_mask, segment_ids, norm_gain, w_gate, w_up, w_down
):
    n_row = lax.axis_size("row")
    n_col = lax.axis_size("col")
    tok_col, feat_loc = stream_in.shape
    tok_row, ff_loc = gate_pre.shape
    total = tok_col * n_col
    xs = stream_in.astype(jnp.float32)
    onehot = (segment_ids[:, None] == jnp.arange(SEGS, dtype=jnp.int32)[None, :]).astype(
        jnp.float32
    )
    stats = jnp.concatenate([jnp.sum(xs * xs, axis=1), jnp.sum(onehot, axis=0)])[None, :]
    (stats_all,) = exchange([(stats, "row", "gather")], 0)
    stats_sum = jnp.sum(stats_all, axis=(0, 1))
    squares, counts = stats_sum[:tok_col], stats_sum[tok_col:]
    weights = jnp.sum(onehot * (total / (SEGS * counts))[None, :], axis=1)
    recip = lax.rsqrt(squares / D + eps)
    normed = (xs * recip[:, None] * norm_gain[None, :]).astype(jnp.bfloat16)
    gate_f = gate_pre.astype(jnp.float32)
    up_f = up_pre.astype(jnp.float32)
    sig = jax.nn.sigmoid(gate_f)
    keep_f = keep_mask.astype(jnp.float32) * keep_scale
    dropped = (gate_f * sig * up_f * keep_f * weights[:, None]).astype(jnp.bfloat16)
    cot_full, normed_full, dropped_full = exchange(
        [(grad_out, "col", "gather"), (normed, "col", "gather"), (dropped, "row", "gather")], 1
    )
    cot_full = cot_full.reshape(total, feat_loc)
    normed_full = normed_full.reshape(total, feat_loc)
    dropped_full = dropped_full.reshape(total, ff_loc)
    (back_parts,) = exchange([(over_width(cot_full, w_down), "row", "scatter")], 2)
    back = jnp.sum(back_parts, axis=0)
    grad_act = back * weights[:, None] * keep_f
    grad_gpre = (grad_act * up_f * sig * (1.0 + gate_f * (1.0 - sig))).astype(jnp.bfloat16)
    grad_upre = (grad_act * gate_f * sig).astype(jnp.bfloat16)
    gpre_full, upre_full = exchange([(grad_gpre, "row", "gather"), (grad_upre, "row", "gather")], 3)
    gpre_full = gpre_full.reshape(total, ff_loc)
    upre_full = upre_full.reshape(total, ff_loc)
    grad_down = over_tokens(dropped_full, cot_full).astype(jnp.bfloat16)
    grad_gate = over_tokens(normed_full, gpre_full).astype(jnp.bfloat16)
    grad_up = over_tokens(normed_full, upre_full).astype(jnp.bfloat16)
    partial = over_width(gpre_full, w_gate) + over_width(upre_full, w_up)
    (gn_parts,) = exchange([(partial, "col", "scatter")], 4)
    grad_normed = jnp.sum(gn_parts, axis=0)
    scaled = grad_normed * norm_gain[None, :]
    (inner_all,) = exchange([(jnp.sum(scaled * xs, axis=1)[None, :], "row", "gather")], 5)
    inner = jnp.sum(inner_all, axis=(0, 1)) / D
    branch = recip[:, None] * (scaled - xs * (recip * recip * inner)[:, None])
    grad_in = (grad_out.astype(jnp.float32) + branch).astype(jnp.bfloat16)
    return (grad_in, grad_gate, grad_up, grad_down)


def solution(mesh):
    return jax.shard_map(
        per_device,
        mesh=mesh,
        in_specs=(
            P("col", "row"),
            P("col", "row"),
            P("row", "col"),
            P("row", "col"),
            P("row", "col"),
            P("row"),
            P("row"),
            P("row", "col"),
            P("row", "col"),
            P("col", "row"),
        ),
        out_specs=(P("col", "row"), P("row", "col"), P("row", "col"), P("col", "row")),
        check_vma=False,
    )
```

time: 676 us -> 622 us (0.920)
  Pallas kernels: 0 us -> 557 us
  waiting for transfers between devices: 545 us -> 0 us
  blocking collectives: 47.9 us -> 0 us
  other arithmetic: 6.63 us -> 21.5 us
  matrix products: 55.5 us -> 42 us
  between operations: 14.1 us -> 0.82 us
    pallas_call x0 -> x6, Pallas kernels: none -> 557 us  [exchange(): pl.pallas_call(functools.partial(_exchange_kernel, modes, axes), out_shap...]
    all_gather x5 -> x0, waiting for transfers between devices: 319 us -> none  [the longest x1 80.8 us: per_device(): lax.all_gather(grad_gpre, 'row', axis=0, tiled=True)]
    reduce_scatter x2 -> x0, waiting for transfers between devices: 224 us -> none  [the longest x1 124 us: per_device(): lax.psum_scatter(over_width(cot_full, w_down), 'row', scatter_dimension=0...]
    psum x2 -> x0, blocking collectives: 47.9 us -> none  [the longest x1 25.7 us: per_device(): lax.psum((jnp.sum(xs * xs, axis=1), jnp.sum(onehot, axis=0)), 'row')]
    dot_general x3, matrix products: 32 us -> 18.4 us  [over_width(): lax.dot_general(left, right, (((1,), (1,)), ((), ())), preferred_element_...]
    reduce_sum x0 -> x5, other arithmetic: none -> 9.97 us  [the longest x1 4.29 us: per_device(): grad_normed = jnp.sum(gn_parts, axis=0)]
  transfers between devices with their start and end apart: 7 -> 0, of which waited for: 7 -> 0; matrix products, arithmetic and copies ran while one was open for 3% -> 0% of each run, Pallas kernels for 0% -> 0%
where the time goes in v2:
time: 622 us
  Pallas kernels  557 us (90%)
  matrix products  42 us (7%)
  other arithmetic  21.5 us (3%)
    pallas_call x6, Pallas kernels, exchange(): pl.pallas_call(functools.partial(_exchange_kernel, modes, axes), out_shap...  557 us
    dot_general x3, matrix products, over_tokens(): lax.dot_general(left, right, (((0,), (0,)), ((), ())), preferred_element_...  23.6 us
    dot_general x3, matrix products, over_width(): lax.dot_general(left, right, (((1,), (1,)), ((), ())), preferred_element_...  18.4 us

profile of v2, /device:TPU:64, one launch (start us, length us, event | category | flops | bytes accessed | tf_op | source)
XLA Modules:
  0.0 621.9 jit_solution(17551963804615644095)
XLA Ops:
  0.6 0.0 copy-start
  0.6 0.9 convert_reduce_fusion
  1.6 1.1 fusion.12
  2.7 0.6 pad_maximum_fusion
  3.2 7.7 %shard_map.129 = f32[8,1,144]{2,1,0:T(1,128)} custom-call(f32[1,144]{1,0:T(1,128)} %bitcast.19), custom_call_target="tpu_custom_call" | custom-call | tf_op jit(solution)/shard_map/pallas_call | solution.py:105
  10.9 0.7 reduce_sum.74
  11.6 0.8 select_reduce_fusion
  12.4 1.8 fusion.14.refs_1_
  14.2 2.6 fusion.2.refs_2_
  16.8 146.4 %shard_map.130 = (bf16[16,128,1024]{2,1,0:T(8,128)(2,1)}, bf16[16,128,1024]{2,1,0:T(8,128)(2,1)}, bf16[8,256,896]{2,1,0:T(8,128)(2,1)}) custom-call(bf16[128,1024]{1,0:T(8,128)(2,1)} %refs_0_.1, bf16[128,1024]{1,0:T(8,128)(2,1)} %fusion.14.refs_1_, bf16[256,896]{1,0:T(8,128)(2,1)} %fusion.2.refs_2_), custom_call_target="tpu_custom_call" | custom-call | tf_op jit(solution)/shard_map/pallas_call | solution.py:105
  163.2 0.0 copy-start.9
  163.2 8.7 %convolution_convert_fusion = bf16[896,1024]{1,0:T(8,128)(2,1)} fusion(bf16[2048,896]{1,0:T(8,128)(2,1)} %bitcast.29, bf16[2048,1024]{1,0:T(8,128)(2,1)} %bitcast.23), kind=kOutput, calls=%fused_computation.1 | convolution fusion | flops 3759013888 | bytes 9699328 | tf_op jit(solution)/shard_map/dot_general | solution.py:19
  171.9 6.6 %fusion.20.refs_0_ = f32[2048,896]{1,0:T(8,128)} fusion(bf16[2048,1024]{1,0:T(8,128)(2,1)S(1)} %bitcast.24, bf16[896,1024]{1,0:T(8,128)(2,1)S(1)} %copy-done.9), kind=kOutput, calls=%fused_computation.43 | convolution fusion | flops 3758096384 | bytes 13369344 | tf_op jit(solution)/shard_map/dot_general | solution.py:25
  178.5 127.9 %shard_map.131 = f32[8,256,896]{2,1,0:T(8,128)} custom-call(f32[2048,896]{1,0:T(8,128)} %fusion.20.refs_0_), custom_call_target="tpu_custom_call" | custom-call | tf_op jit(solution)/shard_map/pallas_call | solution.py:105
  306.4 0.0 copy-start.2
  306.4 3.6 reduce_sum.76
  310.0 2.8 fusion.11
  312.8 120.8 %shard_map.132 = (bf16[8,256,896]{2,1,0:T(8,128)(2,1)}, bf16[8,256,896]{2,1,0:T(8,128)(2,1)}) custom-call(bf16[256,896]{1,0:T(8,128)(2,1)} %get-tuple-element.15.refs_0_, bf16[256,896]{1,0:T(8,128)(2,1)} %get-tuple-element.14.refs_1_), custom_call_target="tpu_custom_call" | custom-call | tf_op jit(solution)/shard_map/pallas_call | solution.py:105
  433.6 9.3 %convolution_convert_fusion.1 = bf16[1024,896]{1,0:T(8,128)(2,1)} fusion(bf16[2048,1024]{1,0:T(8,128)(2,1)} %bitcast.21, bf16[2048,896]{1,0:T(8,128)(2,1)} %bitcast.25), kind=kOutput, calls=%fused_computation.2 | convolution fusion | flops 3759013888 | bytes 9699328 | tf_op jit(solution)/shard_map/dot_general | solution.py:19
  442.9 5.7 convolution_convert_fusion.2
  448.6 4.6 fusion.21
  453.2 0.0 copy-done.7
  453.2 7.2 %convolution_add_fusion.refs_0_ = f32[2048,1024]{1,0:T(8,128)} fusion(f32[2048,1024]{1,0:T(8,128)S(1)} %fusion.21, bf16[2048,896]{1,0:T(8,128)(2,1)S(1)} %bitcast.26, bf16[1024,896]{1,0:T(8,128)(2,1)S(1)} %copy-done.10), kind=kOutput, calls=%fused_computation | convolution fusion | flops 3760193536 | bytes 22282240 | tf_op jit(solution)/shard_map/dot_general | solution.py:25
  460.4 147.2 %shard_map.133 = f32[16,128,1024]{2,1,0:T(8,128)} custom-call(f32[2048,1024]{1,0:T(8,128)} %convolution_add_fusion.refs_0_), custom_call_target="tpu_custom_call" | custom-call | tf_op jit(solution)/shard_map/pallas_call | solution.py:105
  607.6 0.0 copy-start.1
  607.6 0.0 copy-start.4
  607.7 0.0 copy-start.3
  607.7 4.3 reduce_sum.77
  612.0 0.7 fusion.15
  612.6 7.6 %shard_map.134 = f32[8,1,128]{2,1,0:T(1,128)} custom-call(f32[1,128]{1,0:T(1,128)} %bitcast.20), custom_call_target="tpu_custom_call" | custom-call | tf_op jit(solution)/shard_map/pallas_call | solution.py:105
  620.2 0.7 reduce_sum.79
  620.9 0.9 fusion.19
  (18 shorter events, 0.1 us)
Async XLA Ops:
  0.6 448.0 %copy-start = (bf16[1024,896]{1,0:T(8,128)(2,1)S(1)}, bf16[1024,896]{1,0:T(8,128)(2,1)}, u32[]{:S(2)}) copy-start(bf16[1024,896]{1,0:T(8,128)(2,1)} %param.17) | copy-start | bytes 5505028
  163.2 8.7 %copy-start.6 = (bf16[16,128,1024]{2,1,0:T(8,128)(2,1)S(1)}, bf16[16,128,1024]{2,1,0:T(8,128)(2,1)}, u32[]{:S(2)}) copy-start(bf16[16,128,1024]{2,1,0:T(8,128)(2,1)} %get-tuple-element.9) | copy-start | bytes 12582916
  163.2 8.7 %copy-start.9 = (bf16[896,1024]{1,0:T(8,128)(2,1)S(1)}, bf16[896,1024]{1,0:T(8,128)(2,1)}, u32[]{:S(2)}) copy-start(bf16[896,1024]{1,0:T(8,128)(2,1)} %param.19) | copy-start | bytes 5505028
  306.4 3.6 copy-start.2
  433.6 9.3 %copy-start.5 = (bf16[16,128,1024]{2,1,0:T(8,128)(2,1)S(1)}, bf16[16,128,1024]{2,1,0:T(8,128)(2,1)}, u32[]{:S(2)}) copy-start(bf16[16,128,1024]{2,1,0:T(8,128)(2,1)} %get-tuple-element.12) | copy-start | bytes 12582916
  433.6 9.3 %copy-start.8 = (bf16[8,256,896]{2,1,0:T(8,128)(2,1)S(1)}, bf16[8,256,896]{2,1,0:T(8,128)(2,1)}, u32[]{:S(2)}) copy-start(bf16[8,256,896]{2,1,0:T(8,128)(2,1)} %get-tuple-element.10) | copy-start | bytes 11010052
  448.6 4.6 copy-start.7
  448.6 4.6 copy-start.10
  607.6 4.3 copy-start.1
  607.6 4.3 copy-start.4
  607.7 13.3 %copy-start.3 = (bf16[128,1024]{1,0:T(8,128)(2,1)S(1)}, bf16[128,1024]{1,0:T(8,128)(2,1)}, u32[]{:S(2)}) copy-start(bf16[128,1024]{1,0:T(8,128)(2,1)} %refs_0_.1) | copy-start | bytes 786436

commit v3 on v2

--- a/solution.py
+++ b/solution.py
@@ -10,6 +10,7 @@
 D = 8192
 SEGS = 16
 AXES = ("row", "col")
+WIRE = jnp.float32
 
 eps = 1e-05
 keep_scale = 1.0 / 0.9
@@ -65,10 +66,10 @@
             )
             c.start()
             sends.append(c)
-        src = ins[i] if mode == "gather" else ins[i].at[pl.ds(me * m, m)]
-        loc = pltpu.make_async_copy(src, outs[i].at[me], local_sem.at[i])
-        loc.start()
-        sends.append(loc)
+        if mode == "gather":
+            loc = pltpu.make_async_copy(ins[i], outs[i].at[me], local_sem.at[i])
+            loc.start()
+            sends.append(loc)
     for c in sends:
         if c.is_remote:
             c.wait_send()
@@ -116,6 +117,18 @@
     )(*[x for x, _, _ in items])
 
 
+def reduce_scatter(parts, axis, cid, extra=()):
+    k = lax.axis_size(axis)
+    me = lax.axis_index(axis)
+    m = parts.shape[0] // k
+    outs = exchange([(parts.astype(WIRE), axis, "scatter")] + list(extra), cid)
+    slots = outs[0]
+    mine = lax.dynamic_slice_in_dim(parts, me * m, m, axis=0)
+    keep = (jnp.arange(k) != me).reshape((k,) + (1,) * (slots.ndim - 1))
+    other = jnp.sum(jnp.where(keep, slots.astype(jnp.float32), 0.0), axis=0)
+    return (mine + other,) + tuple(outs[1:])
+
+
 def per_device(
     stream_in, grad_out, gate_pre, up_pre, keep_mask, segment_ids, norm_gain, w_gate, w_up, w_down
 ):
@@ -140,14 +153,13 @@
     sig = jax.nn.sigmoid(gate_f)
     keep_f = keep_mask.astype(jnp.float32) * keep_scale
     dropped = (gate_f * sig * up_f * keep_f * weights[:, None]).astype(jnp.bfloat16)
-    cot_full, normed_full, dropped_full = exchange(
-        [(grad_out, "col", "gather"), (normed, "col", "gather"), (dropped, "row", "gather")], 1
-    )
+    cot_full, dropped_full = exchange([(grad_out, "col", "gather"), (dropped, "row", "gather")], 1)
     cot_full = cot_full.reshape(total, feat_loc)
+    dropped_full = dropped_full.reshape(total, ff_loc)
+    back, normed_full = reduce_scatter(
+        over_width(cot_full, w_down), "row", 2, [(normed, "col", "gather")]
+    )
     normed_full = normed_full.reshape(total, feat_loc)
-    dropped_full = dropped_full.reshape(total, ff_loc)
-    (back_parts,) = exchange([(over_width(cot_full, w_down), "row", "scatter")], 2)
-    back = jnp.sum(back_parts, axis=0)
     grad_act = back * weights[:, None] * keep_f
     grad_gpre = (grad_act * up_f * sig * (1.0 + gate_f * (1.0 - sig))).astype(jnp.bfloat16)
     grad_upre = (grad_act * gate_f * sig).astype(jnp.bfloat16)
@@ -158,8 +170,7 @@
     grad_gate = over_tokens(normed_full, gpre_full).astype(jnp.bfloat16)
     grad_up = over_tokens(normed_full, upre_full).astype(jnp.bfloat16)
     partial = over_width(gpre_full, w_gate) + over_width(upre_full, w_up)
-    (gn_parts,) = exchange([(partial, "col", "scatter")], 4)
-    grad_normed = jnp.sum(gn_parts, axis=0)
+    (grad_normed,) = reduce_scatter(partial, "col", 4)
     scaled = grad_normed * norm_gain[None, :]
     (inner_all,) = exchange([(jnp.sum(scaled * xs, axis=1)[None, :], "row", "gather")], 5)
     inner = jnp.sum(inner_all, axis=(0, 1)) / D

time: 622 us -> 601 us (0.966)
  Pallas kernels: 557 us -> 533 us
    pallas_call x6, Pallas kernels: 557 us -> 533 us  [exchange(): pl.pallas_call(functools.partial(_exchange_kernel, modes, axes), out_shap...]
where the time goes in v3:
time: 601 us
  Pallas kernels  533 us (89%)
  matrix products  42 us (7%)
  other arithmetic  25 us (4%)
    pallas_call x6, Pallas kernels, exchange(): pl.pallas_call(functools.partial(_exchange_kernel, modes, axes), out_shap...  533 us
    dot_general x3, matrix products, over_tokens(): lax.dot_general(left, right, (((0,), (0,)), ((), ())), preferred_element_...  23.6 us
    dot_general x3, matrix products, over_width(): lax.dot_general(left, right, (((1,), (1,)), ((), ())), preferred_element_...  18.4 us

profile of v3, /device:TPU:64, one launch (start us, length us, event | category | flops | bytes accessed | tf_op | source)
XLA Modules:
  0.0 600.9 jit_solution(11993562475672596823)
XLA Ops:
  0.6 0.0 copy-start
  0.7 0.9 convert_reduce_fusion
  1.6 1.1 fusion.12
  2.7 0.6 pad_maximum_fusion
  3.3 7.7 %shard_map.129 = f32[8,1,144]{2,1,0:T(1,128)} custom-call(f32[1,144]{1,0:T(1,128)} %bitcast.19), custom_call_target="tpu_custom_call" | custom-call | tf_op jit(solution)/shard_map/pallas_call | solution.py:106
  10.9 0.7 reduce_sum.74
  11.7 0.8 select_reduce_fusion.2
  12.4 1.8 fusion.14.refs_1_
  14.2 2.6 fusion.2.refs_1_
  16.8 91.1 %shard_map.130 = (bf16[16,128,1024]{2,1,0:T(8,128)(2,1)}, bf16[8,256,896]{2,1,0:T(8,128)(2,1)}) custom-call(bf16[128,1024]{1,0:T(8,128)(2,1)} %refs_0_.1, bf16[256,896]{1,0:T(8,128)(2,1)} %fusion.2.refs_1_), custom_call_target="tpu_custom_call" | custom-call | tf_op jit(solution)/shard_map/pallas_call | solution.py:106
  108.0 0.0 copy-start.12
  108.0 8.7 %convolution_convert_fusion = bf16[896,1024]{1,0:T(8,128)(2,1)} fusion(bf16[2048,896]{1,0:T(8,128)(2,1)} %bitcast.29, bf16[2048,1024]{1,0:T(8,128)(2,1)} %bitcast.23), kind=kOutput, calls=%fused_computation.3 | convolution fusion | flops 3759013888 | bytes 9699328 | tf_op jit(solution)/shard_map/dot_general | solution.py:20
  116.7 6.6 %fusion.20.refs_0_ = f32[2048,896]{1,0:T(8,128)} fusion(bf16[2048,1024]{1,0:T(8,128)(2,1)S(1)} %bitcast.24, bf16[896,1024]{1,0:T(8,128)(2,1)S(1)} %copy-done.12), kind=kOutput, calls=%fused_computation.48 | convolution fusion | flops 3758096384 | bytes 13369344 | tf_op jit(solution)/shard_map/dot_general | solution.py:26
  123.3 148.6 %shard_map.131 = (f32[8,256,896]{2,1,0:T(8,128)}, bf16[16,128,1024]{2,1,0:T(8,128)(2,1)}) custom-call(f32[2048,896]{1,0:T(8,128)} %fusion.20.refs_0_, bf16[128,1024]{1,0:T(8,128)(2,1)} %fusion.14.refs_1_), custom_call_target="tpu_custom_call" | custom-call | tf_op jit(solution)/shard_map/pallas_call | solution.py:106
  271.9 0.0 copy-start.4
  271.9 3.9 select_reduce_fusion.1
  275.8 0.0 copy-start.5
  275.8 2.4 fusion.11
  278.2 1.2 fusion.5.refs_0_
  279.4 116.2 %shard_map.132 = (bf16[8,256,896]{2,1,0:T(8,128)(2,1)}, bf16[8,256,896]{2,1,0:T(8,128)(2,1)}) custom-call(bf16[256,896]{1,0:T(8,128)(2,1)} %fusion.5.refs_0_, bf16[256,896]{1,0:T(8,128)(2,1)} %get-tuple-element.16.refs_1_), custom_call_target="tpu_custom_call" | custom-call | tf_op jit(solution)/shard_map/pallas_call | solution.py:106
  395.6 9.3 %convolution_convert_fusion.1 = bf16[1024,896]{1,0:T(8,128)(2,1)} fusion(bf16[2048,1024]{1,0:T(8,128)(2,1)} %bitcast.21, bf16[2048,896]{1,0:T(8,128)(2,1)} %bitcast.25), kind=kOutput, calls=%fused_computation.4 | convolution fusion | flops 3759013888 | bytes 9699328 | tf_op jit(solution)/shard_map/dot_general | solution.py:20
  404.8 5.7 convolution_convert_fusion.2
  410.5 4.6 fusion.21
  415.1 7.2 %convolution_add_fusion.refs_0_ = f32[2048,1024]{1,0:T(8,128)} fusion(f32[2048,1024]{1,0:T(8,128)S(1)} %fusion.21, bf16[2048,896]{1,0:T(8,128)(2,1)S(1)} %bitcast.26, bf16[1024,896]{1,0:T(8,128)(2,1)S(1)} %copy-done.13), kind=kOutput, calls=%fused_computation.2 | convolution fusion | flops 3760193536 | bytes 22282240 | tf_op jit(solution)/shard_map/dot_general | solution.py:26
  422.4 160.6 %shard_map.133 = f32[16,128,1024]{2,1,0:T(8,128)} custom-call(f32[2048,1024]{1,0:T(8,128)} %convolution_add_fusion.refs_0_), custom_call_target="tpu_custom_call" | custom-call | tf_op jit(solution)/shard_map/pallas_call | solution.py:106
  583.0 0.0 copy-start.6
  583.0 0.0 copy-start.1
  583.0 4.7 select_reduce_fusion
  587.7 1.7 fusion.15
  589.5 8.7 %shard_map.134 = f32[8,1,128]{2,1,0:T(1,128)} custom-call(f32[1,128]{1,0:T(1,128)} %bitcast.20), custom_call_target="tpu_custom_call" | custom-call | tf_op jit(solution)/shard_map/pallas_call | solution.py:106
  598.2 0.7 reduce_sum.79
  598.9 2.0 fusion.19
  (27 shorter events, 0.1 us)
Async XLA Ops:
  0.6 409.9 %copy-start = (bf16[1024,896]{1,0:T(8,128)(2,1)S(1)}, bf16[1024,896]{1,0:T(8,128)(2,1)}, u32[]{:S(2)}) copy-start(bf16[1024,896]{1,0:T(8,128)(2,1)} %param.17) | copy-start | bytes 5505028
  108.0 8.7 %copy-start.9 = (bf16[16,128,1024]{2,1,0:T(8,128)(2,1)S(1)}, bf16[16,128,1024]{2,1,0:T(8,128)(2,1)}, u32[]{:S(2)}) copy-start(bf16[16,128,1024]{2,1,0:T(8,128)(2,1)} %get-tuple-element.10) | copy-start | bytes 12582916
  108.0 8.7 %copy-start.12 = (bf16[896,1024]{1,0:T(8,128)(2,1)S(1)}, bf16[896,1024]{1,0:T(8,128)(2,1)}, u32[]{:S(2)}) copy-start(bf16[896,1024]{1,0:T(8,128)(2,1)} %param.19) | copy-start | bytes 5505028
  271.9 3.9 copy-start.3
  271.9 3.9 copy-start.4
  275.8 2.4 copy-start.5
  395.6 9.3 %copy-start.8 = (bf16[16,128,1024]{2,1,0:T(8,128)(2,1)S(1)}, bf16[16,128,1024]{2,1,0:T(8,128)(2,1)}, u32[]{:S(2)}) copy-start(bf16[16,128,1024]{2,1,0:T(8,128)(2,1)} %get-tuple-element.14) | copy-start | bytes 12582916
  395.6 9.3 %copy-start.11 = (bf16[8,256,896]{2,1,0:T(8,128)(2,1)S(1)}, bf16[8,256,896]{2,1,0:T(8,128)(2,1)}, u32[]{:S(2)}) copy-start(bf16[8,256,896]{2,1,0:T(8,128)(2,1)} %get-tuple-element.12) | copy-start | bytes 11010052
  410.5 4.6 copy-start.10
  410.5 4.6 copy-start.13
  583.0 4.7 copy-start.2
  583.0 4.7 copy-start.7
  583.0 15.9 %copy-start.6 = (bf16[128,1024]{1,0:T(8,128)(2,1)S(1)}, bf16[128,1024]{1,0:T(8,128)(2,1)}, u32[]{:S(2)}) copy-start(bf16[128,1024]{1,0:T(8,128)(2,1)} %refs_0_.1) | copy-start | bytes 786436
  583.0 17.8 %copy-start.1 = (bf16[1024,896]{1,0:T(8,128)(2,1)S(1)}, bf16[1024,896]{1,0:T(8,128)(2,1)}, u32[]{:S(2)}) copy-start(bf16[1024,896]{1,0:T(8,128)(2,1)} %param.17) | copy-start | bytes 5505028

commit v4 on v3

--- a/solution.py
+++ b/solution.py
@@ -10,7 +10,7 @@
 D = 8192
 SEGS = 16
 AXES = ("row", "col")
-WIRE = jnp.float32
+WIRE = jnp.bfloat16
 
 eps = 1e-05
 keep_scale = 1.0 / 0.9

time: 601 us -> 466 us (0.78)
  Pallas kernels: 533 us -> 398 us
    pallas_call x6, Pallas kernels: 533 us -> 398 us  [exchange(): pl.pallas_call(functools.partial(_exchange_kernel, modes, axes), out_shap...]
where the time goes in v4:
time: 466 us; the launch traced here: 465 us
  Pallas kernels  398 us (85%)
  matrix products  43.3 us (9%)
  other arithmetic  22.8 us (5%)
    pallas_call x6, Pallas kernels, exchange(): pl.pallas_call(functools.partial(_exchange_kernel, modes, axes), out_shap...  398 us
    dot_general x3, matrix products, over_tokens(): lax.dot_general(left, right, (((0,), (0,)), ((), ())), preferred_element_...  23.6 us
    dot_general x3, matrix products, over_width(): lax.dot_general(left, right, (((1,), (1,)), ((), ())), preferred_element_...  19.6 us

profile of v4, /device:TPU:64, one launch (start us, length us, event | category | flops | bytes accessed | tf_op | source)
XLA Modules:
  0.0 465.2 jit_solution(6282576661351428851)
XLA Ops:
  0.6 0.0 copy-start
  0.7 0.9 convert_reduce_fusion
  1.6 1.1 fusion.12
  2.7 0.6 pad_maximum_fusion
  3.3 7.7 %shard_map.129 = f32[8,1,144]{2,1,0:T(1,128)} custom-call(f32[1,144]{1,0:T(1,128)} %bitcast.19), custom_call_target="tpu_custom_call" | custom-call | tf_op jit(solution)/shard_map/pallas_call | solution.py:106
  10.9 0.7 reduce_sum.74
  11.7 0.8 select_reduce_fusion.2
  12.4 1.8 fusion.14.refs_1_
  14.2 2.6 fusion.2.refs_1_
  16.8 91.1 %shard_map.130 = (bf16[16,128,1024]{2,1,0:T(8,128)(2,1)}, bf16[8,256,896]{2,1,0:T(8,128)(2,1)}) custom-call(bf16[128,1024]{1,0:T(8,128)(2,1)} %refs_0_.1, bf16[256,896]{1,0:T(8,128)(2,1)} %fusion.2.refs_1_), custom_call_target="tpu_custom_call" | custom-call | tf_op jit(solution)/shard_map/pallas_call | solution.py:106
  108.0 0.0 copy-start.11
  108.0 8.7 %convolution_convert_fusion = bf16[896,1024]{1,0:T(8,128)(2,1)} fusion(bf16[2048,896]{1,0:T(8,128)(2,1)} %bitcast.29, bf16[2048,1024]{1,0:T(8,128)(2,1)} %bitcast.23), kind=kOutput, calls=%fused_computation.3 | convolution fusion | flops 3759013888 | bytes 9699328 | tf_op jit(solution)/shard_map/dot_general | solution.py:20
  116.7 7.4 %fusion.20 = (bf16[2048,896]{1,0:T(8,128)(2,1)}, f32[2048,896]{1,0:T(8,128)}) fusion(bf16[2048,1024]{1,0:T(8,128)(2,1)S(1)} %bitcast.24, bf16[896,1024]{1,0:T(8,128)(2,1)S(1)} %copy-done.11), kind=kOutput, calls=%fused_computation.48 | convolution fusion | flops 3759931392 | bytes 17039360 | tf_op jit(solution)/shard_map/dot_general | solution.py:26
  124.1 94.0 %shard_map.131 = (bf16[8,256,896]{2,1,0:T(8,128)(2,1)}, bf16[16,128,1024]{2,1,0:T(8,128)(2,1)}) custom-call(bf16[2048,896]{1,0:T(8,128)(2,1)} %get-tuple-element.18.refs_0_, bf16[128,1024]{1,0:T(8,128)(2,1)} %fusion.14.refs_1_), custom_call_target="tpu_custom_call" | custom-call | tf_op jit(solution)/shard_map/pallas_call | solution.py:106
  218.1 0.0 copy-start.4
  218.1 3.0 select_reduce_fusion.1
  221.1 2.4 fusion.11
  223.5 1.2 fusion.5.refs_0_
  224.6 117.6 %shard_map.132 = (bf16[8,256,896]{2,1,0:T(8,128)(2,1)}, bf16[8,256,896]{2,1,0:T(8,128)(2,1)}) custom-call(bf16[256,896]{1,0:T(8,128)(2,1)} %fusion.5.refs_0_, bf16[256,896]{1,0:T(8,128)(2,1)} %get-tuple-element.16.refs_1_), custom_call_target="tpu_custom_call" | custom-call | tf_op jit(solution)/shard_map/pallas_call | solution.py:106
  342.2 9.3 %convolution_convert_fusion.1 = bf16[1024,896]{1,0:T(8,128)(2,1)} fusion(bf16[2048,1024]{1,0:T(8,128)(2,1)} %bitcast.21, bf16[2048,896]{1,0:T(8,128)(2,1)} %bitcast.25), kind=kOutput, calls=%fused_computation.4 | convolution fusion | flops 3759013888 | bytes 9699328 | tf_op jit(solution)/shard_map/dot_general | solution.py:20
  351.5 5.7 %convolution_convert_fusion.2 = bf16[1024,896]{1,0:T(8,128)(2,1)} fusion(bf16[2048,1024]{1,0:T(8,128)(2,1)S(1)} %bitcast.22, bf16[2048,896]{1,0:T(8,128)(2,1)S(1)} %bitcast.27), kind=kOutput, calls=%fused_computation.5 | convolution fusion | flops 3759013888 | bytes 9699328 | tf_op jit(solution)/shard_map/dot_general | solution.py:20
  357.2 4.7 %fusion.22 = f32[2048,1024]{1,0:T(8,128)S(1)} fusion(bf16[2048,896]{1,0:T(8,128)(2,1)S(1)} %bitcast.28, bf16[1024,896]{1,0:T(8,128)(2,1)S(1)} %copy-done.12), kind=kOutput, calls=%fused_computation.50 | convolution fusion | flops 3758096384 | bytes 13893632 | tf_op jit(solution)/shard_map/dot_general | solution.py:26
  361.9 7.6 %fusion.21 = (bf16[2048,1024]{1,0:T(8,128)(2,1)}, f32[2048,1024]{1,0:T(8,128)}) fusion(f32[2048,1024]{1,0:T(8,128)S(1)} %fusion.22, bf16[2048,896]{1,0:T(8,128)(2,1)S(1)} %bitcast.26, bf16[1024,896]{1,0:T(8,128)(2,1)S(1)} %copy-done), kind=kOutput, calls=%fused_computation.49 | convolution fusion | flops 3762290688 | bytes 26476544 | tf_op jit(solution)/shard_map/dot_general | solution.py:26
  369.5 74.0 %shard_map.133 = bf16[16,128,1024]{2,1,0:T(8,128)(2,1)} custom-call(bf16[2048,1024]{1,0:T(8,128)(2,1)} %get-tuple-element.20.refs_0_), custom_call_target="tpu_custom_call" | custom-call | tf_op jit(solution)/shard_map/pallas_call | solution.py:106
  443.5 0.0 copy-start.1
  443.5 0.0 copy-start.6
  443.5 0.0 copy-start.5
  443.6 3.4 select_reduce_fusion
  446.9 1.7 fusion.15
  448.7 13.8 %shard_map.134 = f32[8,1,128]{2,1,0:T(1,128)} custom-call(f32[1,128]{1,0:T(1,128)} %bitcast.20), custom_call_target="tpu_custom_call" | custom-call | tf_op jit(solution)/shard_map/pallas_call | solution.py:106
  462.5 0.7 reduce_sum.79
  463.2 2.0 fusion.19
  (25 shorter events, 0.1 us)
Async XLA Ops:
  0.6 361.3 %copy-start = (bf16[1024,896]{1,0:T(8,128)(2,1)S(1)}, bf16[1024,896]{1,0:T(8,128)(2,1)}, u32[]{:S(2)}) copy-start(bf16[1024,896]{1,0:T(8,128)(2,1)} %param.18) | copy-start | bytes 5505028
  108.0 8.7 %copy-start.8 = (bf16[16,128,1024]{2,1,0:T(8,128)(2,1)S(1)}, bf16[16,128,1024]{2,1,0:T(8,128)(2,1)}, u32[]{:S(2)}) copy-start(bf16[16,128,1024]{2,1,0:T(8,128)(2,1)} %get-tuple-element.10) | copy-start | bytes 12582916
  108.0 8.7 %copy-start.11 = (bf16[896,1024]{1,0:T(8,128)(2,1)S(1)}, bf16[896,1024]{1,0:T(8,128)(2,1)}, u32[]{:S(2)}) copy-start(bf16[896,1024]{1,0:T(8,128)(2,1)} %param.19) | copy-start | bytes 5505028
  124.1 97.0 %copy-start.2 = (bf16[256,896]{1,0:T(8,128)(2,1)S(1)}, bf16[256,896]{1,0:T(8,128)(2,1)}, u32[]{:S(2)}) copy-start(bf16[256,896]{1,0:T(8,128)(2,1)} %param.12) | copy-start | bytes 1376260
  124.1 97.0 %copy-start.3 = (s32[256,896]{1,0:T(8,128)S(1)}, s32[256,896]{1,0:T(8,128)}, u32[]{:S(2)}) copy-start(s32[256,896]{1,0:T(8,128)} %param.14) | copy-start | bytes 2752516
  218.1 5.4 %copy-start.4 = (bf16[256,896]{1,0:T(8,128)(2,1)S(1)}, bf16[256,896]{1,0:T(8,128)(2,1)}, u32[]{:S(2)}) copy-start(bf16[256,896]{1,0:T(8,128)(2,1)} %param.13) | copy-start | bytes 1376260
  342.2 9.3 %copy-start.7 = (bf16[16,128,1024]{2,1,0:T(8,128)(2,1)S(1)}, bf16[16,128,1024]{2,1,0:T(8,128)(2,1)}, u32[]{:S(2)}) copy-start(bf16[16,128,1024]{2,1,0:T(8,128)(2,1)} %get-tuple-element.14) | copy-start | bytes 12582916
  342.2 9.3 %copy-start.10 = (bf16[8,256,896]{2,1,0:T(8,128)(2,1)S(1)}, bf16[8,256,896]{2,1,0:T(8,128)(2,1)}, u32[]{:S(2)}) copy-start(bf16[8,256,896]{2,1,0:T(8,128)(2,1)} %get-tuple-element.12) | copy-start | bytes 11010052
  351.5 5.7 %copy-start.12 = (bf16[1024,896]{1,0:T(8,128)(2,1)S(1)}, bf16[1024,896]{1,0:T(8,128)(2,1)}, u32[]{:S(2)}) copy-start(bf16[1024,896]{1,0:T(8,128)(2,1)} %param.17) | copy-start | bytes 5505028
  357.2 4.7 %copy-start.9 = (bf16[8,256,896]{2,1,0:T(8,128)(2,1)S(1)}, bf16[8,256,896]{2,1,0:T(8,128)(2,1)}, u32[]{:S(2)}) copy-start(bf16[8,256,896]{2,1,0:T(8,128)(2,1)} %get-tuple-element.13) | copy-start | bytes 11010052
  443.5 3.4 copy-start.1
  443.5 3.4 copy-start.6
  443.5 19.7 %copy-start.5 = (bf16[128,1024]{1,0:T(8,128)(2,1)S(1)}, bf16[128,1024]{1,0:T(8,128)(2,1)}, u32[]{:S(2)}) copy-start(bf16[128,1024]{1,0:T(8,128)(2,1)} %refs_0_.1) | copy-start | bytes 786436

commit v5 on v4

--- a/solution.py
+++ b/solution.py
@@ -163,14 +163,37 @@
     grad_act = back * weights[:, None] * keep_f
     grad_gpre = (grad_act * up_f * sig * (1.0 + gate_f * (1.0 - sig))).astype(jnp.bfloat16)
     grad_upre = (grad_act * gate_f * sig).astype(jnp.bfloat16)
-    gpre_full, upre_full = exchange([(grad_gpre, "row", "gather"), (grad_upre, "row", "gather")], 3)
-    gpre_full = gpre_full.reshape(total, ff_loc)
-    upre_full = upre_full.reshape(total, ff_loc)
+    half = tok_col // 2
+    n_chunk = tok_row // tok_col
+
+    def split(v):
+        v = v.reshape(n_chunk, 2, half, ff_loc)
+        return v[:, 0].reshape(tok_row // 2, ff_loc), v[:, 1].reshape(tok_row // 2, ff_loc)
+
+    def joined(a, b):
+        a = a.reshape(n_row, n_chunk, 1, half, ff_loc)
+        b = b.reshape(n_row, n_chunk, 1, half, ff_loc)
+        return jnp.concatenate([a, b], axis=2).reshape(total, ff_loc)
+
+    gpre_a, gpre_b = split(grad_gpre)
+    upre_a, upre_b = split(grad_upre)
+    ga_full, ua_full = exchange([(gpre_a, "row", "gather"), (upre_a, "row", "gather")], 3)
+    ga_full = ga_full.reshape(total // 2, ff_loc)
+    ua_full = ua_full.reshape(total // 2, ff_loc)
+    part_a = over_width(ga_full, w_gate) + over_width(ua_full, w_up)
+    gn_a, gb_full, ub_full = reduce_scatter(
+        part_a, "col", 4, [(gpre_b, "row", "gather"), (upre_b, "row", "gather")]
+    )
+    gb_full = gb_full.reshape(total // 2, ff_loc)
+    ub_full = ub_full.reshape(total // 2, ff_loc)
+    part_b = over_width(gb_full, w_gate) + over_width(ub_full, w_up)
+    (gn_b,) = reduce_scatter(part_b, "col", 6)
+    grad_normed = jnp.concatenate([gn_a, gn_b], axis=0)
+    gpre_full = joined(ga_full, gb_full)
+    upre_full = joined(ua_full, ub_full)
     grad_down = over_tokens(dropped_full, cot_full).astype(jnp.bfloat16)
     grad_gate = over_tokens(normed_full, gpre_full).astype(jnp.bfloat16)
     grad_up = over_tokens(normed_full, upre_full).astype(jnp.bfloat16)
-    partial = over_width(gpre_full, w_gate) + over_width(upre_full, w_up)
-    (grad_normed,) = reduce_scatter(partial, "col", 4)
     scaled = grad_normed * norm_gain[None, :]
     (inner_all,) = exchange([(jnp.sum(scaled * xs, axis=1)[None, :], "row", "gather")], 5)
     inner = jnp.sum(inner_all, axis=(0, 1)) / D

time: 466 us -> 440 us (0.944)
  Pallas kernels: 398 us -> 369 us
    pallas_call x6 -> x7, Pallas kernels: 398 us -> 369 us  [exchange(): pl.pallas_call(functools.partial(_exchange_kernel, modes, axes), out_shap...]
    dot_general x3 -> x5, matrix products: 19.6 us -> 24.3 us  [over_width(): lax.dot_general(left, right, (((1,), (1,)), ((), ())), preferred_element_...]
where the time goes in v5:
time: 440 us
  Pallas kernels  369 us (84%)
  matrix products  44.6 us (10%)
  other arithmetic  23.3 us (5%)
    pallas_call x7, Pallas kernels, exchange(): pl.pallas_call(functools.partial(_exchange_kernel, modes, axes), out_shap...  369 us
    dot_general x5, matrix products, over_width(): lax.dot_general(left, right, (((1,), (1,)), ((), ())), preferred_element_...  24.3 us
    dot_general x3, matrix products, over_tokens(): lax.dot_general(left, right, (((0,), (0,)), ((), ())), preferred_element_...  20.3 us

profile of v5, /device:TPU:64, one launch (start us, length us, event | category | flops | bytes accessed | tf_op | source)
XLA Modules:
  0.0 439.8 jit_solution(3483177430891600174)
XLA Ops:
  0.7 0.9 convert_reduce_fusion
  1.6 1.1 fusion.12
  3.3 7.7 %shard_map.129 = f32[8,1,144]{2,1,0:T(1,128)} custom-call(f32[1,144]{1,0:T(1,128)} %bitcast.69), custom_call_target="tpu_custom_call" | custom-call | tf_op jit(solution)/shard_map/pallas_call | solution.py:106
  10.9 0.7 reduce_sum.83
  11.7 0.8 select_reduce_fusion.3
  12.4 1.8 fusion.14.refs_1_
  14.2 2.6 fusion.2.refs_1_
  16.8 91.1 %shard_map.130 = (bf16[16,128,1024]{2,1,0:T(8,128)(2,1)}, bf16[8,256,896]{2,1,0:T(8,128)(2,1)}) custom-call(bf16[128,1024]{1,0:T(8,128)(2,1)} %refs_0_.1, bf16[256,896]{1,0:T(8,128)(2,1)} %fusion.2.refs_1_), custom_call_target="tpu_custom_call" | custom-call | tf_op jit(solution)/shard_map/pallas_call | solution.py:106
  108.0 8.7 %convolution_convert_fusion = bf16[896,1024]{1,0:T(8,128)(2,1)} fusion(bf16[2048,896]{1,0:T(8,128)(2,1)} %bitcast.75, bf16[2048,1024]{1,0:T(8,128)(2,1)} %bitcast.73), kind=kOutput, calls=%fused_computation.7 | convolution fusion | flops 3759013888 | bytes 9699328 | tf_op jit(solution)/shard_map/dot_general | solution.py:20
  116.7 7.3 %fusion.22 = (bf16[2048,896]{1,0:T(8,128)(2,1)}, f32[2048,896]{1,0:T(8,128)}) fusion(bf16[2048,1024]{1,0:T(8,128)(2,1)S(1)} %bitcast.74, bf16[896,1024]{1,0:T(8,128)(2,1)S(1)} %copy-done.13), kind=kOutput, calls=%fused_computation.56 | convolution fusion | flops 3759931392 | bytes 17039360 | tf_op jit(solution)/shard_map/dot_general | solution.py:26
  124.0 94.0 %shard_map.131 = (bf16[8,256,896]{2,1,0:T(8,128)(2,1)}, bf16[16,128,1024]{2,1,0:T(8,128)(2,1)}) custom-call(bf16[2048,896]{1,0:T(8,128)(2,1)} %get-tuple-element.30.refs_0_, bf16[128,1024]{1,0:T(8,128)(2,1)} %fusion.14.refs_1_), custom_call_target="tpu_custom_call" | custom-call | tf_op jit(solution)/shard_map/pallas_call | solution.py:106
  218.1 2.9 select_reduce_fusion
  221.0 1.7 fusion.11
  222.7 0.8 fusion.20
  223.9 0.8 fusion.21
  224.7 58.9 %shard_map.132 = (bf16[8,128,896]{2,1,0:T(8,128)(2,1)}, bf16[8,128,896]{2,1,0:T(8,128)(2,1)}) custom-call(bf16[128,896]{1,0:T(8,128)(2,1)} %bitcast.68, bf16[128,896]{1,0:T(8,128)(2,1)} %bitcast.67), custom_call_target="tpu_custom_call" | custom-call | tf_op jit(solution)/shard_map/pallas_call | solution.py:106
  283.6 4.5 %fusion.25 = f32[1024,1024]{1,0:T(8,128)S(1)} fusion(bf16[1024,896]{1,0:T(8,128)(2,1)} %bitcast.55, bf16[1024,896]{1,0:T(8,128)(2,1)} %param.17), kind=kOutput, calls=%fused_computation.59 | convolution fusion | flops 1879048192 | bytes 7864320 | tf_op jit(solution)/shard_map/dot_general | solution.py:26
  288.2 5.0 %fusion.23 = (bf16[1024,1024]{1,0:T(8,128)(2,1)}, f32[1024,1024]{1,0:T(8,128)}) fusion(f32[1024,1024]{1,0:T(8,128)S(1)} %fusion.25, bf16[1024,896]{1,0:T(8,128)(2,1)S(1)} %bitcast.58, bf16[1024,896]{1,0:T(8,128)(2,1)S(1)} %copy-done), kind=kOutput, calls=%fused_computation.57 | convolution fusion | flops 1881145344 | bytes 14155776 | tf_op jit(solution)/shard_map/dot_general | solution.py:26
  293.2 70.7 %shard_map.133 = (bf16[16,64,1024]{2,1,0:T(8,128)(2,1)}, bf16[8,128,896]{2,1,0:T(8,128)(2,1)}, bf16[8,128,896]{2,1,0:T(8,128)(2,1)}) custom-call(bf16[1024,1024]{1,0:T(8,128)(2,1)} %get-tuple-element.32.refs_0_, bf16[128,896]{1,0:T(8,128)(2,1)} %bitcast.66, bf16[128,896]{1,0:T(8,128)(2,1)} %bitcast.65), custom_call_target="tpu_custom_call" | custom-call | tf_op jit(solution)/shard_map/pallas_call | solution.py:106
  364.0 2.6 pad_maximum_fusion.1
  366.5 0.7 copy-done.11
  367.2 5.7 %convolution_convert_fusion.1 = bf16[1024,896]{1,0:T(8,128)(2,1)} fusion(bf16[2048,1024]{1,0:T(8,128)(2,1)S(1)} %bitcast.71, bf16[2048,896]{1,0:T(8,128)(2,1)S(1)} %bitcast.54), kind=kOutput, calls=%fused_computation.8 | convolution fusion | flops 3759013888 | bytes 9699328 | tf_op jit(solution)/shard_map/dot_general | solution.py:20
  373.3 5.9 %convolution_convert_fusion.2 = bf16[1024,896]{1,0:T(8,128)(2,1)} fusion(bf16[2048,1024]{1,0:T(8,128)(2,1)S(1)} %bitcast.72, bf16[2048,896]{1,0:T(8,128)(2,1)S(1)} %bitcast.53), kind=kOutput, calls=%fused_computation.9 | convolution fusion | flops 3759013888 | bytes 9699328 | tf_op jit(solution)/shard_map/dot_general | solution.py:20
  379.2 2.4 fusion.26
  381.6 5.0 %fusion.24 = (bf16[1024,1024]{1,0:T(8,128)(2,1)}, f32[1024,1024]{1,0:T(8,128)}) fusion(f32[1024,1024]{1,0:T(8,128)S(1)} %fusion.26, bf16[1024,896]{1,0:T(8,128)(2,1)S(1)} %bitcast.60, bf16[1024,896]{1,0:T(8,128)(2,1)S(1)} %copy-done), kind=kOutput, calls=%fused_computation.58 | convolution fusion | flops 1881145344 | bytes 14155776 | tf_op jit(solution)/shard_map/dot_general | solution.py:26
  386.6 37.3 %shard_map.134 = bf16[16,64,1024]{2,1,0:T(8,128)(2,1)} custom-call(bf16[1024,1024]{1,0:T(8,128)(2,1)} %get-tuple-element.34.refs_0_), custom_call_target="tpu_custom_call" | custom-call | tf_op jit(solution)/shard_map/pallas_call | solution.py:106
  424.0 3.4 select_reduce_fusion.2
  427.4 1.1 dynamic-slice_add_fusion
  428.6 0.7 fusion.15
  429.2 8.9 %shard_map.135 = f32[8,1,128]{2,1,0:T(1,128)} custom-call(f32[1,128]{1,0:T(1,128)} %bitcast.70), custom_call_target="tpu_custom_call" | custom-call | tf_op jit(solution)/shard_map/pallas_call | solution.py:106
  438.2 0.7 reduce_sum.89
  438.9 0.9 fusion.19
  (37 shorter events, 1.4 us)
Async XLA Ops:
  0.6 287.5 %copy-start = (bf16[1024,896]{1,0:T(8,128)(2,1)S(1)}, bf16[1024,896]{1,0:T(8,128)(2,1)}, u32[]{:S(2)}) copy-start(bf16[1024,896]{1,0:T(8,128)(2,1)} %param.18) | copy-start | bytes 5505028
  108.0 8.7 %copy-start.12 = (bf16[16,128,1024]{2,1,0:T(8,128)(2,1)S(1)}, bf16[16,128,1024]{2,1,0:T(8,128)(2,1)}, u32[]{:S(2)}) copy-start(bf16[16,128,1024]{2,1,0:T(8,128)(2,1)} %get-tuple-element.13) | copy-start | bytes 12582916
  108.0 8.7 %copy-start.13 = (bf16[896,1024]{1,0:T(8,128)(2,1)S(1)}, bf16[896,1024]{1,0:T(8,128)(2,1)}, u32[]{:S(2)}) copy-start(bf16[896,1024]{1,0:T(8,128)(2,1)} %param.19) | copy-start | bytes 5505028
  124.0 97.0 %copy-start.2 = (bf16[256,896]{1,0:T(8,128)(2,1)S(1)}, bf16[256,896]{1,0:T(8,128)(2,1)}, u32[]{:S(2)}) copy-start(bf16[256,896]{1,0:T(8,128)(2,1)} %param.12) | copy-start | bytes 1376260
  124.0 97.0 %copy-start.3 = (s32[256,896]{1,0:T(8,128)S(1)}, s32[256,896]{1,0:T(8,128)}, u32[]{:S(2)}) copy-start(s32[256,896]{1,0:T(8,128)} %param.14) | copy-start | bytes 2752516
  221.0 2.5 copy-start.8
  283.6 4.6 %copy-start.5 = (bf16[8,128,896]{2,1,0:T(8,128)(2,1)S(1)}, bf16[8,128,896]{2,1,0:T(8,128)(2,1)}, u32[]{:S(2)}) copy-start(bf16[8,128,896]{2,1,0:T(8,128)(2,1)} %get-tuple-element.16) | copy-start | bytes 5505028
  363.9 3.3 copy-start.11
  367.2 5.7 %copy-start.4 = (bf16[8,128,896]{2,1,0:T(8,128)(2,1)S(1)}, bf16[8,128,896]{2,1,0:T(8,128)(2,1)}, u32[]{:S(2)}) copy-start(bf16[8,128,896]{2,1,0:T(8,128)(2,1)} %get-tuple-element.15) | copy-start | bytes 5505028
  367.2 5.7 %copy-start.7 = (bf16[8,128,896]{2,1,0:T(8,128)(2,1)S(1)}, bf16[8,128,896]{2,1,0:T(8,128)(2,1)}, u32[]{:S(2)}) copy-start(bf16[8,128,896]{2,1,0:T(8,128)(2,1)} %get-tuple-element.18) | copy-start | bytes 5505028
  373.3 5.9 %copy-start.14 = (bf16[1024,896]{1,0:T(8,128)(2,1)S(1)}, bf16[1024,896]{1,0:T(8,128)(2,1)}, u32[]{:S(2)}) copy-start(bf16[1024,896]{1,0:T(8,128)(2,1)} %param.17) | copy-start | bytes 5505028
  379.2 2.4 copy-start.6
  424.0 4.6 %copy-start.1 = (bf16[128,1024]{1,0:T(8,128)(2,1)S(1)}, bf16[128,1024]{1,0:T(8,128)(2,1)}, u32[]{:S(2)}) copy-start(bf16[128,1024]{1,0:T(8,128)(2,1)} %param.10) | copy-start | bytes 786436
  424.0 4.6 %copy-start.10 = (f32[1024]{0:T(1024)S(1)}, f32[1024]{0:T(1024)}, u32[]{:S(2)}) copy-start(f32[1024]{0:T(1024)} %param.16) | copy-start | bytes 12292
  424.0 14.9 %copy-start.9 = (bf16[128,1024]{1,0:T(8,128)(2,1)S(1)}, bf16[128,1024]{1,0:T(8,128)(2,1)}, u32[]{:S(2)}) copy-start(bf16[128,1024]{1,0:T(8,128)(2,1)} %refs_0_.1) | copy-start | bytes 786436

commit v6 on v5

--- a/solution.py
+++ b/solution.py
@@ -47,10 +47,10 @@
     pl.semaphore_wait(barrier, count)
 
 
-def _exchange_kernel(modes, axes, *refs):
+def _exchange_kernel(modes, axes, n_deps, *refs):
     n = len(modes)
-    ins, outs = refs[:n], refs[n:2 * n]
-    send_sem, recv_sem, local_sem = refs[2 * n:]
+    ins, outs = refs[:n], refs[n + n_deps:2 * n + n_deps]
+    send_sem, recv_sem, local_sem = refs[2 * n + n_deps:]
     _barrier(axes)
     sends = []
     for i, (mode, axis) in enumerate(zip(modes, axes)):
@@ -88,7 +88,7 @@
             ).wait_recv()
 
 
-def exchange(items, cid):
+def exchange(items, cid, deps=()):
     modes = tuple(mode for _, _, mode in items)
     axes = tuple(axis for _, axis, _ in items)
     out_shapes = []
@@ -104,9 +104,9 @@
             )
     n = len(items)
     return pl.pallas_call(
-        functools.partial(_exchange_kernel, modes, axes),
+        functools.partial(_exchange_kernel, modes, axes, len(deps)),
         out_shape=tuple(out_shapes),
-        in_specs=[pl.BlockSpec(memory_space=pl.ANY)] * n,
+        in_specs=[pl.BlockSpec(memory_space=pl.ANY)] * (n + len(deps)),
         out_specs=tuple(pl.BlockSpec(memory_space=pl.ANY) for _ in range(n)),
         scratch_shapes=[
             pltpu.SemaphoreType.DMA((n, kmax)),
@@ -114,14 +114,18 @@
             pltpu.SemaphoreType.DMA((n,)),
         ],
         compiler_params=pltpu.CompilerParams(collective_id=cid, has_side_effects=True),
-    )(*[x for x, _, _ in items])
-
-
-def reduce_scatter(parts, axis, cid, extra=()):
+        cost_estimate=pl.CostEstimate(
+            flops=0, transcendentals=0,
+            bytes_accessed=sum(int(o.size) * o.dtype.itemsize for o in out_shapes) * 40,
+        ),
+    )(*[x for x, _, _ in items], *deps)
+
+
+def reduce_scatter(parts, axis, cid, extra=(), deps=()):
     k = lax.axis_size(axis)
     me = lax.axis_index(axis)
     m = parts.shape[0] // k
-    outs = exchange([(parts.astype(WIRE), axis, "scatter")] + list(extra), cid)
+    outs = exchange([(parts.astype(WIRE), axis, "scatter")] + list(extra), cid, deps)
     slots = outs[0]
     mine = lax.dynamic_slice_in_dim(parts, me * m, m, axis=0)
     keep = (jnp.arange(k) != me).reshape((k,) + (1,) * (slots.ndim - 1))
@@ -153,13 +157,13 @@
     sig = jax.nn.sigmoid(gate_f)
     keep_f = keep_mask.astype(jnp.float32) * keep_scale
     dropped = (gate_f * sig * up_f * keep_f * weights[:, None]).astype(jnp.bfloat16)
-    cot_full, dropped_full = exchange([(grad_out, "col", "gather"), (dropped, "row", "gather")], 1)
+    dropped_full = lax.all_gather(dropped, "row", axis=0, tiled=True)
+    normed_full = lax.all_gather(normed, "col", axis=0, tiled=True)
+    (cot_full,) = exchange([(grad_out, "col", "gather")], 1)
     cot_full = cot_full.reshape(total, feat_loc)
-    dropped_full = dropped_full.reshape(total, ff_loc)
-    back, normed_full = reduce_scatter(
-        over_width(cot_full, w_down), "row", 2, [(normed, "col", "gather")]
-    )
-    normed_full = normed_full.reshape(total, feat_loc)
+    (back,) = reduce_scatter(
+        over_width(cot_full, w_down), "row", 2, deps=(dropped_full,)
+    )
     grad_act = back * weights[:, None] * keep_f
     grad_gpre = (grad_act * up_f * sig * (1.0 + gate_f * (1.0 - sig))).astype(jnp.bfloat16)
     grad_upre = (grad_act * gate_f * sig).astype(jnp.bfloat16)
@@ -177,7 +181,9 @@
 
     gpre_a, gpre_b = split(grad_gpre)
     upre_a, upre_b = split(grad_upre)
-    ga_full, ua_full = exchange([(gpre_a, "row", "gather"), (upre_a, "row", "gather")], 3)
+    ga_full, ua_full = exchange(
+        [(gpre_a, "row", "gather"), (upre_a, "row", "gather")], 3, (normed_full,)
+    )
     ga_full = ga_full.reshape(total // 2, ff_loc)
     ua_full = ua_full.reshape(total // 2, ff_loc)
     part_a = over_width(ga_full, w_gate) + over_width(ua_full, w_up)

time: 440 us -> 448 us (1.018)
  Pallas kernels: 369 us -> 316 us
  waiting for transfers between devices: 0 us -> 42.3 us
  between operations: 0.89 us -> 14.3 us
    pallas_call x7, Pallas kernels: 369 us -> 316 us  [exchange(): pl.pallas_call(functools.partial(_exchange_kernel, modes, axes, len(deps)...]
    all_gather x0 -> x2, waiting for transfers between devices: none -> 42.2 us  [the longest x1 28.4 us: per_device(): dropped_full = lax.all_gather(dropped, 'row', axis=0, tiled=True)]
    dot_general x5, matrix products: 24.3 us -> 30.6 us  [over_width(): lax.dot_general(left, right, (((1,), (1,)), ((), ())), preferred_element_...]
  transfers between devices with their start and end apart: 0 -> 2, of which waited for: 0 -> 2; matrix products, arithmetic and copies ran while one was open for 0% -> 6% of each run, Pallas kernels for 0% -> 31%
where the time goes in v6:
time: 448 us
  Pallas kernels  316 us (71%)
  matrix products  47 us (10%)
  waiting for transfers between devices  42.3 us (9%)
  other arithmetic  23.5 us (5%)
  between operations  14.3 us (3%)
  local copies, waits for them, and re-layouts  4.75 us (1%)
    pallas_call x7, Pallas kernels, exchange(): pl.pallas_call(functools.partial(_exchange_kernel, modes, axes, len(deps)...  316 us
    dot_general x5, matrix products, over_width(): lax.dot_general(left, right, (((1,), (1,)), ((), ())), preferred_element_...  30.6 us
    all_gather x1, waiting for transfers between devices, per_device(): dropped_full = lax.all_gather(dropped, 'row', axis=0, tiled=True)  28.4 us
    dot_general x3, matrix products, over_tokens(): lax.dot_general(left, right, (((0,), (0,)), ((), ())), preferred_element_...  16.5 us
    all_gather x1, waiting for transfers between devices, per_device(): normed_full = lax.all_gather(normed, 'col', axis=0, tiled=True)  13.8 us
  transfers between devices with their start and end apart: 2, of which 2 were waited for; matrix products, arithmetic and copies ran while one was open for 6% of the time, Pallas kernels for 31%

profile of v6, /device:TPU:64, one launch (start us, length us, event | category | flops | bytes accessed | tf_op | source)
XLA Modules:
  0.0 448.1 jit_solution(5663511185473031285)
XLA Ops:
  7.2 0.9 convert_reduce_fusion
  8.1 1.1 fusion.12
  9.8 7.7 %shard_map.129 = f32[8,1,144]{2,1,0:T(1,128)} custom-call(f32[1,144]{1,0:T(1,128)} %bitcast.69), custom_call_target="tpu_custom_call" | custom-call | bytes 184320 | tf_op jit(solution)/shard_map/pallas_call | solution.py:106
  17.5 0.7 reduce_sum.83
  18.2 0.8 select_reduce_fusion.3
  19.0 2.6 fusion.2
  21.7 1.8 fusion.14
  23.5 80.7 %shard_map.130 = bf16[16,128,1024]{2,1,0:T(8,128)(2,1)} custom-call(bf16[128,1024]{1,0:T(8,128)(2,1)} %refs_0_.1), custom_call_target="tpu_custom_call" | custom-call | bytes 167772160 | tf_op jit(solution)/shard_map/pallas_call | solution.py:106
  104.3 11.5 %fusion.22 = (bf16[2048,896]{1,0:T(8,128)(2,1)}, f32[2048,896]{1,0:T(8,128)}) fusion(bf16[2048,1024]{1,0:T(8,128)(2,1)} %bitcast.51, bf16[896,1024]{1,0:T(8,128)(2,1)} %param.19), kind=kOutput, calls=%fused_computation.56 | convolution fusion | flops 3759931392 | bytes 17039360 | tf_op jit(solution)/shard_map/dot_general | solution.py:26
  115.7 28.4 %all-gather.3.cloned.1.call-done.refs_1_ = bf16[2048,896]{1,0:T(8,128)(2,1)} async-done(((bf16[256,896]{1,0:T(8,128)(2,1)}), bf16[2048,896]{1,0:T(8,128)(2,1)}) %all-gather.3.cloned.1.call-update) | async-done | bytes 3670032 | tf_op jit(solution)/shard_map/all_gather | solution.py:160
  144.2 56.1 %shard_map.131 = bf16[8,256,896]{2,1,0:T(8,128)(2,1)} custom-call(bf16[2048,896]{1,0:T(8,128)(2,1)} %get-tuple-element.22.refs_0_, bf16[2048,896]{1,0:T(8,128)(2,1)} %all-gather.3.cloned.1.call-done.refs_1_), custom_call_target="tpu_custom_call" | custom-call | bytes 146800640 | tf_op jit(solution)/shard_map/pallas_call | solution.py:106
  200.3 3.0 select_reduce_fusion
  203.4 1.8 fusion.11
  205.2 0.8 fusion.20
  206.5 0.8 fusion.21
  207.9 5.1 %convolution_convert_fusion = bf16[896,1024]{1,0:T(8,128)(2,1)} fusion(bf16[2048,896]{1,0:T(8,128)(2,1)S(1)} %copy-done.6, bf16[2048,1024]{1,0:T(8,128)(2,1)S(1)} %bitcast.52), kind=kOutput, calls=%fused_computation.7 | convolution fusion | flops 3759013888 | bytes 9699328 | tf_op jit(solution)/shard_map/dot_general | solution.py:20
  213.0 13.8 %all-gather.5.cloned.1.call-done.refs_2_ = bf16[2048,1024]{1,0:T(8,128)(2,1)} async-done(((bf16[128,1024]{1,0:T(8,128)(2,1)}), bf16[2048,1024]{1,0:T(8,128)(2,1)}) %all-gather.5.cloned.1.call-update) | async-done | bytes 4194320 | tf_op jit(solution)/shard_map/all_gather | solution.py:161
  226.8 55.0 %shard_map.132 = (bf16[8,128,896]{2,1,0:T(8,128)(2,1)}, bf16[8,128,896]{2,1,0:T(8,128)(2,1)}) custom-call(bf16[128,896]{1,0:T(8,128)(2,1)} %bitcast.68, bf16[128,896]{1,0:T(8,128)(2,1)} %bitcast.67, bf16[2048,1024]{1,0:T(8,128)(2,1)} %all-gather.5.cloned.1.call-done.refs_2_), custom_call_target="tpu_custom_call" | custom-call | bytes 146800640 | tf_op jit(solution)/shard_map/pallas_call | solution.py:106
  281.9 4.5 %fusion.25 = f32[1024,1024]{1,0:T(8,128)S(1)} fusion(bf16[1024,896]{1,0:T(8,128)(2,1)} %bitcast.55, bf16[1024,896]{1,0:T(8,128)(2,1)} %param.17), kind=kOutput, calls=%fused_computation.59 | convolution fusion | flops 1879048192 | bytes 7864320 | tf_op jit(solution)/shard_map/dot_general | solution.py:26
  286.5 5.0 %fusion.23 = (bf16[1024,1024]{1,0:T(8,128)(2,1)}, f32[1024,1024]{1,0:T(8,128)}) fusion(f32[1024,1024]{1,0:T(8,128)S(1)} %fusion.25, bf16[1024,896]{1,0:T(8,128)(2,1)S(1)} %bitcast.58, bf16[1024,896]{1,0:T(8,128)(2,1)S(1)} %copy-done), kind=kOutput, calls=%fused_computation.57 | convolution fusion | flops 1881145344 | bytes 14155776 | tf_op jit(solution)/shard_map/dot_general | solution.py:26
  291.5 69.6 %shard_map.133 = (bf16[16,64,1024]{2,1,0:T(8,128)(2,1)}, bf16[8,128,896]{2,1,0:T(8,128)(2,1)}, bf16[8,128,896]{2,1,0:T(8,128)(2,1)}) custom-call(bf16[1024,1024]{1,0:T(8,128)(2,1)} %get-tuple-element.24.refs_0_, bf16[128,896]{1,0:T(8,128)(2,1)} %bitcast.66, bf16[128,896]{1,0:T(8,128)(2,1)} %bitcast.65), custom_call_target="tpu_custom_call" | custom-call | bytes 230686720 | tf_op jit(solution)/shard_map/pallas_call | solution.py:106
  361.1 4.5 %fusion.26 = f32[1024,1024]{1,0:T(8,128)S(1)} fusion(bf16[1024,896]{1,0:T(8,128)(2,1)} %bitcast.59, bf16[1024,896]{1,0:T(8,128)(2,1)} %param.17), kind=kOutput, calls=%fused_computation.60 | convolution fusion | flops 1879048192 | bytes 7864320 | tf_op jit(solution)/shard_map/dot_general | solution.py:26
  365.7 5.0 %fusion.24 = (bf16[1024,1024]{1,0:T(8,128)(2,1)}, f32[1024,1024]{1,0:T(8,128)}) fusion(f32[1024,1024]{1,0:T(8,128)S(1)} %fusion.26, bf16[1024,896]{1,0:T(8,128)(2,1)S(1)} %bitcast.62, bf16[1024,896]{1,0:T(8,128)(2,1)S(1)} %copy-done), kind=kOutput, calls=%fused_computation.58 | convolution fusion | flops 1881145344 | bytes 14155776 | tf_op jit(solution)/shard_map/dot_general | solution.py:26
  370.7 39.9 %shard_map.134 = bf16[16,64,1024]{2,1,0:T(8,128)(2,1)} custom-call(bf16[1024,1024]{1,0:T(8,128)(2,1)} %get-tuple-element.26.refs_0_), custom_call_target="tpu_custom_call" | custom-call | bytes 83886080 | tf_op jit(solution)/shard_map/pallas_call | solution.py:106
  410.6 3.4 select_reduce_fusion.2
  414.0 1.1 dynamic-slice_add_fusion
  415.8 7.0 %shard_map.135 = f32[8,1,128]{2,1,0:T(1,128)} custom-call(f32[1,128]{1,0:T(1,128)} %bitcast.70), custom_call_target="tpu_custom_call" | custom-call | bytes 163840 | tf_op jit(solution)/shard_map/pallas_call | solution.py:106
  423.6 0.9 fusion.19
  424.5 2.6 pad_maximum_fusion.1
  428.0 1.8 copy-done.1
  429.9 5.7 %convolution_convert_fusion.1 = bf16[1024,896]{1,0:T(8,128)(2,1)} fusion(bf16[2048,1024]{1,0:T(8,128)(2,1)S(1)} %copy-done.1, bf16[2048,896]{1,0:T(8,128)(2,1)S(1)} %bitcast.53), kind=kOutput, calls=%fused_computation.8 | convolution fusion | flops 3759013888 | bytes 9699328 | tf_op jit(solution)/shard_map/dot_general | solution.py:20
  435.5 5.7 %convolution_convert_fusion.2 = bf16[1024,896]{1,0:T(8,128)(2,1)} fusion(bf16[2048,1024]{1,0:T(8,128)(2,1)S(1)} %copy-done.1, bf16[2048,896]{1,0:T(8,128)(2,1)S(1)} %bitcast.54), kind=kOutput, calls=%fused_computation.9 | convolution fusion | flops 3759013888 | bytes 9699328 | tf_op jit(solution)/shard_map/dot_general | solution.py:20
  (41 shorter events, 4.2 us)
Async XLA Ops:
  7.2 279.3 %copy-start = (bf16[1024,896]{1,0:T(8,128)(2,1)S(1)}, bf16[1024,896]{1,0:T(8,128)(2,1)}, u32[]{:S(2)}) copy-start(bf16[1024,896]{1,0:T(8,128)(2,1)} %param.18) | copy-start | bytes 5505028
  7.2 137.0 %all-gather.3.cloned.1.call-start = ((), (), s32[]{:S(2)}) async-start(), calls=%async_computation | async-start | bytes 4128768 | tf_op jit(solution)/shard_map/all_gather | solution.py:160
  21.6 205.2 %all-gather.5.cloned.1.call-start = ((), (), s32[]{:S(2)}) async-start(), calls=%async_computation.1 | async-start | bytes 4456448 | tf_op jit(solution)/shard_map/all_gather | solution.py:161
  200.3 3.1 copy-start.4
  200.3 3.1 copy-start.5
  203.4 2.7 copy-start.11
  203.4 3.8 copy-start.2
  203.4 4.5 %copy-start.6 = (bf16[2048,896]{1,0:T(8,128)(2,1)S(1)}, bf16[2048,896]{1,0:T(8,128)(2,1)}, u32[]{:S(2)}) copy-start(bf16[2048,896]{1,0:T(8,128)(2,1)} %all-gather.3.cloned.1.call-done.refs_1_) | copy-start | bytes 11010052
  281.9 4.6 %copy-start.8 = (bf16[8,128,896]{2,1,0:T(8,128)(2,1)S(1)}, bf16[8,128,896]{2,1,0:T(8,128)(2,1)}, u32[]{:S(2)}) copy-start(bf16[8,128,896]{2,1,0:T(8,128)(2,1)} %get-tuple-element.10) | copy-start | bytes 5505028
  361.1 4.6 %copy-start.10 = (bf16[8,128,896]{2,1,0:T(8,128)(2,1)S(1)}, bf16[8,128,896]{2,1,0:T(8,128)(2,1)}, u32[]{:S(2)}) copy-start(bf16[8,128,896]{2,1,0:T(8,128)(2,1)} %get-tuple-element.13) | copy-start | bytes 5505028
  410.5 4.6 %copy-start.3 = (bf16[128,1024]{1,0:T(8,128)(2,1)S(1)}, bf16[128,1024]{1,0:T(8,128)(2,1)}, u32[]{:S(2)}) copy-start(bf16[128,1024]{1,0:T(8,128)(2,1)} %param.10) | copy-start | bytes 786436
  410.6 4.6 %copy-start.13 = (f32[1024]{0:T(1024)S(1)}, f32[1024]{0:T(1024)}, u32[]{:S(2)}) copy-start(f32[1024]{0:T(1024)} %param.16) | copy-start | bytes 12292
  410.6 13.0 %copy-start.12 = (bf16[128,1024]{1,0:T(8,128)(2,1)S(1)}, bf16[128,1024]{1,0:T(8,128)(2,1)}, u32[]{:S(2)}) copy-start(bf16[128,1024]{1,0:T(8,128)(2,1)} %refs_0_.1) | copy-start | bytes 786436
  424.5 2.6 copy-start.7
  424.5 3.2 copy-start.9
  427.7 2.2 copy-start.1
Sparse Core Ops, SparseCore 0:
  21.7 122.3 all-gather.2
  147.1 79.6 all-gather.4

commit v7 on v6

--- a/solution.py
+++ b/solution.py
@@ -116,7 +116,7 @@
         compiler_params=pltpu.CompilerParams(collective_id=cid, has_side_effects=True),
         cost_estimate=pl.CostEstimate(
             flops=0, transcendentals=0,
-            bytes_accessed=sum(int(o.size) * o.dtype.itemsize for o in out_shapes) * 40,
+            bytes_accessed=sum(int(o.size) * o.dtype.itemsize for o in out_shapes),
         ),
     )(*[x for x, _, _ in items], *deps)
 
@@ -161,9 +161,7 @@
     normed_full = lax.all_gather(normed, "col", axis=0, tiled=True)
     (cot_full,) = exchange([(grad_out, "col", "gather")], 1)
     cot_full = cot_full.reshape(total, feat_loc)
-    (back,) = reduce_scatter(
-        over_width(cot_full, w_down), "row", 2, deps=(dropped_full,)
-    )
+    (back,) = reduce_scatter(over_width(cot_full, w_down), "row", 2)
     grad_act = back * weights[:, None] * keep_f
     grad_gpre = (grad_act * up_f * sig * (1.0 + gate_f * (1.0 - sig))).astype(jnp.bfloat16)
     grad_upre = (grad_act * gate_f * sig).astype(jnp.bfloat16)
@@ -181,9 +179,7 @@
 
     gpre_a, gpre_b = split(grad_gpre)
     upre_a, upre_b = split(grad_upre)
-    ga_full, ua_full = exchange(
-        [(gpre_a, "row", "gather"), (upre_a, "row", "gather")], 3, (normed_full,)
-    )
+    ga_full, ua_full = exchange([(gpre_a, "row", "gather"), (upre_a, "row", "gather")], 3)
     ga_full = ga_full.reshape(total // 2, ff_loc)
     ua_full = ua_full.reshape(total // 2, ff_loc)
     part_a = over_width(ga_full, w_gate) + over_width(ua_full, w_up)
@@ -193,7 +189,7 @@
     gb_full = gb_full.reshape(total // 2, ff_loc)
     ub_full = ub_full.reshape(total // 2, ff_loc)
     part_b = over_width(gb_full, w_gate) + over_width(ub_full, w_up)
-    (gn_b,) = reduce_scatter(part_b, "col", 6)
+    (gn_b,) = reduce_scatter(part_b, "col", 6, deps=(dropped_full, normed_full))
     grad_normed = jnp.concatenate([gn_a, gn_b], axis=0)
     gpre_full = joined(ga_full, gb_full)
     upre_full = joined(ua_full, ub_full)

time: 448 us -> 484 us (1.080)
  Pallas kernels: 316 us -> 356 us
  waiting for transfers between devices: 42.3 us -> 33.4 us
  matrix products: 47 us -> 52 us
    pallas_call x7, Pallas kernels: 316 us -> 356 us  [exchange(): pl.pallas_call(functools.partial(_exchange_kernel, modes, axes, len(deps)...]
    all_gather x1, waiting for transfers between devices: 28.4 us -> 0.01 us  [per_device(): dropped_full = lax.all_gather(dropped, 'row', axis=0, tiled=True)]
    all_gather x1, waiting for transfers between devices: 13.8 us -> 33.3 us  [per_device(): normed_full = lax.all_gather(normed, 'col', axis=0, tiled=True)]
    dot_general x3, matrix products: 16.5 us -> 23.5 us  [over_tokens(): lax.dot_general(left, right, (((0,), (0,)), ((), ())), preferred_element_...]
  transfers between devices with their start and end apart: 2 -> 2, of which waited for: 2 -> 1; matrix products, arithmetic and copies ran while one was open for 6% -> 7% of each run, Pallas kernels for 31% -> 35%
where the time goes in v7:
time: 484 us
  Pallas kernels  356 us (74%)
  matrix products  52 us (11%)
  waiting for transfers between devices  33.4 us (7%)
  other arithmetic  25.5 us (5%)
  between operations  14.3 us (3%)
    pallas_call x7, Pallas kernels, exchange(): pl.pallas_call(functools.partial(_exchange_kernel, modes, axes, len(deps)...  356 us
    all_gather x1, waiting for transfers between devices, per_device(): normed_full = lax.all_gather(normed, 'col', axis=0, tiled=True)  33.3 us
    dot_general x5, matrix products, over_width(): lax.dot_general(left, right, (((1,), (1,)), ((), ())), preferred_element_...  28.5 us
    dot_general x3, matrix products, over_tokens(): lax.dot_general(left, right, (((0,), (0,)), ((), ())), preferred_element_...  23.5 us
  transfers between devices with their start and end apart: 2, of which 1 were waited for; matrix products, arithmetic and copies ran while one was open for 7% of the time, Pallas kernels for 35%

profile of v7, /device:TPU:64, one launch (start us, length us, event | category | flops | bytes accessed | tf_op | source)
XLA Modules:
  0.0 483.5 jit_solution(11993225887709169311)
XLA Ops:
  7.2 0.9 convert_reduce_fusion
  8.2 1.1 fusion.12
  9.8 7.7 %shard_map.129 = f32[8,1,144]{2,1,0:T(1,128)} custom-call(f32[1,144]{1,0:T(1,128)} %bitcast.61), custom_call_target="tpu_custom_call" | custom-call | bytes 4608 | tf_op jit(solution)/shard_map/pallas_call | solution.py:106
  17.5 0.7 reduce_sum.83
  18.2 0.8 select_reduce_fusion.3
  19.0 74.7 %shard_map.130 = bf16[16,128,1024]{2,1,0:T(8,128)(2,1)} custom-call(bf16[128,1024]{1,0:T(8,128)(2,1)} %refs_0_.1), custom_call_target="tpu_custom_call" | custom-call | bytes 4194304 | tf_op jit(solution)/shard_map/pallas_call | solution.py:106
  93.7 11.5 %fusion.22 = (bf16[2048,896]{1,0:T(8,128)(2,1)}, f32[2048,896]{1,0:T(8,128)}) fusion(bf16[2048,1024]{1,0:T(8,128)(2,1)} %bitcast.43, bf16[896,1024]{1,0:T(8,128)(2,1)} %param.19), kind=kOutput, calls=%fused_computation.56 | convolution fusion | flops 3759931392 | bytes 17039360 | tf_op jit(solution)/shard_map/dot_general | solution.py:26
  105.1 55.9 %shard_map.131 = bf16[8,256,896]{2,1,0:T(8,128)(2,1)} custom-call(bf16[2048,896]{1,0:T(8,128)(2,1)} %get-tuple-element.23.refs_0_), custom_call_target="tpu_custom_call" | custom-call | bytes 3670016 | tf_op jit(solution)/shard_map/pallas_call | solution.py:106
  161.1 3.0 select_reduce_fusion
  164.2 2.6 fusion.11
  167.1 0.8 fusion.14
  167.9 0.8 fusion.20
  168.8 1.5 fusion.2
  170.3 0.8 fusion.21
  171.1 77.0 %shard_map.132 = (bf16[8,128,896]{2,1,0:T(8,128)(2,1)}, bf16[8,128,896]{2,1,0:T(8,128)(2,1)}) custom-call(bf16[128,896]{1,0:T(8,128)(2,1)} %bitcast.60, bf16[128,896]{1,0:T(8,128)(2,1)} %bitcast.59), custom_call_target="tpu_custom_call" | custom-call | bytes 3670016 | tf_op jit(solution)/shard_map/pallas_call | solution.py:106
  248.2 4.6 fusion.25
  252.8 5.1 %fusion.23 = (bf16[1024,1024]{1,0:T(8,128)(2,1)}, f32[1024,1024]{1,0:T(8,128)}) fusion(f32[1024,1024]{1,0:T(8,128)S(1)} %fusion.25, bf16[1024,896]{1,0:T(8,128)(2,1)S(1)} %bitcast.51, bf16[1024,896]{1,0:T(8,128)(2,1)S(1)} %copy-done), kind=kOutput, calls=%fused_computation.57 | convolution fusion | flops 1881145344 | bytes 14155776 | tf_op jit(solution)/shard_map/dot_general | solution.py:26
  257.8 93.5 %shard_map.133 = (bf16[16,64,1024]{2,1,0:T(8,128)(2,1)}, bf16[8,128,896]{2,1,0:T(8,128)(2,1)}, bf16[8,128,896]{2,1,0:T(8,128)(2,1)}) custom-call(bf16[1024,1024]{1,0:T(8,128)(2,1)} %get-tuple-element.25.refs_0_, bf16[128,896]{1,0:T(8,128)(2,1)} %bitcast.58, bf16[128,896]{1,0:T(8,128)(2,1)} %bitcast.57), custom_call_target="tpu_custom_call" | custom-call | bytes 5767168 | tf_op jit(solution)/shard_map/pallas_call | solution.py:106
  351.4 4.4 pad_maximum_fusion.1
  355.8 2.2 pad_maximum_fusion
  358.0 2.4 fusion.26
  360.3 5.1 %fusion.24 = (bf16[1024,1024]{1,0:T(8,128)(2,1)}, f32[1024,1024]{1,0:T(8,128)}) fusion(f32[1024,1024]{1,0:T(8,128)S(1)} %fusion.26, bf16[1024,896]{1,0:T(8,128)(2,1)S(1)} %bitcast.53, bf16[1024,896]{1,0:T(8,128)(2,1)S(1)} %copy-done), kind=kOutput, calls=%fused_computation.58 | convolution fusion | flops 1881145344 | bytes 14155776 | tf_op jit(solution)/shard_map/dot_general | solution.py:26
  365.4 8.5 %convolution_convert_fusion = bf16[896,1024]{1,0:T(8,128)(2,1)} fusion(bf16[2048,896]{1,0:T(8,128)(2,1)} %all-gather.3.cloned.1.call-done.refs_1_, bf16[2048,1024]{1,0:T(8,128)(2,1)} %bitcast.44), kind=kOutput, calls=%fused_computation.7 | convolution fusion | flops 3759013888 | bytes 9699328 | tf_op jit(solution)/shard_map/dot_general | solution.py:20
  374.0 33.3 %all-gather.5.cloned.1.call-done.refs_2_ = bf16[2048,1024]{1,0:T(8,128)(2,1)} async-done(((bf16[128,1024]{1,0:T(8,128)(2,1)}), bf16[2048,1024]{1,0:T(8,128)(2,1)}) %all-gather.5.cloned.1.call-update) | async-done | bytes 4194320 | tf_op jit(solution)/shard_map/all_gather | solution.py:161
  407.3 40.5 %shard_map.134 = bf16[16,64,1024]{2,1,0:T(8,128)(2,1)} custom-call(bf16[1024,1024]{1,0:T(8,128)(2,1)} %get-tuple-element.27.refs_0_, bf16[2048,896]{1,0:T(8,128)(2,1)} %all-gather.3.cloned.1.call-done.refs_1_, bf16[2048,1024]{1,0:T(8,128)(2,1)} %all-gather.5.cloned.1.call-done.refs_2_), custom_call_target="tpu_custom_call" | custom-call | bytes 2097152 | tf_op jit(solution)/shard_map/pallas_call | solution.py:106
  447.8 3.4 select_reduce_fusion.2
  451.2 1.1 dynamic-slice_add_fusion
  453.0 7.1 %shard_map.135 = f32[8,1,128]{2,1,0:T(1,128)} custom-call(f32[1,128]{1,0:T(1,128)} %bitcast.62), custom_call_target="tpu_custom_call" | custom-call | bytes 4096 | tf_op jit(solution)/shard_map/pallas_call | solution.py:106
  460.1 0.7 reduce_sum.89
  460.8 0.9 fusion.19
  461.7 9.3 %convolution_convert_fusion.1 = bf16[1024,896]{1,0:T(8,128)(2,1)} fusion(bf16[2048,1024]{1,0:T(8,128)(2,1)} %all-gather.5.cloned.1.call-done.refs_2_, bf16[2048,896]{1,0:T(8,128)(2,1)} %bitcast.46), kind=kOutput, calls=%fused_computation.8 | convolution fusion | flops 3759013888 | bytes 9699328 | tf_op jit(solution)/shard_map/dot_general | solution.py:20
  471.0 5.7 %convolution_convert_fusion.2 = bf16[1024,896]{1,0:T(8,128)(2,1)} fusion(bf16[2048,1024]{1,0:T(8,128)(2,1)S(1)} %copy-done.1, bf16[2048,896]{1,0:T(8,128)(2,1)S(1)} %bitcast.45), kind=kOutput, calls=%fused_computation.9 | convolution fusion | flops 3759013888 | bytes 9699328 | tf_op jit(solution)/shard_map/dot_general | solution.py:20
  (40 shorter events, 1.6 us)
Async XLA Ops:
  7.2 245.6 %copy-start = (bf16[1024,896]{1,0:T(8,128)(2,1)S(1)}, bf16[1024,896]{1,0:T(8,128)(2,1)}, u32[]{:S(2)}) copy-start(bf16[1024,896]{1,0:T(8,128)(2,1)} %param.18) | copy-start | bytes 5505028
  7.2 358.2 %all-gather.3.cloned.1.call-start = ((), (), s32[]{:S(2)}) async-start(), calls=%async_computation | async-start | bytes 4128768 | tf_op jit(solution)/shard_map/all_gather | solution.py:160
  161.1 3.1 copy-start.8
  161.1 3.1 copy-start.9
  161.1 3.1 copy-start.11
  164.2 2.9 copy-start.2
  164.2 2.9 copy-start.12
  166.8 240.4 %all-gather.5.cloned.1.call-start = ((), (), s32[]{:S(2)}) async-start(), calls=%async_computation.1 | async-start | bytes 4456448 | tf_op jit(solution)/shard_map/all_gather | solution.py:161
  248.1 4.6 copy-start.5
  351.3 4.4 copy-start.4
  351.4 4.4 copy-start.7
  355.7 2.2 copy-start.13
  358.0 2.4 copy-start.6
  447.8 13.0 %copy-start.10 = (bf16[128,1024]{1,0:T(8,128)(2,1)S(1)}, bf16[128,1024]{1,0:T(8,128)(2,1)}, u32[]{:S(2)}) copy-start(bf16[128,1024]{1,0:T(8,128)(2,1)} %refs_0_.1) | copy-start | bytes 786436
  461.7 9.3 %copy-start.1 = (bf16[2048,1024]{1,0:T(8,128)(2,1)S(1)}, bf16[2048,1024]{1,0:T(8,128)(2,1)}, u32[]{:S(2)}) copy-start(bf16[2048,1024]{1,0:T(8,128)(2,1)} %all-gather.5.cloned.1.call-done.refs_2_) | copy-start | bytes 12582916
  461.7 9.3 %copy-start.3 = (bf16[8,2,2,64,896]{4,3,2,1,0:T(8,128)(2,1)S(1)}, bf16[8,2,2,64,896]{4,3,2,1,0:T(8,128)(2,1)}, u32[]{:S(2)}) copy-start(bf16[8,2,2,64,896]{4,3,2,1,0:T(8,128)(2,1)} %pad_maximum_fusion) | copy-start | bytes 11010052
Sparse Core Ops, SparseCore 0:
  166.9 186.5 all-gather.2
  356.5 50.7 all-gather.4

commit v8 on v5

--- a/solution.py
+++ b/solution.py
@@ -52,10 +52,24 @@
     ins, outs = refs[:n], refs[n:2 * n]
     send_sem, recv_sem, local_sem = refs[2 * n:]
     _barrier(axes)
-    sends = []
+    sends, relays = [], []
     for i, (mode, axis) in enumerate(zip(modes, axes)):
         k = lax.axis_size(axis)
         me = lax.axis_index(axis)
+        if mode == "pgather":
+            p = me % 2
+            for d in range(1, k // 2):
+                tgt = (me + 2 * d) % k
+                c = pltpu.make_async_remote_copy(
+                    ins[i], outs[i].at[p, me // 2], send_sem.at[i, d], recv_sem.at[i, me],
+                    device_id=_dev(axis, tgt), device_id_type=pl.DeviceIdType.MESH,
+                )
+                c.start()
+                sends.append(c)
+            loc = pltpu.make_async_copy(ins[i], outs[i].at[p, me // 2], local_sem.at[i])
+            loc.start()
+            relays.append((i, loc))
+            continue
         m = outs[i].shape[1]
         for d in range(1, k):
             tgt = (me + d) % k
@@ -70,6 +84,25 @@
             loc = pltpu.make_async_copy(ins[i], outs[i].at[me], local_sem.at[i])
             loc.start()
             sends.append(loc)
+    for i, loc in relays:
+        axis = axes[i]
+        k = lax.axis_size(axis)
+        me = lax.axis_index(axis)
+        p = me % 2
+        partner = me + 1 - 2 * p
+        for d in range(1, k // 2):
+            srcdev = (me + k - 2 * d) % k
+            pltpu.make_async_remote_copy(
+                ins[i], outs[i].at[p, srcdev // 2], send_sem.at[i, d], recv_sem.at[i, srcdev],
+                device_id=_dev(axis, srcdev), device_id_type=pl.DeviceIdType.MESH,
+            ).wait_recv()
+        loc.wait()
+        c = pltpu.make_async_remote_copy(
+            outs[i].at[p], outs[i].at[p], send_sem.at[i, 0], recv_sem.at[i, me],
+            device_id=_dev(axis, partner), device_id_type=pl.DeviceIdType.MESH,
+        )
+        c.start()
+        sends.append(c)
     for c in sends:
         if c.is_remote:
             c.wait_send()
@@ -78,6 +111,14 @@
     for i, (mode, axis) in enumerate(zip(modes, axes)):
         k = lax.axis_size(axis)
         me = lax.axis_index(axis)
+        if mode == "pgather":
+            p = me % 2
+            partner = me + 1 - 2 * p
+            pltpu.make_async_remote_copy(
+                outs[i].at[1 - p], outs[i].at[1 - p], send_sem.at[i, 0], recv_sem.at[i, partner],
+                device_id=_dev(axis, partner), device_id_type=pl.DeviceIdType.MESH,
+            ).wait_recv()
+            continue
         m = outs[i].shape[1]
         for d in range(1, k):
             srcdev = (me + k - d) % k
@@ -98,6 +139,8 @@
         kmax = max(kmax, k)
         if mode == "gather":
             out_shapes.append(jax.ShapeDtypeStruct((k,) + x.shape, x.dtype))
+        elif mode == "pgather":
+            out_shapes.append(jax.ShapeDtypeStruct((2, k // 2) + x.shape, x.dtype))
         else:
             out_shapes.append(
                 jax.ShapeDtypeStruct((k, x.shape[0] // k) + x.shape[1:], x.dtype)
@@ -117,6 +160,10 @@
     )(*[x for x, _, _ in items])
 
 
+def pair_order(v):
+    return jnp.swapaxes(v, 0, 1).reshape((-1,) + v.shape[3:])
+
+
 def reduce_scatter(parts, axis, cid, extra=()):
     k = lax.axis_size(axis)
     me = lax.axis_index(axis)
@@ -153,13 +200,13 @@
     sig = jax.nn.sigmoid(gate_f)
     keep_f = keep_mask.astype(jnp.float32) * keep_scale
     dropped = (gate_f * sig * up_f * keep_f * weights[:, None]).astype(jnp.bfloat16)
-    cot_full, dropped_full = exchange([(grad_out, "col", "gather"), (dropped, "row", "gather")], 1)
-    cot_full = cot_full.reshape(total, feat_loc)
+    cot_full, dropped_full = exchange([(grad_out, "col", "pgather"), (dropped, "row", "gather")], 1)
+    cot_full = pair_order(cot_full)
     dropped_full = dropped_full.reshape(total, ff_loc)
     back, normed_full = reduce_scatter(
-        over_width(cot_full, w_down), "row", 2, [(normed, "col", "gather")]
-    )
-    normed_full = normed_full.reshape(total, feat_loc)
+        over_width(cot_full, w_down), "row", 2, [(normed, "col", "pgather")]
+    )
+    normed_full = pair_order(normed_full)
     grad_act = back * weights[:, None] * keep_f
     grad_gpre = (grad_act * up_f * sig * (1.0 + gate_f * (1.0 - sig))).astype(jnp.bfloat16)
     grad_upre = (grad_act * gate_f * sig).astype(jnp.bfloat16)

time: 440 us -> 407 us (0.925)
  Pallas kernels: 369 us -> 334 us
  local copies, waits for them, and re-layouts: 2.39 us -> 8.07 us
    pallas_call x7, Pallas kernels: 369 us -> 334 us  [exchange(): pl.pallas_call(functools.partial(_exchange_kernel, modes, axes), out_shap...]
    transpose x0 -> x2, local copies, waits for them, and re-layouts: none -> 5.2 us  [pair_order(): return jnp.swapaxes(v, 0, 1).reshape((-1,) + v.shape[3:])]
where the time goes in v8:
time: 407 us; the launch traced here: 406 us
  Pallas kernels  334 us (82%)
  matrix products  40.5 us (10%)
  other arithmetic  23.4 us (6%)
  local copies, waits for them, and re-layouts  8.07 us (2%)
    pallas_call x7, Pallas kernels, exchange(): pl.pallas_call(functools.partial(_exchange_kernel, modes, axes), out_shap...  334 us
    dot_general x5, matrix products, over_width(): lax.dot_general(left, right, (((1,), (1,)), ((), ())), preferred_element_...  24 us
    dot_general x3, matrix products, over_tokens(): lax.dot_general(left, right, (((0,), (0,)), ((), ())), preferred_element_...  16.5 us

profile of v8, /device:TPU:64, one launch (start us, length us, event | category | flops | bytes accessed | tf_op | source)
XLA Modules:
  0.0 406.5 jit_solution(17789191481914596298)
XLA Ops:
  0.7 0.9 convert_reduce_fusion
  1.6 1.1 fusion.12
  3.3 7.7 %shard_map.129 = f32[8,1,144]{2,1,0:T(1,128)} custom-call(f32[1,144]{1,0:T(1,128)} %bitcast.77), custom_call_target="tpu_custom_call" | custom-call | tf_op jit(solution)/shard_map/pallas_call | solution.py:149
  10.9 0.7 reduce_sum.83
  11.7 0.8 select_reduce_fusion.3
  12.4 1.8 fusion.14.refs_1_
  14.2 2.6 fusion.2.refs_1_
  16.8 72.6 %shard_map.130 = (bf16[2,8,128,1024]{3,2,1,0:T(8,128)(2,1)}, bf16[8,256,896]{2,1,0:T(8,128)(2,1)}) custom-call(bf16[128,1024]{1,0:T(8,128)(2,1)} %refs_0_.1, bf16[256,896]{1,0:T(8,128)(2,1)} %fusion.2.refs_1_), custom_call_target="tpu_custom_call" | custom-call | tf_op jit(solution)/shard_map/pallas_call | solution.py:149
  89.5 2.8 copy.28
  92.8 5.1 %convolution_convert_fusion = bf16[896,1024]{1,0:T(8,128)(2,1)} fusion(bf16[2048,896]{1,0:T(8,128)(2,1)S(1)} %bitcast.79, bf16[2048,1024]{1,0:T(8,128)(2,1)S(1)} %bitcast.58), kind=kOutput, calls=%fused_computation.7 | convolution fusion | flops 3759013888 | bytes 9699328 | tf_op jit(solution)/shard_map/dot_general | solution.py:20
  97.9 7.2 %fusion.22 = (bf16[2048,896]{1,0:T(8,128)(2,1)}, f32[2048,896]{1,0:T(8,128)}) fusion(bf16[2048,1024]{1,0:T(8,128)(2,1)S(1)} %bitcast.59, bf16[896,1024]{1,0:T(8,128)(2,1)S(1)} %copy-done.14), kind=kOutput, calls=%fused_computation.56 | convolution fusion | flops 3759931392 | bytes 17039360 | tf_op jit(solution)/shard_map/dot_general | solution.py:26
  105.1 72.8 %shard_map.131 = (bf16[8,256,896]{2,1,0:T(8,128)(2,1)}, bf16[2,8,128,1024]{3,2,1,0:T(8,128)(2,1)}) custom-call(bf16[2048,896]{1,0:T(8,128)(2,1)} %get-tuple-element.30.refs_0_, bf16[128,1024]{1,0:T(8,128)(2,1)} %fusion.14.refs_1_), custom_call_target="tpu_custom_call" | custom-call | tf_op jit(solution)/shard_map/pallas_call | solution.py:149
  177.9 3.1 select_reduce_fusion
  181.0 1.6 fusion.11
  182.6 2.4 copy.33
  185.1 0.8 fusion.20
  186.3 0.8 fusion.21
  187.1 59.3 %shard_map.132 = (bf16[8,128,896]{2,1,0:T(8,128)(2,1)}, bf16[8,128,896]{2,1,0:T(8,128)(2,1)}) custom-call(bf16[128,896]{1,0:T(8,128)(2,1)} %bitcast.76, bf16[128,896]{1,0:T(8,128)(2,1)} %bitcast.75), custom_call_target="tpu_custom_call" | custom-call | tf_op jit(solution)/shard_map/pallas_call | solution.py:149
  246.4 4.5 %fusion.25 = f32[1024,1024]{1,0:T(8,128)S(1)} fusion(bf16[1024,896]{1,0:T(8,128)(2,1)} %bitcast.63, bf16[1024,896]{1,0:T(8,128)(2,1)} %param.17), kind=kOutput, calls=%fused_computation.59 | convolution fusion | flops 1879048192 | bytes 7864320 | tf_op jit(solution)/shard_map/dot_general | solution.py:26
  250.9 4.9 %fusion.23 = (bf16[1024,1024]{1,0:T(8,128)(2,1)}, f32[1024,1024]{1,0:T(8,128)}) fusion(f32[1024,1024]{1,0:T(8,128)S(1)} %fusion.25, bf16[1024,896]{1,0:T(8,128)(2,1)S(1)} %bitcast.66, bf16[1024,896]{1,0:T(8,128)(2,1)S(1)} %copy-done), kind=kOutput, calls=%fused_computation.57 | convolution fusion | flops 1881145344 | bytes 14155776 | tf_op jit(solution)/shard_map/dot_general | solution.py:26
  255.8 77.0 %shard_map.133 = (bf16[16,64,1024]{2,1,0:T(8,128)(2,1)}, bf16[8,128,896]{2,1,0:T(8,128)(2,1)}, bf16[8,128,896]{2,1,0:T(8,128)(2,1)}) custom-call(bf16[1024,1024]{1,0:T(8,128)(2,1)} %get-tuple-element.32.refs_0_, bf16[128,896]{1,0:T(8,128)(2,1)} %bitcast.74, bf16[128,896]{1,0:T(8,128)(2,1)} %bitcast.73), custom_call_target="tpu_custom_call" | custom-call | tf_op jit(solution)/shard_map/pallas_call | solution.py:149
  332.9 2.6 pad_maximum_fusion.1
  335.4 0.7 copy-done.1
  336.1 5.7 %convolution_convert_fusion.1 = bf16[1024,896]{1,0:T(8,128)(2,1)} fusion(bf16[2048,1024]{1,0:T(8,128)(2,1)S(1)} %bitcast.55, bf16[2048,896]{1,0:T(8,128)(2,1)S(1)} %bitcast.62), kind=kOutput, calls=%fused_computation.8 | convolution fusion | flops 3759013888 | bytes 9699328 | tf_op jit(solution)/shard_map/dot_general | solution.py:20
  342.2 5.7 %convolution_convert_fusion.2 = bf16[1024,896]{1,0:T(8,128)(2,1)} fusion(bf16[2048,1024]{1,0:T(8,128)(2,1)S(1)} %bitcast.56, bf16[2048,896]{1,0:T(8,128)(2,1)S(1)} %bitcast.61), kind=kOutput, calls=%fused_computation.9 | convolution fusion | flops 3759013888 | bytes 9699328 | tf_op jit(solution)/shard_map/dot_general | solution.py:20
  347.9 2.4 fusion.26
  350.3 5.0 %fusion.24 = (bf16[1024,1024]{1,0:T(8,128)(2,1)}, f32[1024,1024]{1,0:T(8,128)}) fusion(f32[1024,1024]{1,0:T(8,128)S(1)} %fusion.26, bf16[1024,896]{1,0:T(8,128)(2,1)S(1)} %bitcast.68, bf16[1024,896]{1,0:T(8,128)(2,1)S(1)} %copy-done), kind=kOutput, calls=%fused_computation.58 | convolution fusion | flops 1881145344 | bytes 14155776 | tf_op jit(solution)/shard_map/dot_general | solution.py:26
  355.3 37.8 %shard_map.134 = bf16[16,64,1024]{2,1,0:T(8,128)(2,1)} custom-call(bf16[1024,1024]{1,0:T(8,128)(2,1)} %get-tuple-element.34.refs_0_), custom_call_target="tpu_custom_call" | custom-call | tf_op jit(solution)/shard_map/pallas_call | solution.py:149
  393.2 3.4 select_reduce_fusion.2
  396.6 1.1 dynamic-slice_add_fusion
  398.4 6.4 %shard_map.135 = f32[8,1,128]{2,1,0:T(1,128)} custom-call(f32[1,128]{1,0:T(1,128)} %bitcast.78), custom_call_target="tpu_custom_call" | custom-call | tf_op jit(solution)/shard_map/pallas_call | solution.py:149
  405.6 0.9 fusion.19
  (41 shorter events, 3.3 us)
Async XLA Ops:
  0.6 250.3 %copy-start = (bf16[1024,896]{1,0:T(8,128)(2,1)S(1)}, bf16[1024,896]{1,0:T(8,128)(2,1)}, u32[]{:S(2)}) copy-start(bf16[1024,896]{1,0:T(8,128)(2,1)} %param.18) | copy-start | bytes 5505028
  89.5 3.3 copy-start.13
  92.8 5.1 %copy-start.14 = (bf16[896,1024]{1,0:T(8,128)(2,1)S(1)}, bf16[896,1024]{1,0:T(8,128)(2,1)}, u32[]{:S(2)}) copy-start(bf16[896,1024]{1,0:T(8,128)(2,1)} %param.19) | copy-start | bytes 5505028
  105.1 75.9 %copy-start.4 = (bf16[256,896]{1,0:T(8,128)(2,1)S(1)}, bf16[256,896]{1,0:T(8,128)(2,1)}, u32[]{:S(2)}) copy-start(bf16[256,896]{1,0:T(8,128)(2,1)} %param.12) | copy-start | bytes 1376260
  105.1 75.9 %copy-start.5 = (s32[256,896]{1,0:T(8,128)S(1)}, s32[256,896]{1,0:T(8,128)}, u32[]{:S(2)}) copy-start(s32[256,896]{1,0:T(8,128)} %param.14) | copy-start | bytes 2752516
  177.9 4.7 %copy-start.2 = (bf16[2,8,128,1024]{3,2,1,0:T(8,128)(2,1)S(1)}, bf16[2,8,128,1024]{3,2,1,0:T(8,128)(2,1)}, u32[]{:S(2)}) copy-start(bf16[2,8,128,1024]{3,2,1,0:T(8,128)(2,1)} %get-tuple-element.20) | copy-start | bytes 12582916
  182.6 3.2 copy-start.10
  246.3 4.6 %copy-start.7 = (bf16[8,128,896]{2,1,0:T(8,128)(2,1)S(1)}, bf16[8,128,896]{2,1,0:T(8,128)(2,1)}, u32[]{:S(2)}) copy-start(bf16[8,128,896]{2,1,0:T(8,128)(2,1)} %get-tuple-element.16) | copy-start | bytes 5505028
  332.9 3.3 copy-start.1
  336.1 5.7 %copy-start.6 = (bf16[8,128,896]{2,1,0:T(8,128)(2,1)S(1)}, bf16[8,128,896]{2,1,0:T(8,128)(2,1)}, u32[]{:S(2)}) copy-start(bf16[8,128,896]{2,1,0:T(8,128)(2,1)} %get-tuple-element.15) | copy-start | bytes 5505028
  336.1 5.7 %copy-start.9 = (bf16[8,128,896]{2,1,0:T(8,128)(2,1)S(1)}, bf16[8,128,896]{2,1,0:T(8,128)(2,1)}, u32[]{:S(2)}) copy-start(bf16[8,128,896]{2,1,0:T(8,128)(2,1)} %get-tuple-element.18) | copy-start | bytes 5505028
  342.2 5.7 %copy-start.15 = (bf16[1024,896]{1,0:T(8,128)(2,1)S(1)}, bf16[1024,896]{1,0:T(8,128)(2,1)}, u32[]{:S(2)}) copy-start(bf16[1024,896]{1,0:T(8,128)(2,1)} %param.17) | copy-start | bytes 5505028
  347.9 2.4 copy-start.8
  393.2 4.6 %copy-start.3 = (bf16[128,1024]{1,0:T(8,128)(2,1)S(1)}, bf16[128,1024]{1,0:T(8,128)(2,1)}, u32[]{:S(2)}) copy-start(bf16[128,1024]{1,0:T(8,128)(2,1)} %param.10) | copy-start | bytes 786436
  393.2 4.6 %copy-start.12 = (f32[1024]{0:T(1024)S(1)}, f32[1024]{0:T(1024)}, u32[]{:S(2)}) copy-start(f32[1024]{0:T(1024)} %param.16) | copy-start | bytes 12292
  393.2 12.4 %copy-start.11 = (bf16[128,1024]{1,0:T(8,128)(2,1)S(1)}, bf16[128,1024]{1,0:T(8,128)(2,1)}, u32[]{:S(2)}) copy-start(bf16[128,1024]{1,0:T(8,128)(2,1)} %refs_0_.1) | copy-start | bytes 786436

commit v9 on v8

--- a/solution.py
+++ b/solution.py
@@ -32,18 +32,25 @@
     return tuple(idx if a == axis else lax.axis_index(a) for a in AXES)
 
 
-def _barrier(axes):
+def _barrier(modes, axes):
     barrier = pltpu.get_barrier_semaphore()
     count = 0
     for axis in sorted(set(axes)):
         k = lax.axis_size(axis)
         me = lax.axis_index(axis)
-        for d in range(1, k):
+        kinds = {mode for mode, a in zip(modes, axes) if a == axis}
+        if kinds <= {"pswap"}:
+            peers = [1 - 2 * (me % 2)]
+        elif kinds <= {"pswap", "pgather", "pscatter"}:
+            peers = [2 * d for d in range(1, k // 2)] + [1 - 2 * (me % 2)]
+        else:
+            peers = list(range(1, k))
+        for d in peers:
             pl.semaphore_signal(
                 barrier, inc=1, device_id=_dev(axis, (me + d) % k),
                 device_id_type=pl.DeviceIdType.MESH,
             )
-        count += k - 1
+        count += len(peers)
     pl.semaphore_wait(barrier, count)
 
 
@@ -51,11 +58,31 @@
     n = len(modes)
     ins, outs = refs[:n], refs[n:2 * n]
     send_sem, recv_sem, local_sem = refs[2 * n:]
-    _barrier(axes)
+    _barrier(modes, axes)
     sends, relays = [], []
     for i, (mode, axis) in enumerate(zip(modes, axes)):
         k = lax.axis_size(axis)
         me = lax.axis_index(axis)
+        if mode == "pswap":
+            c = pltpu.make_async_remote_copy(
+                ins[i], outs[i], send_sem.at[i, 0], recv_sem.at[i, me],
+                device_id=_dev(axis, me + 1 - 2 * (me % 2)),
+                device_id_type=pl.DeviceIdType.MESH,
+            )
+            c.start()
+            sends.append(c)
+            continue
+        if mode == "pscatter":
+            for d in range(1, k // 2):
+                tgt = (me + 2 * d) % k
+                c = pltpu.make_async_remote_copy(
+                    ins[i].at[tgt // 2], outs[i].at[me // 2], send_sem.at[i, d],
+                    recv_sem.at[i, me], device_id=_dev(axis, tgt),
+                    device_id_type=pl.DeviceIdType.MESH,
+                )
+                c.start()
+                sends.append(c)
+            continue
         if mode == "pgather":
             p = me % 2
             for d in range(1, k // 2):
@@ -111,6 +138,22 @@
     for i, (mode, axis) in enumerate(zip(modes, axes)):
         k = lax.axis_size(axis)
         me = lax.axis_index(axis)
+        if mode == "pswap":
+            partner = me + 1 - 2 * (me % 2)
+            pltpu.make_async_remote_copy(
+                ins[i], outs[i], send_sem.at[i, 0], recv_sem.at[i, partner],
+                device_id=_dev(axis, partner), device_id_type=pl.DeviceIdType.MESH,
+            ).wait_recv()
+            continue
+        if mode == "pscatter":
+            for d in range(1, k // 2):
+                srcdev = (me + k - 2 * d) % k
+                pltpu.make_async_remote_copy(
+                    ins[i].at[0], outs[i].at[srcdev // 2], send_sem.at[i, d],
+                    recv_sem.at[i, srcdev], device_id=_dev(axis, srcdev),
+                    device_id_type=pl.DeviceIdType.MESH,
+                ).wait_recv()
+            continue
         if mode == "pgather":
             p = me % 2
             partner = me + 1 - 2 * p
@@ -139,6 +182,8 @@
         kmax = max(kmax, k)
         if mode == "gather":
             out_shapes.append(jax.ShapeDtypeStruct((k,) + x.shape, x.dtype))
+        elif mode in ("pswap", "pscatter"):
+            out_shapes.append(jax.ShapeDtypeStruct(x.shape, x.dtype))
         elif mode == "pgather":
             out_shapes.append(jax.ShapeDtypeStruct((2, k // 2) + x.shape, x.dtype))
         else:
@@ -176,6 +221,24 @@
     return (mine + other,) + tuple(outs[1:])
 
 
+def pair_reduce_scatter(parts, axis, cid, extra=()):
+    k = lax.axis_size(axis)
+    me = lax.axis_index(axis)
+    p = me % 2
+    m = parts.shape[0] // k
+    quad = parts.reshape((k // 2, 2, m) + parts.shape[1:])
+    mine_half = jnp.where(p == 0, quad[:, 0], quad[:, 1])
+    theirs_half = jnp.where(p == 0, quad[:, 1], quad[:, 0])
+    (got,) = exchange([(theirs_half, axis, "pswap")], cid)
+    pair = mine_half + got
+    outs = exchange([(pair.astype(WIRE), axis, "pscatter")] + list(extra), cid + 1)
+    slots = outs[0]
+    own = lax.dynamic_index_in_dim(pair, me // 2, axis=0, keepdims=False)
+    keep = (jnp.arange(k // 2) != me // 2).reshape((k // 2,) + (1,) * (slots.ndim - 1))
+    other = jnp.sum(jnp.where(keep, slots.astype(jnp.float32), 0.0), axis=0)
+    return (own + other,) + tuple(outs[1:])
+
+
 def per_device(
     stream_in, grad_out, gate_pre, up_pre, keep_mask, segment_ids, norm_gain, w_gate, w_up, w_down
 ):
@@ -228,13 +291,13 @@
     ga_full = ga_full.reshape(total // 2, ff_loc)
     ua_full = ua_full.reshape(total // 2, ff_loc)
     part_a = over_width(ga_full, w_gate) + over_width(ua_full, w_up)
-    gn_a, gb_full, ub_full = reduce_scatter(
+    gn_a, gb_full, ub_full = pair_reduce_scatter(
         part_a, "col", 4, [(gpre_b, "row", "gather"), (upre_b, "row", "gather")]
     )
     gb_full = gb_full.reshape(total // 2, ff_loc)
     ub_full = ub_full.reshape(total // 2, ff_loc)
     part_b = over_width(gb_full, w_gate) + over_width(ub_full, w_up)
-    (gn_b,) = reduce_scatter(part_b, "col", 6)
+    (gn_b,) = pair_reduce_scatter(part_b, "col", 6)
     grad_normed = jnp.concatenate([gn_a, gn_b], axis=0)
     gpre_full = joined(ga_full, gb_full)
     upre_full = joined(ua_full, ub_full)
@@ -242,7 +305,7 @@
     grad_gate = over_tokens(normed_full, gpre_full).astype(jnp.bfloat16)
     grad_up = over_tokens(normed_full, upre_full).astype(jnp.bfloat16)
     scaled = grad_normed * norm_gain[None, :]
-    (inner_all,) = exchange([(jnp.sum(scaled * xs, axis=1)[None, :], "row", "gather")], 5)
+    (inner_all,) = exchange([(jnp.sum(scaled * xs, axis=1)[None, :], "row", "gather")], 8)
     inner = jnp.sum(inner_all, axis=(0, 1)) / D
     branch = recip[:, None] * (scaled - xs * (recip * recip * inner)[:, None])
     grad_in = (grad_out.astype(jnp.float32) + branch).astype(jnp.bfloat16)

time: 407 us -> 400 us (0.983)
  Pallas kernels: 334 us -> 314 us
  other arithmetic: 23.4 us -> 36.1 us
  matrix products: 40.5 us -> 35.3 us
  local copies, waits for them, and re-layouts: 8.07 us -> 12.7 us
    pallas_call x7 -> x9, Pallas kernels: 334 us -> 314 us  [exchange(): pl.pallas_call(functools.partial(_exchange_kernel, modes, axes), out_shap...]
    convert_element_type x0 -> x2, other arithmetic: none -> 11.1 us  [pair_reduce_scatter(): pair.astype(WIRE)]
    dot_general x5, matrix products: 24 us -> 18.8 us  [over_width(): lax.dot_general(left, right, (((1,), (1,)), ((), ())), preferred_element_...]
    unnamed x32 -> x42, local copies, waits for them, and re-layouts: 1.27 us -> 5.88 us
where the time goes in v9:
time: 400 us; the launch traced here: 399 us
  Pallas kernels  314 us (78%)
  other arithmetic  36.1 us (9%)
  matrix products  35.3 us (9%)
  local copies, waits for them, and re-layouts  12.7 us (3%)
    pallas_call x9, Pallas kernels, exchange(): pl.pallas_call(functools.partial(_exchange_kernel, modes, axes), out_shap...  314 us
    dot_general x5, matrix products, over_width(): lax.dot_general(left, right, (((1,), (1,)), ((), ())), preferred_element_...  18.8 us
    dot_general x3, matrix products, over_tokens(): lax.dot_general(left, right, (((0,), (0,)), ((), ())), preferred_element_...  16.5 us
    convert_element_type x2, other arithmetic, pair_reduce_scatter(): pair.astype(WIRE)  11.1 us

profile of v9, /device:TPU:64, one launch (start us, length us, event | category | flops | bytes accessed | tf_op | source)
XLA Modules:
  0.0 398.7 jit_solution(13124256070816975390)
XLA Ops:
  3.3 7.7 %shard_map.129 = f32[8,1,144]{2,1,0:T(1,128)} custom-call(f32[1,144]{1,0:T(1,128)} %bitcast.125), custom_call_target="tpu_custom_call" | custom-call | tf_op jit(solution)/shard_map/pallas_call | solution.py:194
  12.5 1.8 fusion.14.refs_1_
  14.2 2.6 fusion.2.refs_1_
  16.9 66.7 %shard_map.130 = (bf16[2,8,128,1024]{3,2,1,0:T(8,128)(2,1)}, bf16[8,256,896]{2,1,0:T(8,128)(2,1)}) custom-call(bf16[128,1024]{1,0:T(8,128)(2,1)} %refs_0_.1, bf16[256,896]{1,0:T(8,128)(2,1)} %fusion.2.refs_1_), custom_call_target="tpu_custom_call" | custom-call | tf_op jit(solution)/shard_map/pallas_call | solution.py:194
  83.6 2.8 copy.32
  86.9 5.1 %convolution_convert_fusion = bf16[896,1024]{1,0:T(8,128)(2,1)} fusion(bf16[2048,896]{1,0:T(8,128)(2,1)S(1)} %bitcast.127, bf16[2048,1024]{1,0:T(8,128)(2,1)S(1)} %bitcast.106), kind=kOutput, calls=%fused_computation.15 | convolution fusion | flops 3759013888 | bytes 9699328 | tf_op jit(solution)/shard_map/dot_general | solution.py:20
  92.0 7.1 %fusion.24 = (bf16[2048,896]{1,0:T(8,128)(2,1)}, f32[2048,896]{1,0:T(8,128)}) fusion(bf16[2048,1024]{1,0:T(8,128)(2,1)S(1)} %bitcast.107, bf16[896,1024]{1,0:T(8,128)(2,1)S(1)} %copy-done), kind=kOutput, calls=%fused_computation.66 | convolution fusion | flops 3759931392 | bytes 17039360 | tf_op jit(solution)/shard_map/dot_general | solution.py:26
  99.1 79.6 %shard_map.131 = (bf16[8,256,896]{2,1,0:T(8,128)(2,1)}, bf16[2,8,128,1024]{3,2,1,0:T(8,128)(2,1)}) custom-call(bf16[2048,896]{1,0:T(8,128)(2,1)} %get-tuple-element.34.refs_0_, bf16[128,1024]{1,0:T(8,128)(2,1)} %fusion.14.refs_1_), custom_call_target="tpu_custom_call" | custom-call | tf_op jit(solution)/shard_map/pallas_call | solution.py:194
  178.8 3.0 select_reduce_fusion
  181.8 1.8 fusion.11
  184.3 2.4 copy.41
  188.7 53.5 %shard_map.132 = (bf16[8,128,896]{2,1,0:T(8,128)(2,1)}, bf16[8,128,896]{2,1,0:T(8,128)(2,1)}) custom-call(bf16[128,896]{1,0:T(8,128)(2,1)} %bitcast.122, bf16[128,896]{1,0:T(8,128)(2,1)} %bitcast.121), custom_call_target="tpu_custom_call" | custom-call | tf_op jit(solution)/shard_map/pallas_call | solution.py:194
  242.3 4.6 %fusion.25 = f32[1024,1024]{1,0:T(8,128)S(1)} fusion(bf16[1024,896]{1,0:T(8,128)(2,1)} %bitcast.111, bf16[1024,896]{1,0:T(8,128)(2,1)} %param.17), kind=kOutput, calls=%fused_computation.67 | convolution fusion | flops 1879048192 | bytes 7864320 | tf_op jit(solution)/shard_map/dot_general | solution.py:26
  246.8 2.4 convolution_add_fusion.1
  249.2 2.0 copy-done.3
  251.2 1.8 select_bitcast_fusion.1.refs_0_
  252.9 4.8 %shard_map.133 = f32[8,64,1024]{2,1,0:T(8,128)} custom-call(f32[8,64,1024]{2,1,0:T(8,128)} %select_bitcast_fusion.1.refs_0_), custom_call_target="tpu_custom_call" | custom-call | tf_op jit(solution)/shard_map/pallas_call | solution.py:194
  257.7 5.5 %fusion.21 = (bf16[8,64,1024]{2,1,0:T(8,128)(2,1)}, f32[8,64,1024]{2,1,0:T(8,128)}) fusion(f32[8,64,1024]{2,1,0:T(8,128)} %shard_map.133, f32[8,2,64,1024]{3,2,1,0:T(8,128)} %bitcast.102, pred[]{:T(512)S(6)} %eq.25), kind=kLoop, calls=%fused_computation.63 | loop fusion | flops 1572864 | bytes 9437185 | tf_op jit(solution)/shard_map/convert_element_type | solution.py:234
  263.3 66.1 %shard_map.134 = (bf16[8,64,1024]{2,1,0:T(8,128)(2,1)}, bf16[8,128,896]{2,1,0:T(8,128)(2,1)}, bf16[8,128,896]{2,1,0:T(8,128)(2,1)}) custom-call(bf16[8,64,1024]{2,1,0:T(8,128)(2,1)} %get-tuple-element.26.refs_0_, bf16[128,896]{1,0:T(8,128)(2,1)} %bitcast.124, bf16[128,896]{1,0:T(8,128)(2,1)} %bitcast.123), custom_call_target="tpu_custom_call" | custom-call | tf_op jit(solution)/shard_map/pallas_call | solution.py:194
  329.4 2.0 pad_maximum_fusion.1
  332.1 5.7 %convolution_convert_fusion.1 = bf16[1024,896]{1,0:T(8,128)(2,1)} fusion(bf16[2048,1024]{1,0:T(8,128)(2,1)S(1)} %bitcast.103, bf16[2048,896]{1,0:T(8,128)(2,1)S(1)} %bitcast.110), kind=kOutput, calls=%fused_computation.16 | convolution fusion | flops 3759013888 | bytes 9699328 | tf_op jit(solution)/shard_map/dot_general | solution.py:20
  338.2 5.7 %convolution_convert_fusion.2 = bf16[1024,896]{1,0:T(8,128)(2,1)} fusion(bf16[2048,1024]{1,0:T(8,128)(2,1)S(1)} %bitcast.104, bf16[2048,896]{1,0:T(8,128)(2,1)S(1)} %bitcast.109), kind=kOutput, calls=%fused_computation.17 | convolution fusion | flops 3759013888 | bytes 9699328 | tf_op jit(solution)/shard_map/dot_general | solution.py:20
  343.9 2.4 fusion.26
  346.3 2.4 convolution_add_fusion
  348.7 1.9 copy-done.2
  350.6 1.7 select_bitcast_fusion.refs_0_
  352.3 4.8 %shard_map.135 = f32[8,64,1024]{2,1,0:T(8,128)} custom-call(f32[8,64,1024]{2,1,0:T(8,128)} %select_bitcast_fusion.refs_0_), custom_call_target="tpu_custom_call" | custom-call | tf_op jit(solution)/shard_map/pallas_call | solution.py:194
  357.1 5.6 %fusion.20 = (bf16[8,64,1024]{2,1,0:T(8,128)(2,1)}, f32[8,64,1024]{2,1,0:T(8,128)}) fusion(f32[8,64,1024]{2,1,0:T(8,128)} %shard_map.135, f32[8,2,64,1024]{3,2,1,0:T(8,128)} %bitcast.100, pred[]{:T(512)S(6)} %eq.25), kind=kLoop, calls=%fused_computation.62 | loop fusion | flops 1572864 | bytes 9437185 | tf_op jit(solution)/shard_map/convert_element_type | solution.py:234
  362.7 19.8 %shard_map.136 = bf16[8,64,1024]{2,1,0:T(8,128)(2,1)} custom-call(bf16[8,64,1024]{2,1,0:T(8,128)(2,1)} %get-tuple-element.24.refs_0_), custom_call_target="tpu_custom_call" | custom-call | tf_op jit(solution)/shard_map/pallas_call | solution.py:194
  382.6 2.0 select_reduce_fusion.2
  384.6 1.1 bitcast_add_fusion.2
  386.4 10.6 %shard_map.137 = f32[8,1,128]{2,1,0:T(1,128)} custom-call(f32[1,128]{1,0:T(1,128)} %bitcast.126), custom_call_target="tpu_custom_call" | custom-call | tf_op jit(solution)/shard_map/pallas_call | solution.py:194
  (57 shorter events, 10.8 us)
Async XLA Ops:
  0.6 91.3 %copy-start = (bf16[896,1024]{1,0:T(8,128)(2,1)S(1)}, bf16[896,1024]{1,0:T(8,128)(2,1)}, u32[]{:S(2)}) copy-start(bf16[896,1024]{1,0:T(8,128)(2,1)} %param.19) | copy-start | bytes 5505028
  83.6 3.3 copy-start.17
  178.8 3.0 copy-start.7
  178.8 3.0 copy-start.8
  181.8 2.5 copy-start.5
  184.3 3.2 copy-start.13
  242.2 4.6 %copy-start.10 = (bf16[8,128,896]{2,1,0:T(8,128)(2,1)S(1)}, bf16[8,128,896]{2,1,0:T(8,128)(2,1)}, u32[]{:S(2)}) copy-start(bf16[8,128,896]{2,1,0:T(8,128)(2,1)} %get-tuple-element.16) | copy-start | bytes 5505028
  242.2 4.6 %copy-start.19 = (bf16[1024,896]{1,0:T(8,128)(2,1)S(1)}, bf16[1024,896]{1,0:T(8,128)(2,1)}, u32[]{:S(2)}) copy-start(bf16[1024,896]{1,0:T(8,128)(2,1)} %param.18) | copy-start | bytes 5505028
  249.2 2.0 copy-start.3
  329.4 2.7 copy-start.4
  332.1 5.7 %copy-start.9 = (bf16[8,128,896]{2,1,0:T(8,128)(2,1)S(1)}, bf16[8,128,896]{2,1,0:T(8,128)(2,1)}, u32[]{:S(2)}) copy-start(bf16[8,128,896]{2,1,0:T(8,128)(2,1)} %get-tuple-element.15) | copy-start | bytes 5505028
  332.1 5.7 %copy-start.12 = (bf16[8,128,896]{2,1,0:T(8,128)(2,1)S(1)}, bf16[8,128,896]{2,1,0:T(8,128)(2,1)}, u32[]{:S(2)}) copy-start(bf16[8,128,896]{2,1,0:T(8,128)(2,1)} %get-tuple-element.18) | copy-start | bytes 5505028
  338.2 5.7 %copy-start.18 = (bf16[1024,896]{1,0:T(8,128)(2,1)S(1)}, bf16[1024,896]{1,0:T(8,128)(2,1)}, u32[]{:S(2)}) copy-start(bf16[1024,896]{1,0:T(8,128)(2,1)} %param.17) | copy-start | bytes 5505028
  343.9 2.4 copy-start.11
  343.9 2.4 copy-start.20
  348.7 1.9 copy-start.2
  362.7 19.9 %copy-start.14 = (bf16[8,64,1024]{2,1,0:T(8,128)(2,1)S(1)}, bf16[8,64,1024]{2,1,0:T(8,128)(2,1)}, u32[]{:S(2)}) copy-start(bf16[8,64,1024]{2,1,0:T(8,128)(2,1)} %get-tuple-element.17) | copy-start | bytes 3145732
  382.6 3.1 copy-start.6
  382.6 3.1 copy-start.16
  382.6 15.1 %copy-start.15 = (bf16[128,1024]{1,0:T(8,128)(2,1)S(1)}, bf16[128,1024]{1,0:T(8,128)(2,1)}, u32[]{:S(2)}) copy-start(bf16[128,1024]{1,0:T(8,128)(2,1)} %refs_0_.1) | copy-start | bytes 786436
  382.6 16.1 %copy-start.1 = (bf16[896,1024]{1,0:T(8,128)(2,1)S(1)}, bf16[896,1024]{1,0:T(8,128)(2,1)}, u32[]{:S(2)}) copy-start(bf16[896,1024]{1,0:T(8,128)(2,1)} %param.19) | copy-start | bytes 5505028

commit v10 on v9

--- a/solution.py
+++ b/solution.py
@@ -63,6 +63,38 @@
     for i, (mode, axis) in enumerate(zip(modes, axes)):
         k = lax.axis_size(axis)
         me = lax.axis_index(axis)
+        if mode == "rgather":
+            ym, zm = me // 2, me % 2
+            ny = k // 2
+            direct = [ym * 2 + 1 - zm] + [((ym + dy) % ny) * 2 + z for dy in (1, ny - 1) for z in (0, 1)]
+            for d, tgt in enumerate(direct):
+                c = pltpu.make_async_remote_copy(
+                    ins[i], outs[i].at[me], send_sem.at[i, d], recv_sem.at[i, me],
+                    device_id=_dev(axis, tgt), device_id_type=pl.DeviceIdType.MESH,
+                )
+                c.start()
+                sends.append(c)
+            loc = pltpu.make_async_copy(ins[i], outs[i].at[me], local_sem.at[i])
+            loc.start()
+            sends.append(loc)
+            m = outs[i].shape[1]
+            h = m // 2
+            for e, (dy, lo, off) in enumerate([(ny - 1, 0, 0), (1, h, k)]):
+                for z in (0, 1):
+                    src = ((ym + dy) % ny) * 2 + z
+                    pltpu.make_async_remote_copy(
+                        ins[i], outs[i].at[src], send_sem.at[i, 0], recv_sem.at[i, src],
+                        device_id=_dev(axis, src), device_id_type=pl.DeviceIdType.MESH,
+                    ).wait_recv()
+                    fwd = ((ym + ny - dy) % ny) * 2 + zm
+                    c = pltpu.make_async_remote_copy(
+                        outs[i].at[src, pl.ds(lo, h)], outs[i].at[src, pl.ds(lo, h)],
+                        send_sem.at[i, k + 2 * e + z], recv_sem.at[i, off + src],
+                        device_id=_dev(axis, fwd), device_id_type=pl.DeviceIdType.MESH,
+                    )
+                    c.start()
+                    sends.append(c)
+            continue
         if mode == "pswap":
             c = pltpu.make_async_remote_copy(
                 ins[i], outs[i], send_sem.at[i, 0], recv_sem.at[i, me],
@@ -138,6 +170,25 @@
     for i, (mode, axis) in enumerate(zip(modes, axes)):
         k = lax.axis_size(axis)
         me = lax.axis_index(axis)
+        if mode == "rgather":
+            ym, zm = me // 2, me % 2
+            ny = k // 2
+            m = outs[i].shape[1]
+            h = m // 2
+            partner = ym * 2 + 1 - zm
+            pltpu.make_async_remote_copy(
+                ins[i], outs[i].at[partner], send_sem.at[i, 0], recv_sem.at[i, partner],
+                device_id=_dev(axis, partner), device_id_type=pl.DeviceIdType.MESH,
+            ).wait_recv()
+            for z in (0, 1):
+                far = ((ym + 2) % ny) * 2 + z
+                for lo, off in ((0, 0), (h, k)):
+                    pltpu.make_async_remote_copy(
+                        outs[i].at[far, pl.ds(lo, h)], outs[i].at[far, pl.ds(lo, h)],
+                        send_sem.at[i, 0], recv_sem.at[i, off + far],
+                        device_id=_dev(axis, far), device_id_type=pl.DeviceIdType.MESH,
+                    ).wait_recv()
+            continue
         if mode == "pswap":
             partner = me + 1 - 2 * (me % 2)
             pltpu.make_async_remote_copy(
@@ -180,7 +231,7 @@
     for x, axis, mode in items:
         k = lax.axis_size(axis)
         kmax = max(kmax, k)
-        if mode == "gather":
+        if mode in ("gather", "rgather"):
             out_shapes.append(jax.ShapeDtypeStruct((k,) + x.shape, x.dtype))
         elif mode in ("pswap", "pscatter"):
             out_shapes.append(jax.ShapeDtypeStruct(x.shape, x.dtype))
@@ -197,8 +248,8 @@
         in_specs=[pl.BlockSpec(memory_space=pl.ANY)] * n,
         out_specs=tuple(pl.BlockSpec(memory_space=pl.ANY) for _ in range(n)),
         scratch_shapes=[
-            pltpu.SemaphoreType.DMA((n, kmax)),
-            pltpu.SemaphoreType.DMA((n, kmax)),
+            pltpu.SemaphoreType.DMA((n, 2 * kmax)),
+            pltpu.SemaphoreType.DMA((n, 2 * kmax)),
             pltpu.SemaphoreType.DMA((n,)),
         ],
         compiler_params=pltpu.CompilerParams(collective_id=cid, has_side_effects=True),
@@ -244,6 +295,7 @@
 ):
     n_row = lax.axis_size("row")
     n_col = lax.axis_size("col")
+    RG = "rgather" if n_row == 8 else "gather"
     tok_col, feat_loc = stream_in.shape
     tok_row, ff_loc = gate_pre.shape
     total = tok_col * n_col
@@ -263,7 +315,7 @@
     sig = jax.nn.sigmoid(gate_f)
     keep_f = keep_mask.astype(jnp.float32) * keep_scale
     dropped = (gate_f * sig * up_f * keep_f * weights[:, None]).astype(jnp.bfloat16)
-    cot_full, dropped_full = exchange([(grad_out, "col", "pgather"), (dropped, "row", "gather")], 1)
+    cot_full, dropped_full = exchange([(grad_out, "col", "pgather"), (dropped, "row", RG)], 1)
     cot_full = pair_order(cot_full)
     dropped_full = dropped_full.reshape(total, ff_loc)
     back, normed_full = reduce_scatter(
@@ -287,12 +339,12 @@
 
     gpre_a, gpre_b = split(grad_gpre)
     upre_a, upre_b = split(grad_upre)
-    ga_full, ua_full = exchange([(gpre_a, "row", "gather"), (upre_a, "row", "gather")], 3)
+    ga_full, ua_full = exchange([(gpre_a, "row", RG), (upre_a, "row", RG)], 3)
     ga_full = ga_full.reshape(total // 2, ff_loc)
     ua_full = ua_full.reshape(total // 2, ff_loc)
     part_a = over_width(ga_full, w_gate) + over_width(ua_full, w_up)
     gn_a, gb_full, ub_full = pair_reduce_scatter(
-        part_a, "col", 4, [(gpre_b, "row", "gather"), (upre_b, "row", "gather")]
+        part_a, "col", 4, [(gpre_b, "row", RG), (upre_b, "row", RG)]
     )
     gb_full = gb_full.reshape(total // 2, ff_loc)
     ub_full = ub_full.reshape(total // 2, ff_loc)

time: 400 us -> 362 us (0.905)
  Pallas kernels: 314 us -> 277 us
    pallas_call x9, Pallas kernels: 314 us -> 277 us  [exchange(): pl.pallas_call(functools.partial(_exchange_kernel, modes, axes), out_shap...]
where the time goes in v10:
time: 362 us
  Pallas kernels  277 us (77%)
  other arithmetic  36.1 us (10%)
  matrix products  35.5 us (10%)
  local copies, waits for them, and re-layouts  12.7 us (4%)
    pallas_call x9, Pallas kernels, exchange(): pl.pallas_call(functools.partial(_exchange_kernel, modes, axes), out_shap...  277 us
    dot_general x5, matrix products, over_width(): lax.dot_general(left, right, (((1,), (1,)), ((), ())), preferred_element_...  18.8 us
    dot_general x3, matrix products, over_tokens(): lax.dot_general(left, right, (((0,), (0,)), ((), ())), preferred_element_...  16.7 us
    convert_element_type x2, other arithmetic, pair_reduce_scatter(): pair.astype(WIRE)  11.1 us

profile of v10, /device:TPU:64, one launch (start us, length us, event | category | flops | bytes accessed | tf_op | source)
XLA Modules:
  0.0 361.8 jit_solution(13838082307490476212)
XLA Ops:
  3.3 7.8 %shard_map.129 = f32[8,1,144]{2,1,0:T(1,128)} custom-call(f32[1,144]{1,0:T(1,128)} %bitcast.125), custom_call_target="tpu_custom_call" | custom-call | tf_op jit(solution)/shard_map/pallas_call | solution.py:245
  12.6 1.8 fusion.14.refs_1_
  14.4 2.6 fusion.2.refs_1_
  17.0 57.4 %shard_map.130 = (bf16[2,8,128,1024]{3,2,1,0:T(8,128)(2,1)}, bf16[8,256,896]{2,1,0:T(8,128)(2,1)}) custom-call(bf16[128,1024]{1,0:T(8,128)(2,1)} %refs_0_.1, bf16[256,896]{1,0:T(8,128)(2,1)} %fusion.2.refs_1_), custom_call_target="tpu_custom_call" | custom-call | tf_op jit(solution)/shard_map/pallas_call | solution.py:245
  74.5 2.8 copy.32
  77.7 5.1 %convolution_convert_fusion = bf16[896,1024]{1,0:T(8,128)(2,1)} fusion(bf16[2048,896]{1,0:T(8,128)(2,1)S(1)} %bitcast.127, bf16[2048,1024]{1,0:T(8,128)(2,1)S(1)} %bitcast.106), kind=kOutput, calls=%fused_computation.15 | convolution fusion | flops 3759013888 | bytes 9699328 | tf_op jit(solution)/shard_map/dot_general | solution.py:20
  82.9 7.1 %fusion.24 = (bf16[2048,896]{1,0:T(8,128)(2,1)}, f32[2048,896]{1,0:T(8,128)}) fusion(bf16[2048,1024]{1,0:T(8,128)(2,1)S(1)} %bitcast.107, bf16[896,1024]{1,0:T(8,128)(2,1)S(1)} %copy-done), kind=kOutput, calls=%fused_computation.66 | convolution fusion | flops 3759931392 | bytes 17039360 | tf_op jit(solution)/shard_map/dot_general | solution.py:26
  90.0 69.9 %shard_map.131 = (bf16[8,256,896]{2,1,0:T(8,128)(2,1)}, bf16[2,8,128,1024]{3,2,1,0:T(8,128)(2,1)}) custom-call(bf16[2048,896]{1,0:T(8,128)(2,1)} %get-tuple-element.34.refs_0_, bf16[128,1024]{1,0:T(8,128)(2,1)} %fusion.14.refs_1_), custom_call_target="tpu_custom_call" | custom-call | tf_op jit(solution)/shard_map/pallas_call | solution.py:245
  159.9 3.0 select_reduce_fusion
  163.0 1.8 fusion.11
  165.4 2.4 copy.41
  169.8 48.5 %shard_map.132 = (bf16[8,128,896]{2,1,0:T(8,128)(2,1)}, bf16[8,128,896]{2,1,0:T(8,128)(2,1)}) custom-call(bf16[128,896]{1,0:T(8,128)(2,1)} %bitcast.122, bf16[128,896]{1,0:T(8,128)(2,1)} %bitcast.121), custom_call_target="tpu_custom_call" | custom-call | tf_op jit(solution)/shard_map/pallas_call | solution.py:245
  218.3 4.6 %fusion.25 = f32[1024,1024]{1,0:T(8,128)S(1)} fusion(bf16[1024,896]{1,0:T(8,128)(2,1)} %bitcast.111, bf16[1024,896]{1,0:T(8,128)(2,1)} %param.17), kind=kOutput, calls=%fused_computation.67 | convolution fusion | flops 1879048192 | bytes 7864320 | tf_op jit(solution)/shard_map/dot_general | solution.py:26
  222.9 2.4 convolution_add_fusion.1
  225.3 2.0 copy-done.3
  227.3 1.8 select_bitcast_fusion.1.refs_0_
  229.0 5.1 %shard_map.133 = f32[8,64,1024]{2,1,0:T(8,128)} custom-call(f32[8,64,1024]{2,1,0:T(8,128)} %select_bitcast_fusion.1.refs_0_), custom_call_target="tpu_custom_call" | custom-call | tf_op jit(solution)/shard_map/pallas_call | solution.py:245
  234.1 5.5 %fusion.21 = (bf16[8,64,1024]{2,1,0:T(8,128)(2,1)}, f32[8,64,1024]{2,1,0:T(8,128)}) fusion(f32[8,64,1024]{2,1,0:T(8,128)} %shard_map.133, f32[8,2,64,1024]{3,2,1,0:T(8,128)} %bitcast.102, pred[]{:T(512)S(6)} %eq.25), kind=kLoop, calls=%fused_computation.63 | loop fusion | flops 1572864 | bytes 9437185 | tf_op jit(solution)/shard_map/convert_element_type | solution.py:285
  239.6 52.5 %shard_map.134 = (bf16[8,64,1024]{2,1,0:T(8,128)(2,1)}, bf16[8,128,896]{2,1,0:T(8,128)(2,1)}, bf16[8,128,896]{2,1,0:T(8,128)(2,1)}) custom-call(bf16[8,64,1024]{2,1,0:T(8,128)(2,1)} %get-tuple-element.26.refs_0_, bf16[128,896]{1,0:T(8,128)(2,1)} %bitcast.124, bf16[128,896]{1,0:T(8,128)(2,1)} %bitcast.123), custom_call_target="tpu_custom_call" | custom-call | tf_op jit(solution)/shard_map/pallas_call | solution.py:245
  292.2 2.0 pad_maximum_fusion.1
  294.9 5.7 %convolution_convert_fusion.1 = bf16[1024,896]{1,0:T(8,128)(2,1)} fusion(bf16[2048,1024]{1,0:T(8,128)(2,1)S(1)} %bitcast.103, bf16[2048,896]{1,0:T(8,128)(2,1)S(1)} %bitcast.110), kind=kOutput, calls=%fused_computation.16 | convolution fusion | flops 3759013888 | bytes 9699328 | tf_op jit(solution)/shard_map/dot_general | solution.py:20
  301.0 5.9 %convolution_convert_fusion.2 = bf16[1024,896]{1,0:T(8,128)(2,1)} fusion(bf16[2048,1024]{1,0:T(8,128)(2,1)S(1)} %bitcast.104, bf16[2048,896]{1,0:T(8,128)(2,1)S(1)} %bitcast.109), kind=kOutput, calls=%fused_computation.17 | convolution fusion | flops 3759013888 | bytes 9699328 | tf_op jit(solution)/shard_map/dot_general | solution.py:20
  306.9 2.4 fusion.26
  309.3 2.4 convolution_add_fusion
  311.7 1.9 copy-done.2
  313.6 1.7 select_bitcast_fusion.refs_0_
  315.4 5.1 %shard_map.135 = f32[8,64,1024]{2,1,0:T(8,128)} custom-call(f32[8,64,1024]{2,1,0:T(8,128)} %select_bitcast_fusion.refs_0_), custom_call_target="tpu_custom_call" | custom-call | tf_op jit(solution)/shard_map/pallas_call | solution.py:245
  320.4 5.6 %fusion.20 = (bf16[8,64,1024]{2,1,0:T(8,128)(2,1)}, f32[8,64,1024]{2,1,0:T(8,128)}) fusion(f32[8,64,1024]{2,1,0:T(8,128)} %shard_map.135, f32[8,2,64,1024]{3,2,1,0:T(8,128)} %bitcast.100, pred[]{:T(512)S(6)} %eq.25), kind=kLoop, calls=%fused_computation.62 | loop fusion | flops 1572864 | bytes 9437185 | tf_op jit(solution)/shard_map/convert_element_type | solution.py:285
  326.0 20.5 %shard_map.136 = bf16[8,64,1024]{2,1,0:T(8,128)(2,1)} custom-call(bf16[8,64,1024]{2,1,0:T(8,128)(2,1)} %get-tuple-element.24.refs_0_), custom_call_target="tpu_custom_call" | custom-call | tf_op jit(solution)/shard_map/pallas_call | solution.py:245
  346.5 2.0 select_reduce_fusion.2
  348.5 1.1 bitcast_add_fusion.2
  350.3 9.9 %shard_map.137 = f32[8,1,128]{2,1,0:T(1,128)} custom-call(f32[1,128]{1,0:T(1,128)} %bitcast.126), custom_call_target="tpu_custom_call" | custom-call | tf_op jit(solution)/shard_map/pallas_call | solution.py:245
  (57 shorter events, 10.8 us)
Async XLA Ops:
  0.6 82.2 %copy-start = (bf16[896,1024]{1,0:T(8,128)(2,1)S(1)}, bf16[896,1024]{1,0:T(8,128)(2,1)}, u32[]{:S(2)}) copy-start(bf16[896,1024]{1,0:T(8,128)(2,1)} %param.19) | copy-start | bytes 5505028
  74.4 3.3 copy-start.17
  159.9 3.0 copy-start.7
  159.9 3.0 copy-start.8
  163.0 2.5 copy-start.5
  165.4 3.2 copy-start.13
  218.3 4.6 %copy-start.10 = (bf16[8,128,896]{2,1,0:T(8,128)(2,1)S(1)}, bf16[8,128,896]{2,1,0:T(8,128)(2,1)}, u32[]{:S(2)}) copy-start(bf16[8,128,896]{2,1,0:T(8,128)(2,1)} %get-tuple-element.16) | copy-start | bytes 5505028
  218.3 4.6 %copy-start.19 = (bf16[1024,896]{1,0:T(8,128)(2,1)S(1)}, bf16[1024,896]{1,0:T(8,128)(2,1)}, u32[]{:S(2)}) copy-start(bf16[1024,896]{1,0:T(8,128)(2,1)} %param.18) | copy-start | bytes 5505028
  225.3 2.0 copy-start.3
  292.2 2.7 copy-start.4
  294.9 5.7 %copy-start.9 = (bf16[8,128,896]{2,1,0:T(8,128)(2,1)S(1)}, bf16[8,128,896]{2,1,0:T(8,128)(2,1)}, u32[]{:S(2)}) copy-start(bf16[8,128,896]{2,1,0:T(8,128)(2,1)} %get-tuple-element.15) | copy-start | bytes 5505028
  294.9 5.7 %copy-start.12 = (bf16[8,128,896]{2,1,0:T(8,128)(2,1)S(1)}, bf16[8,128,896]{2,1,0:T(8,128)(2,1)}, u32[]{:S(2)}) copy-start(bf16[8,128,896]{2,1,0:T(8,128)(2,1)} %get-tuple-element.18) | copy-start | bytes 5505028
  301.0 5.9 %copy-start.18 = (bf16[1024,896]{1,0:T(8,128)(2,1)S(1)}, bf16[1024,896]{1,0:T(8,128)(2,1)}, u32[]{:S(2)}) copy-start(bf16[1024,896]{1,0:T(8,128)(2,1)} %param.17) | copy-start | bytes 5505028
  306.9 2.4 copy-start.11
  306.9 2.4 copy-start.20
  311.7 1.9 copy-start.2
  326.0 20.5 %copy-start.14 = (bf16[8,64,1024]{2,1,0:T(8,128)(2,1)S(1)}, bf16[8,64,1024]{2,1,0:T(8,128)(2,1)}, u32[]{:S(2)}) copy-start(bf16[8,64,1024]{2,1,0:T(8,128)(2,1)} %get-tuple-element.17) | copy-start | bytes 3145732
  346.5 3.1 copy-start.6
  346.5 3.1 copy-start.16
  346.5 14.4 %copy-start.15 = (bf16[128,1024]{1,0:T(8,128)(2,1)S(1)}, bf16[128,1024]{1,0:T(8,128)(2,1)}, u32[]{:S(2)}) copy-start(bf16[128,1024]{1,0:T(8,128)(2,1)} %refs_0_.1) | copy-start | bytes 786436
  346.5 15.3 %copy-start.1 = (bf16[896,1024]{1,0:T(8,128)(2,1)S(1)}, bf16[896,1024]{1,0:T(8,128)(2,1)}, u32[]{:S(2)}) copy-start(bf16[896,1024]{1,0:T(8,128)(2,1)} %param.19) | copy-start | bytes 5505028

commit v11 on v9

--- a/solution.py
+++ b/solution.py
@@ -41,7 +41,7 @@
         kinds = {mode for mode, a in zip(modes, axes) if a == axis}
         if kinds <= {"pswap"}:
             peers = [1 - 2 * (me % 2)]
-        elif kinds <= {"pswap", "pgather", "pscatter"}:
+        elif kinds <= {"pswap", "pgather", "pscatter", "prgather"}:
             peers = [2 * d for d in range(1, k // 2)] + [1 - 2 * (me % 2)]
         else:
             peers = list(range(1, k))
@@ -52,6 +52,54 @@
             )
         count += len(peers)
     pl.semaphore_wait(barrier, count)
+
+
+def _ring_pair_send(i, src_ref, slot, dev, me_g, ng, send_sem, recv_sem, sends, axis):
+    ny = ng // 2
+    ym, zm = me_g // 2, me_g % 2
+    direct = [ym * 2 + 1 - zm] + [((ym + dy) % ny) * 2 + z for dy in (1, ny - 1) for z in (0, 1)]
+    for d, tgt in enumerate(direct):
+        c = pltpu.make_async_remote_copy(
+            src_ref, slot(me_g), send_sem.at[i, d], recv_sem.at[i, me_g],
+            device_id=_dev(axis, dev(tgt)), device_id_type=pl.DeviceIdType.MESH,
+        )
+        c.start()
+        sends.append(c)
+    h = src_ref.shape[0] // 2
+    for e, (dy, lo, off) in enumerate([(ny - 1, 0, 0), (1, h, ng)]):
+        for z in (0, 1):
+            src = ((ym + dy) % ny) * 2 + z
+            pltpu.make_async_remote_copy(
+                src_ref, slot(src), send_sem.at[i, 0], recv_sem.at[i, src],
+                device_id=_dev(axis, dev(src)), device_id_type=pl.DeviceIdType.MESH,
+            ).wait_recv()
+            fwd = ((ym + ny - dy) % ny) * 2 + zm
+            c = pltpu.make_async_remote_copy(
+                slot(src).at[pl.ds(lo, h)], slot(src).at[pl.ds(lo, h)],
+                send_sem.at[i, ng + 2 * e + z], recv_sem.at[i, off + src],
+                device_id=_dev(axis, dev(fwd)), device_id_type=pl.DeviceIdType.MESH,
+            )
+            c.start()
+            sends.append(c)
+
+
+def _ring_pair_wait(i, src_ref, slot, dev, me_g, ng, send_sem, recv_sem, axis):
+    ny = ng // 2
+    ym, zm = me_g // 2, me_g % 2
+    h = src_ref.shape[0] // 2
+    peer = ym * 2 + 1 - zm
+    pltpu.make_async_remote_copy(
+        src_ref, slot(peer), send_sem.at[i, 0], recv_sem.at[i, peer],
+        device_id=_dev(axis, dev(peer)), device_id_type=pl.DeviceIdType.MESH,
+    ).wait_recv()
+    for z in (0, 1):
+        far = ((ym + 2) % ny) * 2 + z
+        for lo, off in ((0, 0), (h, ng)):
+            pltpu.make_async_remote_copy(
+                slot(far).at[pl.ds(lo, h)], slot(far).at[pl.ds(lo, h)],
+                send_sem.at[i, 0], recv_sem.at[i, off + far],
+                device_id=_dev(axis, dev(far)), device_id_type=pl.DeviceIdType.MESH,
+            ).wait_recv()
 
 
 def _exchange_kernel(modes, axes, *refs):
@@ -63,6 +111,30 @@
     for i, (mode, axis) in enumerate(zip(modes, axes)):
         k = lax.axis_size(axis)
         me = lax.axis_index(axis)
+        if mode == "rgather":
+            loc = pltpu.make_async_copy(ins[i], outs[i].at[me], local_sem.at[i])
+            loc.start()
+            sends.append(loc)
+            _ring_pair_send(i, ins[i], lambda g: outs[i].at[g], lambda g: g, me, k,
+                            send_sem, recv_sem, sends, axis)
+            continue
+        if mode == "prgather":
+            p = me % 2
+            partner = me + 1 - 2 * p
+            slot = lambda g: outs[i].at[p, g]
+            dev = lambda g: g * 2 + p
+            loc = pltpu.make_async_copy(ins[i], slot(me // 2), local_sem.at[i])
+            loc.start()
+            _ring_pair_send(i, ins[i], slot, dev, me // 2, k // 2, send_sem, recv_sem, sends, axis)
+            _ring_pair_wait(i, ins[i], slot, dev, me // 2, k // 2, send_sem, recv_sem, axis)
+            loc.wait()
+            c = pltpu.make_async_remote_copy(
+                outs[i].at[p], outs[i].at[p], send_sem.at[i, 2 * k - 1], recv_sem.at[i, 2 * k - 1],
+                device_id=_dev(axis, partner), device_id_type=pl.DeviceIdType.MESH,
+            )
+            c.start()
+            sends.append(c)
+            continue
         if mode == "pswap":
             c = pltpu.make_async_remote_copy(
                 ins[i], outs[i], send_sem.at[i, 0], recv_sem.at[i, me],
@@ -138,6 +210,19 @@
     for i, (mode, axis) in enumerate(zip(modes, axes)):
         k = lax.axis_size(axis)
         me = lax.axis_index(axis)
+        if mode == "rgather":
+            _ring_pair_wait(i, ins[i], lambda g: outs[i].at[g], lambda g: g, me, k,
+                            send_sem, recv_sem, axis)
+            continue
+        if mode == "prgather":
+            p = me % 2
+            partner = me + 1 - 2 * p
+            pltpu.make_async_remote_copy(
+                outs[i].at[1 - p], outs[i].at[1 - p], send_sem.at[i, 2 * k - 1],
+                recv_sem.at[i, 2 * k - 1],
+                device_id=_dev(axis, partner), device_id_type=pl.DeviceIdType.MESH,
+            ).wait_recv()
+            continue
         if mode == "pswap":
             partner = me + 1 - 2 * (me % 2)
             pltpu.make_async_remote_copy(
@@ -180,11 +265,11 @@
     for x, axis, mode in items:
         k = lax.axis_size(axis)
         kmax = max(kmax, k)
-        if mode == "gather":
+        if mode in ("gather", "rgather"):
             out_shapes.append(jax.ShapeDtypeStruct((k,) + x.shape, x.dtype))
         elif mode in ("pswap", "pscatter"):
             out_shapes.append(jax.ShapeDtypeStruct(x.shape, x.dtype))
-        elif mode == "pgather":
+        elif mode in ("pgather", "prgather"):
             out_shapes.append(jax.ShapeDtypeStruct((2, k // 2) + x.shape, x.dtype))
         else:
             out_shapes.append(
@@ -197,8 +282,8 @@
         in_specs=[pl.BlockSpec(memory_space=pl.ANY)] * n,
         out_specs=tuple(pl.BlockSpec(memory_space=pl.ANY) for _ in range(n)),
         scratch_shapes=[
-            pltpu.SemaphoreType.DMA((n, kmax)),
-            pltpu.SemaphoreType.DMA((n, kmax)),
+            pltpu.SemaphoreType.DMA((n, 2 * kmax)),
+            pltpu.SemaphoreType.DMA((n, 2 * kmax)),
             pltpu.SemaphoreType.DMA((n,)),
         ],
         compiler_params=pltpu.CompilerParams(collective_id=cid, has_side_effects=True),
@@ -244,6 +329,8 @@
 ):
     n_row = lax.axis_size("row")
     n_col = lax.axis_size("col")
+    RG = "rgather" if n_row == 8 else "gather"
+    PG = "prgather" if n_col == 16 else "pgather"
     tok_col, feat_loc = stream_in.shape
     tok_row, ff_loc = gate_pre.shape
     total = tok_col * n_col
@@ -263,11 +350,11 @@
     sig = jax.nn.sigmoid(gate_f)
     keep_f = keep_mask.astype(jnp.float32) * keep_scale
     dropped = (gate_f * sig * up_f * keep_f * weights[:, None]).astype(jnp.bfloat16)
-    cot_full, dropped_full = exchange([(grad_out, "col", "pgather"), (dropped, "row", "gather")], 1)
+    cot_full, dropped_full = exchange([(grad_out, "col", PG), (dropped, "row", RG)], 1)
     cot_full = pair_order(cot_full)
     dropped_full = dropped_full.reshape(total, ff_loc)
     back, normed_full = reduce_scatter(
-        over_width(cot_full, w_down), "row", 2, [(normed, "col", "pgather")]
+        over_width(cot_full, w_down), "row", 2, [(normed, "col", PG)]
     )
     normed_full = pair_order(normed_full)
     grad_act = back * weights[:, None] * keep_f
@@ -287,12 +374,12 @@
 
     gpre_a, gpre_b = split(grad_gpre)
     upre_a, upre_b = split(grad_upre)
-    ga_full, ua_full = exchange([(gpre_a, "row", "gather"), (upre_a, "row", "gather")], 3)
+    ga_full, ua_full = exchange([(gpre_a, "row", RG), (upre_a, "row", RG)], 3)
     ga_full = ga_full.reshape(total // 2, ff_loc)
     ua_full = ua_full.reshape(total // 2, ff_loc)
     part_a = over_width(ga_full, w_gate) + over_width(ua_full, w_up)
     gn_a, gb_full, ub_full = pair_reduce_scatter(
-        part_a, "col", 4, [(gpre_b, "row", "gather"), (upre_b, "row", "gather")]
+        part_a, "col", 4, [(gpre_b, "row", RG), (upre_b, "row", RG)]
     )
     gb_full = gb_full.reshape(total // 2, ff_loc)
     ub_full = ub_full.reshape(total // 2, ff_loc)

time: 400 us -> 361 us (0.902)
  Pallas kernels: 314 us -> 275 us
    pallas_call x9, Pallas kernels: 314 us -> 275 us  [exchange(): pl.pallas_call(functools.partial(_exchange_kernel, modes, axes), out_shap...]
where the time goes in v11:
time: 361 us; the launch traced here: 360 us
  Pallas kernels  275 us (76%)
  other arithmetic  36.1 us (10%)
  matrix products  35.5 us (10%)
  local copies, waits for them, and re-layouts  12.7 us (4%)
    pallas_call x9, Pallas kernels, exchange(): pl.pallas_call(functools.partial(_exchange_kernel, modes, axes), out_shap...  275 us
    dot_general x5, matrix products, over_width(): lax.dot_general(left, right, (((1,), (1,)), ((), ())), preferred_element_...  18.8 us
    dot_general x3, matrix products, over_tokens(): lax.dot_general(left, right, (((0,), (0,)), ((), ())), preferred_element_...  16.7 us
    convert_element_type x2, other arithmetic, pair_reduce_scatter(): pair.astype(WIRE)  11.1 us

profile of v11, /device:TPU:64, one launch (start us, length us, event | category | flops | bytes accessed | tf_op | source)
XLA Modules:
  0.0 360.3 jit_solution(451587185928908448)
XLA Ops:
  3.3 7.8 %shard_map.129 = f32[8,1,144]{2,1,0:T(1,128)} custom-call(f32[1,144]{1,0:T(1,128)} %bitcast.125), custom_call_target="tpu_custom_call" | custom-call | tf_op jit(solution)/shard_map/pallas_call | solution.py:279
  12.6 1.8 fusion.14.refs_1_
  14.4 2.6 fusion.2.refs_1_
  17.0 55.2 %shard_map.130 = (bf16[2,8,128,1024]{3,2,1,0:T(8,128)(2,1)}, bf16[8,256,896]{2,1,0:T(8,128)(2,1)}) custom-call(bf16[128,1024]{1,0:T(8,128)(2,1)} %refs_0_.1, bf16[256,896]{1,0:T(8,128)(2,1)} %fusion.2.refs_1_), custom_call_target="tpu_custom_call" | custom-call | tf_op jit(solution)/shard_map/pallas_call | solution.py:279
  72.2 2.8 copy.32
  75.5 5.1 %convolution_convert_fusion = bf16[896,1024]{1,0:T(8,128)(2,1)} fusion(bf16[2048,896]{1,0:T(8,128)(2,1)S(1)} %bitcast.127, bf16[2048,1024]{1,0:T(8,128)(2,1)S(1)} %bitcast.106), kind=kOutput, calls=%fused_computation.15 | convolution fusion | flops 3759013888 | bytes 9699328 | tf_op jit(solution)/shard_map/dot_general | solution.py:20
  80.6 7.1 %fusion.24 = (bf16[2048,896]{1,0:T(8,128)(2,1)}, f32[2048,896]{1,0:T(8,128)}) fusion(bf16[2048,1024]{1,0:T(8,128)(2,1)S(1)} %bitcast.107, bf16[896,1024]{1,0:T(8,128)(2,1)S(1)} %copy-done), kind=kOutput, calls=%fused_computation.66 | convolution fusion | flops 3759931392 | bytes 17039360 | tf_op jit(solution)/shard_map/dot_general | solution.py:26
  87.8 73.5 %shard_map.131 = (bf16[8,256,896]{2,1,0:T(8,128)(2,1)}, bf16[2,8,128,1024]{3,2,1,0:T(8,128)(2,1)}) custom-call(bf16[2048,896]{1,0:T(8,128)(2,1)} %get-tuple-element.34.refs_0_, bf16[128,1024]{1,0:T(8,128)(2,1)} %fusion.14.refs_1_), custom_call_target="tpu_custom_call" | custom-call | tf_op jit(solution)/shard_map/pallas_call | solution.py:279
  161.3 3.0 select_reduce_fusion
  164.3 1.8 fusion.11
  166.8 2.4 copy.41
  171.2 45.2 %shard_map.132 = (bf16[8,128,896]{2,1,0:T(8,128)(2,1)}, bf16[8,128,896]{2,1,0:T(8,128)(2,1)}) custom-call(bf16[128,896]{1,0:T(8,128)(2,1)} %bitcast.122, bf16[128,896]{1,0:T(8,128)(2,1)} %bitcast.121), custom_call_target="tpu_custom_call" | custom-call | tf_op jit(solution)/shard_map/pallas_call | solution.py:279
  216.4 4.6 %fusion.25 = f32[1024,1024]{1,0:T(8,128)S(1)} fusion(bf16[1024,896]{1,0:T(8,128)(2,1)} %bitcast.111, bf16[1024,896]{1,0:T(8,128)(2,1)} %param.17), kind=kOutput, calls=%fused_computation.67 | convolution fusion | flops 1879048192 | bytes 7864320 | tf_op jit(solution)/shard_map/dot_general | solution.py:26
  221.0 2.4 convolution_add_fusion.1
  223.4 2.0 copy-done.3
  225.3 1.8 select_bitcast_fusion.1.refs_0_
  227.1 5.1 %shard_map.133 = f32[8,64,1024]{2,1,0:T(8,128)} custom-call(f32[8,64,1024]{2,1,0:T(8,128)} %select_bitcast_fusion.1.refs_0_), custom_call_target="tpu_custom_call" | custom-call | tf_op jit(solution)/shard_map/pallas_call | solution.py:279
  232.2 5.5 %fusion.21 = (bf16[8,64,1024]{2,1,0:T(8,128)(2,1)}, f32[8,64,1024]{2,1,0:T(8,128)}) fusion(f32[8,64,1024]{2,1,0:T(8,128)} %shard_map.133, f32[8,2,64,1024]{3,2,1,0:T(8,128)} %bitcast.102, pred[]{:T(512)S(6)} %eq.25), kind=kLoop, calls=%fused_computation.63 | loop fusion | flops 1572864 | bytes 9437185 | tf_op jit(solution)/shard_map/convert_element_type | solution.py:319
  237.7 53.9 %shard_map.134 = (bf16[8,64,1024]{2,1,0:T(8,128)(2,1)}, bf16[8,128,896]{2,1,0:T(8,128)(2,1)}, bf16[8,128,896]{2,1,0:T(8,128)(2,1)}) custom-call(bf16[8,64,1024]{2,1,0:T(8,128)(2,1)} %get-tuple-element.26.refs_0_, bf16[128,896]{1,0:T(8,128)(2,1)} %bitcast.124, bf16[128,896]{1,0:T(8,128)(2,1)} %bitcast.123), custom_call_target="tpu_custom_call" | custom-call | tf_op jit(solution)/shard_map/pallas_call | solution.py:279
  291.6 2.0 pad_maximum_fusion.1
  294.3 5.7 %convolution_convert_fusion.1 = bf16[1024,896]{1,0:T(8,128)(2,1)} fusion(bf16[2048,1024]{1,0:T(8,128)(2,1)S(1)} %bitcast.103, bf16[2048,896]{1,0:T(8,128)(2,1)S(1)} %bitcast.110), kind=kOutput, calls=%fused_computation.16 | convolution fusion | flops 3759013888 | bytes 9699328 | tf_op jit(solution)/shard_map/dot_general | solution.py:20
  300.4 5.9 %convolution_convert_fusion.2 = bf16[1024,896]{1,0:T(8,128)(2,1)} fusion(bf16[2048,1024]{1,0:T(8,128)(2,1)S(1)} %bitcast.104, bf16[2048,896]{1,0:T(8,128)(2,1)S(1)} %bitcast.109), kind=kOutput, calls=%fused_computation.17 | convolution fusion | flops 3759013888 | bytes 9699328 | tf_op jit(solution)/shard_map/dot_general | solution.py:20
  306.3 2.4 fusion.26
  308.7 2.4 convolution_add_fusion
  311.1 1.9 copy-done.2
  313.0 1.7 select_bitcast_fusion.refs_0_
  314.8 5.1 %shard_map.135 = f32[8,64,1024]{2,1,0:T(8,128)} custom-call(f32[8,64,1024]{2,1,0:T(8,128)} %select_bitcast_fusion.refs_0_), custom_call_target="tpu_custom_call" | custom-call | tf_op jit(solution)/shard_map/pallas_call | solution.py:279
  319.9 5.6 %fusion.20 = (bf16[8,64,1024]{2,1,0:T(8,128)(2,1)}, f32[8,64,1024]{2,1,0:T(8,128)}) fusion(f32[8,64,1024]{2,1,0:T(8,128)} %shard_map.135, f32[8,2,64,1024]{3,2,1,0:T(8,128)} %bitcast.100, pred[]{:T(512)S(6)} %eq.25), kind=kLoop, calls=%fused_computation.62 | loop fusion | flops 1572864 | bytes 9437185 | tf_op jit(solution)/shard_map/convert_element_type | solution.py:319
  325.4 20.1 %shard_map.136 = bf16[8,64,1024]{2,1,0:T(8,128)(2,1)} custom-call(bf16[8,64,1024]{2,1,0:T(8,128)(2,1)} %get-tuple-element.24.refs_0_), custom_call_target="tpu_custom_call" | custom-call | tf_op jit(solution)/shard_map/pallas_call | solution.py:279
  345.6 2.0 select_reduce_fusion.2
  347.6 1.1 bitcast_add_fusion.2
  349.4 9.2 %shard_map.137 = f32[8,1,128]{2,1,0:T(1,128)} custom-call(f32[1,128]{1,0:T(1,128)} %bitcast.126), custom_call_target="tpu_custom_call" | custom-call | tf_op jit(solution)/shard_map/pallas_call | solution.py:279
  (57 shorter events, 10.8 us)
Async XLA Ops:
  0.6 80.0 %copy-start = (bf16[896,1024]{1,0:T(8,128)(2,1)S(1)}, bf16[896,1024]{1,0:T(8,128)(2,1)}, u32[]{:S(2)}) copy-start(bf16[896,1024]{1,0:T(8,128)(2,1)} %param.19) | copy-start | bytes 5505028
  72.2 3.3 copy-start.17
  161.3 3.0 copy-start.7
  161.3 3.0 copy-start.8
  164.3 2.5 copy-start.5
  166.8 3.2 copy-start.13
  216.4 4.6 %copy-start.10 = (bf16[8,128,896]{2,1,0:T(8,128)(2,1)S(1)}, bf16[8,128,896]{2,1,0:T(8,128)(2,1)}, u32[]{:S(2)}) copy-start(bf16[8,128,896]{2,1,0:T(8,128)(2,1)} %get-tuple-element.16) | copy-start | bytes 5505028
  216.4 4.6 %copy-start.19 = (bf16[1024,896]{1,0:T(8,128)(2,1)S(1)}, bf16[1024,896]{1,0:T(8,128)(2,1)}, u32[]{:S(2)}) copy-start(bf16[1024,896]{1,0:T(8,128)(2,1)} %param.18) | copy-start | bytes 5505028
  223.3 2.0 copy-start.3
  291.6 2.7 copy-start.4
  294.3 5.7 %copy-start.9 = (bf16[8,128,896]{2,1,0:T(8,128)(2,1)S(1)}, bf16[8,128,896]{2,1,0:T(8,128)(2,1)}, u32[]{:S(2)}) copy-start(bf16[8,128,896]{2,1,0:T(8,128)(2,1)} %get-tuple-element.15) | copy-start | bytes 5505028
  294.3 5.7 %copy-start.12 = (bf16[8,128,896]{2,1,0:T(8,128)(2,1)S(1)}, bf16[8,128,896]{2,1,0:T(8,128)(2,1)}, u32[]{:S(2)}) copy-start(bf16[8,128,896]{2,1,0:T(8,128)(2,1)} %get-tuple-element.18) | copy-start | bytes 5505028
  300.4 5.9 %copy-start.18 = (bf16[1024,896]{1,0:T(8,128)(2,1)S(1)}, bf16[1024,896]{1,0:T(8,128)(2,1)}, u32[]{:S(2)}) copy-start(bf16[1024,896]{1,0:T(8,128)(2,1)} %param.17) | copy-start | bytes 5505028
  306.3 2.4 copy-start.11
  306.3 2.4 copy-start.20
  311.1 1.9 copy-start.2
  325.4 20.1 %copy-start.14 = (bf16[8,64,1024]{2,1,0:T(8,128)(2,1)S(1)}, bf16[8,64,1024]{2,1,0:T(8,128)(2,1)}, u32[]{:S(2)}) copy-start(bf16[8,64,1024]{2,1,0:T(8,128)(2,1)} %get-tuple-element.17) | copy-start | bytes 3145732
  345.6 3.1 copy-start.6
  345.6 3.1 copy-start.16
  345.6 13.8 %copy-start.15 = (bf16[128,1024]{1,0:T(8,128)(2,1)S(1)}, bf16[128,1024]{1,0:T(8,128)(2,1)}, u32[]{:S(2)}) copy-start(bf16[128,1024]{1,0:T(8,128)(2,1)} %refs_0_.1) | copy-start | bytes 786436
  345.6 14.7 %copy-start.1 = (bf16[896,1024]{1,0:T(8,128)(2,1)S(1)}, bf16[896,1024]{1,0:T(8,128)(2,1)}, u32[]{:S(2)}) copy-start(bf16[896,1024]{1,0:T(8,128)(2,1)} %param.19) | copy-start | bytes 5505028

commit v12 on v11

--- a/solution.py
+++ b/solution.py
@@ -111,6 +111,48 @@
     for i, (mode, axis) in enumerate(zip(modes, axes)):
         k = lax.axis_size(axis)
         me = lax.axis_index(axis)
+        if mode == "rscatter":
+            ny = k // 2
+            ym, zm = me // 2, me % 2
+            m = outs[i].shape[1]
+            h = m // 2
+            direct = [ym * 2 + 1 - zm] + [((ym + dy) % ny) * 2 + z for dy in (1, ny - 1) for z in (0, 1)]
+            for d, tgt in enumerate(direct):
+                c = pltpu.make_async_remote_copy(
+                    ins[i].at[pl.ds(tgt * m, m)], outs[i].at[me], send_sem.at[i, d],
+                    recv_sem.at[i, me], device_id=_dev(axis, tgt),
+                    device_id_type=pl.DeviceIdType.MESH,
+                )
+                c.start()
+                sends.append(c)
+            for zt in (0, 1):
+                far = ((ym + 2) % ny) * 2 + zt
+                for e, (dy, lo) in enumerate(((1, 0), (ny - 1, h))):
+                    relay = ((ym + dy) % ny) * 2 + zt
+                    c = pltpu.make_async_remote_copy(
+                        ins[i].at[pl.ds(far * m + lo, h)], outs[i].at[k + e, pl.ds(zm * h, h)],
+                        send_sem.at[i, 5 + 2 * e + zt], recv_sem.at[i, 3 * k + 2 * e + zm],
+                        device_id=_dev(axis, relay), device_id_type=pl.DeviceIdType.MESH,
+                    )
+                    c.start()
+                    sends.append(c)
+            for e, (dy, lo, off) in enumerate(((ny - 1, 0, k), (1, h, 2 * k))):
+                for z in (0, 1):
+                    src = ((ym + dy) % ny) * 2 + z
+                    buf = outs[i].at[k + e, pl.ds(z * h, h)]
+                    pltpu.make_async_remote_copy(
+                        buf, buf, send_sem.at[i, 0], recv_sem.at[i, 3 * k + 2 * e + z],
+                        device_id=_dev(axis, src), device_id_type=pl.DeviceIdType.MESH,
+                    ).wait_recv()
+                    tgt = ((ym + ny - dy) % ny) * 2 + zm
+                    c = pltpu.make_async_remote_copy(
+                        buf, outs[i].at[src, pl.ds(lo, h)], send_sem.at[i, 9 + 2 * e + z],
+                        recv_sem.at[i, off + src], device_id=_dev(axis, tgt),
+                        device_id_type=pl.DeviceIdType.MESH,
+                    )
+                    c.start()
+                    sends.append(c)
+            continue
         if mode == "rgather":
             loc = pltpu.make_async_copy(ins[i], outs[i].at[me], local_sem.at[i])
             loc.start()
@@ -210,6 +252,27 @@
     for i, (mode, axis) in enumerate(zip(modes, axes)):
         k = lax.axis_size(axis)
         me = lax.axis_index(axis)
+        if mode == "rscatter":
+            ny = k // 2
+            ym, zm = me // 2, me % 2
+            m = outs[i].shape[1]
+            h = m // 2
+            direct = [ym * 2 + 1 - zm] + [((ym + dy) % ny) * 2 + z for dy in (1, ny - 1) for z in (0, 1)]
+            for srcdev in direct:
+                pltpu.make_async_remote_copy(
+                    ins[i].at[pl.ds(0, m)], outs[i].at[srcdev], send_sem.at[i, 0],
+                    recv_sem.at[i, srcdev], device_id=_dev(axis, srcdev),
+                    device_id_type=pl.DeviceIdType.MESH,
+                ).wait_recv()
+            for z in (0, 1):
+                far = ((ym + 2) % ny) * 2 + z
+                for lo, off in ((0, k), (h, 2 * k)):
+                    dst = outs[i].at[far, pl.ds(lo, h)]
+                    pltpu.make_async_remote_copy(
+                        dst, dst, send_sem.at[i, 0], recv_sem.at[i, off + far],
+                        device_id=_dev(axis, far), device_id_type=pl.DeviceIdType.MESH,
+                    ).wait_recv()
+            continue
         if mode == "rgather":
             _ring_pair_wait(i, ins[i], lambda g: outs[i].at[g], lambda g: g, me, k,
                             send_sem, recv_sem, axis)
@@ -267,6 +330,10 @@
         kmax = max(kmax, k)
         if mode in ("gather", "rgather"):
             out_shapes.append(jax.ShapeDtypeStruct((k,) + x.shape, x.dtype))
+        elif mode == "rscatter":
+            out_shapes.append(
+                jax.ShapeDtypeStruct((k + 2, x.shape[0] // k) + x.shape[1:], x.dtype)
+            )
         elif mode in ("pswap", "pscatter"):
             out_shapes.append(jax.ShapeDtypeStruct(x.shape, x.dtype))
         elif mode in ("pgather", "prgather"):
@@ -282,8 +349,8 @@
         in_specs=[pl.BlockSpec(memory_space=pl.ANY)] * n,
         out_specs=tuple(pl.BlockSpec(memory_space=pl.ANY) for _ in range(n)),
         scratch_shapes=[
-            pltpu.SemaphoreType.DMA((n, 2 * kmax)),
-            pltpu.SemaphoreType.DMA((n, 2 * kmax)),
+            pltpu.SemaphoreType.DMA((n, 4 * kmax)),
+            pltpu.SemaphoreType.DMA((n, 4 * kmax)),
             pltpu.SemaphoreType.DMA((n,)),
         ],
         compiler_params=pltpu.CompilerParams(collective_id=cid, has_side_effects=True),
@@ -294,12 +361,12 @@
     return jnp.swapaxes(v, 0, 1).reshape((-1,) + v.shape[3:])
 
 
-def reduce_scatter(parts, axis, cid, extra=()):
+def reduce_scatter(parts, axis, cid, extra=(), mode="scatter"):
     k = lax.axis_size(axis)
     me = lax.axis_index(axis)
     m = parts.shape[0] // k
-    outs = exchange([(parts.astype(WIRE), axis, "scatter")] + list(extra), cid)
-    slots = outs[0]
+    outs = exchange([(parts.astype(WIRE), axis, mode)] + list(extra), cid)
+    slots = outs[0][:k]
     mine = lax.dynamic_slice_in_dim(parts, me * m, m, axis=0)
     keep = (jnp.arange(k) != me).reshape((k,) + (1,) * (slots.ndim - 1))
     other = jnp.sum(jnp.where(keep, slots.astype(jnp.float32), 0.0), axis=0)
@@ -354,7 +421,8 @@
     cot_full = pair_order(cot_full)
     dropped_full = dropped_full.reshape(total, ff_loc)
     back, normed_full = reduce_scatter(
-        over_width(cot_full, w_down), "row", 2, [(normed, "col", PG)]
+        over_width(cot_full, w_down), "row", 2, [(normed, "col", PG)],
+        "rscatter" if n_row == 8 else "scatter",
     )
     normed_full = pair_order(normed_full)
     grad_act = back * weights[:, None] * keep_f

time: 361 us -> 367 us (1.017)
  Pallas kernels: 275 us -> 281 us
    pallas_call x9, Pallas kernels: 275 us -> 281 us  [exchange(): pl.pallas_call(functools.partial(_exchange_kernel, modes, axes), out_shap...]
where the time goes in v12:
time: 367 us; the launch traced here: 366 us
  Pallas kernels  281 us (77%)
  other arithmetic  36.1 us (10%)
  matrix products  35.3 us (10%)
  local copies, waits for them, and re-layouts  12.7 us (3%)
    pallas_call x9, Pallas kernels, exchange(): pl.pallas_call(functools.partial(_exchange_kernel, modes, axes), out_shap...  281 us
    dot_general x5, matrix products, over_width(): lax.dot_general(left, right, (((1,), (1,)), ((), ())), preferred_element_...  18.8 us
    dot_general x3, matrix products, over_tokens(): lax.dot_general(left, right, (((0,), (0,)), ((), ())), preferred_element_...  16.5 us
    convert_element_type x2, other arithmetic, pair_reduce_scatter(): pair.astype(WIRE)  11.1 us

profile of v12, /device:TPU:64, one launch (start us, length us, event | category | flops | bytes accessed | tf_op | source)
XLA Modules:
  0.0 366.4 jit_solution(16427457156911014626)
XLA Ops:
  3.3 8.1 %shard_map.129 = f32[8,1,144]{2,1,0:T(1,128)} custom-call(f32[1,144]{1,0:T(1,128)} %bitcast.125), custom_call_target="tpu_custom_call" | custom-call | tf_op jit(solution)/shard_map/pallas_call | solution.py:346
  12.9 1.8 fusion.14.refs_1_
  14.7 2.6 fusion.2.refs_1_
  17.3 56.4 %shard_map.130 = (bf16[2,8,128,1024]{3,2,1,0:T(8,128)(2,1)}, bf16[8,256,896]{2,1,0:T(8,128)(2,1)}) custom-call(bf16[128,1024]{1,0:T(8,128)(2,1)} %refs_0_.1, bf16[256,896]{1,0:T(8,128)(2,1)} %fusion.2.refs_1_), custom_call_target="tpu_custom_call" | custom-call | tf_op jit(solution)/shard_map/pallas_call | solution.py:346
  73.7 2.8 copy.32
  77.0 5.1 %convolution_convert_fusion = bf16[896,1024]{1,0:T(8,128)(2,1)} fusion(bf16[2048,896]{1,0:T(8,128)(2,1)S(1)} %bitcast.127, bf16[2048,1024]{1,0:T(8,128)(2,1)S(1)} %bitcast.106), kind=kOutput, calls=%fused_computation.15 | convolution fusion | flops 3759013888 | bytes 9699328 | tf_op jit(solution)/shard_map/dot_general | solution.py:20
  82.1 7.1 %fusion.24 = (bf16[2048,896]{1,0:T(8,128)(2,1)}, f32[2048,896]{1,0:T(8,128)}) fusion(bf16[2048,1024]{1,0:T(8,128)(2,1)S(1)} %bitcast.107, bf16[896,1024]{1,0:T(8,128)(2,1)S(1)} %copy-done), kind=kOutput, calls=%fused_computation.66 | convolution fusion | flops 3759931392 | bytes 17039360 | tf_op jit(solution)/shard_map/dot_general | solution.py:26
  89.2 76.0 %shard_map.131 = (bf16[10,256,896]{2,1,0:T(8,128)(2,1)}, bf16[2,8,128,1024]{3,2,1,0:T(8,128)(2,1)}) custom-call(bf16[2048,896]{1,0:T(8,128)(2,1)} %get-tuple-element.34.refs_0_, bf16[128,1024]{1,0:T(8,128)(2,1)} %fusion.14.refs_1_), custom_call_target="tpu_custom_call" | custom-call | tf_op jit(solution)/shard_map/pallas_call | solution.py:346
  165.3 3.0 select_reduce_fusion
  168.3 1.8 fusion.11
  170.8 2.4 copy.41
  175.2 45.1 %shard_map.132 = (bf16[8,128,896]{2,1,0:T(8,128)(2,1)}, bf16[8,128,896]{2,1,0:T(8,128)(2,1)}) custom-call(bf16[128,896]{1,0:T(8,128)(2,1)} %bitcast.122, bf16[128,896]{1,0:T(8,128)(2,1)} %bitcast.121), custom_call_target="tpu_custom_call" | custom-call | tf_op jit(solution)/shard_map/pallas_call | solution.py:346
  220.3 4.6 %fusion.25 = f32[1024,1024]{1,0:T(8,128)S(1)} fusion(bf16[1024,896]{1,0:T(8,128)(2,1)} %bitcast.111, bf16[1024,896]{1,0:T(8,128)(2,1)} %param.17), kind=kOutput, calls=%fused_computation.67 | convolution fusion | flops 1879048192 | bytes 7864320 | tf_op jit(solution)/shard_map/dot_general | solution.py:26
  224.9 2.4 convolution_add_fusion.1
  227.2 2.0 copy-done.3
  229.2 1.8 select_bitcast_fusion.1.refs_0_
  231.0 5.7 %shard_map.133 = f32[8,64,1024]{2,1,0:T(8,128)} custom-call(f32[8,64,1024]{2,1,0:T(8,128)} %select_bitcast_fusion.1.refs_0_), custom_call_target="tpu_custom_call" | custom-call | tf_op jit(solution)/shard_map/pallas_call | solution.py:346
  236.6 5.5 %fusion.21 = (bf16[8,64,1024]{2,1,0:T(8,128)(2,1)}, f32[8,64,1024]{2,1,0:T(8,128)}) fusion(f32[8,64,1024]{2,1,0:T(8,128)} %shard_map.133, f32[8,2,64,1024]{3,2,1,0:T(8,128)} %bitcast.102, pred[]{:T(512)S(6)} %eq.25), kind=kLoop, calls=%fused_computation.63 | loop fusion | flops 1572864 | bytes 9437185 | tf_op jit(solution)/shard_map/convert_element_type | solution.py:386
  242.2 52.2 %shard_map.134 = (bf16[8,64,1024]{2,1,0:T(8,128)(2,1)}, bf16[8,128,896]{2,1,0:T(8,128)(2,1)}, bf16[8,128,896]{2,1,0:T(8,128)(2,1)}) custom-call(bf16[8,64,1024]{2,1,0:T(8,128)(2,1)} %get-tuple-element.26.refs_0_, bf16[128,896]{1,0:T(8,128)(2,1)} %bitcast.124, bf16[128,896]{1,0:T(8,128)(2,1)} %bitcast.123), custom_call_target="tpu_custom_call" | custom-call | tf_op jit(solution)/shard_map/pallas_call | solution.py:346
  294.4 2.0 pad_maximum_fusion.1
  297.1 5.7 %convolution_convert_fusion.1 = bf16[1024,896]{1,0:T(8,128)(2,1)} fusion(bf16[2048,1024]{1,0:T(8,128)(2,1)S(1)} %bitcast.103, bf16[2048,896]{1,0:T(8,128)(2,1)S(1)} %bitcast.110), kind=kOutput, calls=%fused_computation.16 | convolution fusion | flops 3759013888 | bytes 9699328 | tf_op jit(solution)/shard_map/dot_general | solution.py:20
  303.2 5.7 %convolution_convert_fusion.2 = bf16[1024,896]{1,0:T(8,128)(2,1)} fusion(bf16[2048,1024]{1,0:T(8,128)(2,1)S(1)} %bitcast.104, bf16[2048,896]{1,0:T(8,128)(2,1)S(1)} %bitcast.109), kind=kOutput, calls=%fused_computation.17 | convolution fusion | flops 3759013888 | bytes 9699328 | tf_op jit(solution)/shard_map/dot_general | solution.py:20
  308.9 2.4 fusion.26
  311.3 2.4 convolution_add_fusion
  313.7 1.9 copy-done.2
  315.6 1.7 select_bitcast_fusion.refs_0_
  317.3 5.7 %shard_map.135 = f32[8,64,1024]{2,1,0:T(8,128)} custom-call(f32[8,64,1024]{2,1,0:T(8,128)} %select_bitcast_fusion.refs_0_), custom_call_target="tpu_custom_call" | custom-call | tf_op jit(solution)/shard_map/pallas_call | solution.py:346
  323.0 5.6 %fusion.20 = (bf16[8,64,1024]{2,1,0:T(8,128)(2,1)}, f32[8,64,1024]{2,1,0:T(8,128)}) fusion(f32[8,64,1024]{2,1,0:T(8,128)} %shard_map.135, f32[8,2,64,1024]{3,2,1,0:T(8,128)} %bitcast.100, pred[]{:T(512)S(6)} %eq.25), kind=kLoop, calls=%fused_computation.62 | loop fusion | flops 1572864 | bytes 9437185 | tf_op jit(solution)/shard_map/convert_element_type | solution.py:386
  328.6 21.5 %shard_map.136 = bf16[8,64,1024]{2,1,0:T(8,128)(2,1)} custom-call(bf16[8,64,1024]{2,1,0:T(8,128)(2,1)} %get-tuple-element.24.refs_0_), custom_call_target="tpu_custom_call" | custom-call | tf_op jit(solution)/shard_map/pallas_call | solution.py:346
  350.2 2.0 select_reduce_fusion.2
  352.2 1.1 bitcast_add_fusion.2
  354.0 10.8 %shard_map.137 = f32[8,1,128]{2,1,0:T(1,128)} custom-call(f32[1,128]{1,0:T(1,128)} %bitcast.126), custom_call_target="tpu_custom_call" | custom-call | tf_op jit(solution)/shard_map/pallas_call | solution.py:346
  (57 shorter events, 10.8 us)
Async XLA Ops:
  0.6 81.4 %copy-start = (bf16[896,1024]{1,0:T(8,128)(2,1)S(1)}, bf16[896,1024]{1,0:T(8,128)(2,1)}, u32[]{:S(2)}) copy-start(bf16[896,1024]{1,0:T(8,128)(2,1)} %param.19) | copy-start | bytes 5505028
  73.7 3.3 copy-start.17
  165.2 3.0 copy-start.7
  165.3 3.0 copy-start.8
  168.3 2.5 copy-start.5
  170.8 3.2 copy-start.13
  220.3 4.6 %copy-start.10 = (bf16[8,128,896]{2,1,0:T(8,128)(2,1)S(1)}, bf16[8,128,896]{2,1,0:T(8,128)(2,1)}, u32[]{:S(2)}) copy-start(bf16[8,128,896]{2,1,0:T(8,128)(2,1)} %get-tuple-element.16) | copy-start | bytes 5505028
  220.3 4.6 %copy-start.19 = (bf16[1024,896]{1,0:T(8,128)(2,1)S(1)}, bf16[1024,896]{1,0:T(8,128)(2,1)}, u32[]{:S(2)}) copy-start(bf16[1024,896]{1,0:T(8,128)(2,1)} %param.18) | copy-start | bytes 5505028
  227.2 2.0 copy-start.3
  294.4 2.7 copy-start.4
  297.1 5.7 %copy-start.9 = (bf16[8,128,896]{2,1,0:T(8,128)(2,1)S(1)}, bf16[8,128,896]{2,1,0:T(8,128)(2,1)}, u32[]{:S(2)}) copy-start(bf16[8,128,896]{2,1,0:T(8,128)(2,1)} %get-tuple-element.15) | copy-start | bytes 5505028
  297.1 5.7 %copy-start.12 = (bf16[8,128,896]{2,1,0:T(8,128)(2,1)S(1)}, bf16[8,128,896]{2,1,0:T(8,128)(2,1)}, u32[]{:S(2)}) copy-start(bf16[8,128,896]{2,1,0:T(8,128)(2,1)} %get-tuple-element.18) | copy-start | bytes 5505028
  303.2 5.7 %copy-start.18 = (bf16[1024,896]{1,0:T(8,128)(2,1)S(1)}, bf16[1024,896]{1,0:T(8,128)(2,1)}, u32[]{:S(2)}) copy-start(bf16[1024,896]{1,0:T(8,128)(2,1)} %param.17) | copy-start | bytes 5505028
  308.9 2.4 copy-start.11
  308.9 2.4 copy-start.20
  313.7 1.9 copy-start.2
  328.6 21.6 %copy-start.14 = (bf16[8,64,1024]{2,1,0:T(8,128)(2,1)S(1)}, bf16[8,64,1024]{2,1,0:T(8,128)(2,1)}, u32[]{:S(2)}) copy-start(bf16[8,64,1024]{2,1,0:T(8,128)(2,1)} %get-tuple-element.17) | copy-start | bytes 3145732
  350.1 3.1 copy-start.6
  350.2 3.1 copy-start.16
  350.2 15.3 %copy-start.15 = (bf16[128,1024]{1,0:T(8,128)(2,1)S(1)}, bf16[128,1024]{1,0:T(8,128)(2,1)}, u32[]{:S(2)}) copy-start(bf16[128,1024]{1,0:T(8,128)(2,1)} %refs_0_.1) | copy-start | bytes 786436
  350.2 16.2 %copy-start.1 = (bf16[896,1024]{1,0:T(8,128)(2,1)S(1)}, bf16[896,1024]{1,0:T(8,128)(2,1)}, u32[]{:S(2)}) copy-start(bf16[896,1024]{1,0:T(8,128)(2,1)} %param.19) | copy-start | bytes 5505028

commit v13 on v11

--- a/solution.py
+++ b/solution.py
@@ -350,9 +350,8 @@
     sig = jax.nn.sigmoid(gate_f)
     keep_f = keep_mask.astype(jnp.float32) * keep_scale
     dropped = (gate_f * sig * up_f * keep_f * weights[:, None]).astype(jnp.bfloat16)
-    cot_full, dropped_full = exchange([(grad_out, "col", PG), (dropped, "row", RG)], 1)
+    (cot_full,) = exchange([(grad_out, "col", PG)], 1)
     cot_full = pair_order(cot_full)
-    dropped_full = dropped_full.reshape(total, ff_loc)
     back, normed_full = reduce_scatter(
         over_width(cot_full, w_down), "row", 2, [(normed, "col", PG)]
     )
@@ -384,7 +383,8 @@
     gb_full = gb_full.reshape(total // 2, ff_loc)
     ub_full = ub_full.reshape(total // 2, ff_loc)
     part_b = over_width(gb_full, w_gate) + over_width(ub_full, w_up)
-    (gn_b,) = pair_reduce_scatter(part_b, "col", 6)
+    gn_b, dropped_full = pair_reduce_scatter(part_b, "col", 6, [(dropped, "row", RG)])
+    dropped_full = dropped_full.reshape(total, ff_loc)
     grad_normed = jnp.concatenate([gn_a, gn_b], axis=0)
     gpre_full = joined(ga_full, gb_full)
     upre_full = joined(ua_full, ub_full)

time: 361 us -> 368 us (1.019)
  Pallas kernels: 275 us -> 280 us
    pallas_call x9, Pallas kernels: 275 us -> 280 us  [exchange(): pl.pallas_call(functools.partial(_exchange_kernel, modes, axes), out_shap...]
where the time goes in v13:
time: 368 us; the launch traced here: 365 us
  Pallas kernels  280 us (76%)
  matrix products  37.6 us (10%)
  other arithmetic  34.3 us (9%)
  local copies, waits for them, and re-layouts  11.4 us (3%)
    pallas_call x9, Pallas kernels, exchange(): pl.pallas_call(functools.partial(_exchange_kernel, modes, axes), out_shap...  280 us
    dot_general x5, matrix products, over_width(): lax.dot_general(left, right, (((1,), (1,)), ((), ())), preferred_element_...  18.8 us
    dot_general x3, matrix products, over_tokens(): lax.dot_general(left, right, (((0,), (0,)), ((), ())), preferred_element_...  18.7 us
    convert_element_type x2, other arithmetic, pair_reduce_scatter(): pair.astype(WIRE)  11.1 us

profile of v13, /device:TPU:64, one launch (start us, length us, event | category | flops | bytes accessed | tf_op | source)
XLA Modules:
  0.0 364.8 jit_solution(6288714964777339288)
XLA Ops:
  1.6 1.1 fusion.12
  3.3 7.8 %shard_map.129 = f32[8,1,144]{2,1,0:T(1,128)} custom-call(f32[1,144]{1,0:T(1,128)} %bitcast.117), custom_call_target="tpu_custom_call" | custom-call | tf_op jit(solution)/shard_map/pallas_call | solution.py:279
  12.6 1.8 fusion.14.refs_1_
  14.4 31.3 %shard_map.130 = bf16[2,8,128,1024]{3,2,1,0:T(8,128)(2,1)} custom-call(bf16[128,1024]{1,0:T(8,128)(2,1)} %refs_0_.1), custom_call_target="tpu_custom_call" | custom-call | tf_op jit(solution)/shard_map/pallas_call | solution.py:279
  45.7 2.6 copy.24
  48.4 7.2 %fusion.24 = (bf16[2048,896]{1,0:T(8,128)(2,1)}, f32[2048,896]{1,0:T(8,128)}) fusion(bf16[2048,1024]{1,0:T(8,128)(2,1)S(1)} %bitcast.96, bf16[896,1024]{1,0:T(8,128)(2,1)S(1)} %copy-done), kind=kOutput, calls=%fused_computation.66 | convolution fusion | flops 3759931392 | bytes 17039360 | tf_op jit(solution)/shard_map/dot_general | solution.py:26
  55.6 61.4 %shard_map.131 = (bf16[8,256,896]{2,1,0:T(8,128)(2,1)}, bf16[2,8,128,1024]{3,2,1,0:T(8,128)(2,1)}) custom-call(bf16[2048,896]{1,0:T(8,128)(2,1)} %get-tuple-element.35.refs_0_, bf16[128,1024]{1,0:T(8,128)(2,1)} %fusion.14.refs_1_), custom_call_target="tpu_custom_call" | custom-call | tf_op jit(solution)/shard_map/pallas_call | solution.py:279
  117.0 3.0 select_reduce_fusion
  120.1 2.7 fusion.11
  122.9 2.4 copy.29
  127.2 55.0 %shard_map.132 = (bf16[8,128,896]{2,1,0:T(8,128)(2,1)}, bf16[8,128,896]{2,1,0:T(8,128)(2,1)}) custom-call(bf16[128,896]{1,0:T(8,128)(2,1)} %bitcast.114, bf16[128,896]{1,0:T(8,128)(2,1)} %bitcast.113), custom_call_target="tpu_custom_call" | custom-call | tf_op jit(solution)/shard_map/pallas_call | solution.py:279
  182.3 4.6 %fusion.25 = f32[1024,1024]{1,0:T(8,128)S(1)} fusion(bf16[1024,896]{1,0:T(8,128)(2,1)} %bitcast.104, bf16[1024,896]{1,0:T(8,128)(2,1)} %param.17), kind=kOutput, calls=%fused_computation.67 | convolution fusion | flops 1879048192 | bytes 7864320 | tf_op jit(solution)/shard_map/dot_general | solution.py:26
  186.8 2.4 convolution_add_fusion.1
  189.2 2.0 copy-done.3
  191.3 1.7 select_bitcast_fusion.1.refs_0_
  193.0 5.1 %shard_map.133 = f32[8,64,1024]{2,1,0:T(8,128)} custom-call(f32[8,64,1024]{2,1,0:T(8,128)} %select_bitcast_fusion.1.refs_0_), custom_call_target="tpu_custom_call" | custom-call | tf_op jit(solution)/shard_map/pallas_call | solution.py:279
  198.1 5.5 %fusion.21 = (bf16[8,64,1024]{2,1,0:T(8,128)(2,1)}, f32[8,64,1024]{2,1,0:T(8,128)}) fusion(f32[8,64,1024]{2,1,0:T(8,128)} %shard_map.133, f32[8,2,64,1024]{3,2,1,0:T(8,128)} %bitcast.94, pred[]{:T(512)S(6)} %eq.25), kind=kLoop, calls=%fused_computation.63 | loop fusion | flops 1572864 | bytes 9437185 | tf_op jit(solution)/shard_map/convert_element_type | solution.py:319
  203.6 49.7 %shard_map.134 = (bf16[8,64,1024]{2,1,0:T(8,128)(2,1)}, bf16[8,128,896]{2,1,0:T(8,128)(2,1)}, bf16[8,128,896]{2,1,0:T(8,128)(2,1)}) custom-call(bf16[8,64,1024]{2,1,0:T(8,128)(2,1)} %get-tuple-element.26.refs_0_, bf16[128,896]{1,0:T(8,128)(2,1)} %bitcast.116, bf16[128,896]{1,0:T(8,128)(2,1)} %bitcast.115), custom_call_target="tpu_custom_call" | custom-call | tf_op jit(solution)/shard_map/pallas_call | solution.py:279
  253.3 2.0 pad_maximum_fusion.1
  256.1 5.7 %convolution_convert_fusion.1 = bf16[1024,896]{1,0:T(8,128)(2,1)} fusion(bf16[2048,1024]{1,0:T(8,128)(2,1)S(1)} %bitcast.98, bf16[2048,896]{1,0:T(8,128)(2,1)S(1)} %bitcast.102), kind=kOutput, calls=%fused_computation.16 | convolution fusion | flops 3759013888 | bytes 9699328 | tf_op jit(solution)/shard_map/dot_general | solution.py:20
  262.2 5.7 %convolution_convert_fusion.2 = bf16[1024,896]{1,0:T(8,128)(2,1)} fusion(bf16[2048,1024]{1,0:T(8,128)(2,1)S(1)} %bitcast.99, bf16[2048,896]{1,0:T(8,128)(2,1)S(1)} %bitcast.101), kind=kOutput, calls=%fused_computation.17 | convolution fusion | flops 3759013888 | bytes 9699328 | tf_op jit(solution)/shard_map/dot_general | solution.py:20
  267.9 2.4 fusion.26
  270.3 2.4 convolution_add_fusion
  272.6 1.9 copy-done.2
  274.6 1.7 select_bitcast_fusion.refs_0_
  276.3 5.1 %shard_map.135 = f32[8,64,1024]{2,1,0:T(8,128)} custom-call(f32[8,64,1024]{2,1,0:T(8,128)} %select_bitcast_fusion.refs_0_), custom_call_target="tpu_custom_call" | custom-call | tf_op jit(solution)/shard_map/pallas_call | solution.py:279
  281.4 5.5 %fusion.20 = (bf16[8,64,1024]{2,1,0:T(8,128)(2,1)}, f32[8,64,1024]{2,1,0:T(8,128)}) fusion(f32[8,64,1024]{2,1,0:T(8,128)} %shard_map.135, f32[8,2,64,1024]{3,2,1,0:T(8,128)} %bitcast.92, pred[]{:T(512)S(6)} %eq.25), kind=kLoop, calls=%fused_computation.62 | loop fusion | flops 1572864 | bytes 9437185 | tf_op jit(solution)/shard_map/convert_element_type | solution.py:319
  286.9 51.0 %shard_map.136 = (bf16[8,64,1024]{2,1,0:T(8,128)(2,1)}, bf16[8,256,896]{2,1,0:T(8,128)(2,1)}) custom-call(bf16[8,64,1024]{2,1,0:T(8,128)(2,1)} %get-tuple-element.24.refs_0_, bf16[256,896]{1,0:T(8,128)(2,1)} %get-tuple-element.30.refs_1_), custom_call_target="tpu_custom_call" | custom-call | tf_op jit(solution)/shard_map/pallas_call | solution.py:279
  337.9 2.0 select_reduce_fusion.2
  339.9 1.1 bitcast_add_fusion.2
  341.0 7.3 %convolution_convert_fusion = bf16[896,1024]{1,0:T(8,128)(2,1)} fusion(bf16[2048,896]{1,0:T(8,128)(2,1)} %bitcast.119, bf16[2048,1024]{1,0:T(8,128)(2,1)S(1)} %bitcast.97), kind=kOutput, calls=%fused_computation.15 | convolution fusion | flops 3759013888 | bytes 9699328 | tf_op jit(solution)/shard_map/dot_general | solution.py:20
  349.1 14.1 %shard_map.137 = f32[8,1,128]{2,1,0:T(1,128)} custom-call(f32[1,128]{1,0:T(1,128)} %bitcast.118), custom_call_target="tpu_custom_call" | custom-call | tf_op jit(solution)/shard_map/pallas_call | solution.py:279
  (58 shorter events, 8.5 us)
Async XLA Ops:
  0.6 47.7 %copy-start = (bf16[896,1024]{1,0:T(8,128)(2,1)S(1)}, bf16[896,1024]{1,0:T(8,128)(2,1)}, u32[]{:S(2)}) copy-start(bf16[896,1024]{1,0:T(8,128)(2,1)} %param.19) | copy-start | bytes 5505028
  48.3 7.2 %copy-start.4 = (bf16[8,2,128,1024]{3,2,1,0:T(8,128)(2,1)}, bf16[8,2,128,1024]{3,2,1,0:T(8,128)(2,1)S(1)}, u32[]{:S(2)}) copy-start(bf16[8,2,128,1024]{3,2,1,0:T(8,128)(2,1)S(1)} %copy.24) | copy-start | bytes 12582916
  117.0 3.1 copy-start.13
  117.0 3.1 copy-start.14
  117.0 3.1 copy-start.17
  120.1 2.7 copy-start.7
  182.2 4.6 %copy-start.10 = (bf16[8,128,896]{2,1,0:T(8,128)(2,1)S(1)}, bf16[8,128,896]{2,1,0:T(8,128)(2,1)}, u32[]{:S(2)}) copy-start(bf16[8,128,896]{2,1,0:T(8,128)(2,1)} %get-tuple-element.15) | copy-start | bytes 5505028
  182.3 4.6 %copy-start.20 = (bf16[1024,896]{1,0:T(8,128)(2,1)S(1)}, bf16[1024,896]{1,0:T(8,128)(2,1)}, u32[]{:S(2)}) copy-start(bf16[1024,896]{1,0:T(8,128)(2,1)} %param.18) | copy-start | bytes 5505028
  189.2 2.0 copy-start.3
  253.3 2.7 copy-start.6
  256.1 5.7 %copy-start.9 = (bf16[8,128,896]{2,1,0:T(8,128)(2,1)S(1)}, bf16[8,128,896]{2,1,0:T(8,128)(2,1)}, u32[]{:S(2)}) copy-start(bf16[8,128,896]{2,1,0:T(8,128)(2,1)} %get-tuple-element.14) | copy-start | bytes 5505028
  256.1 5.7 %copy-start.12 = (bf16[8,128,896]{2,1,0:T(8,128)(2,1)S(1)}, bf16[8,128,896]{2,1,0:T(8,128)(2,1)}, u32[]{:S(2)}) copy-start(bf16[8,128,896]{2,1,0:T(8,128)(2,1)} %get-tuple-element.17) | copy-start | bytes 5505028
  262.2 5.7 %copy-start.19 = (bf16[1024,896]{1,0:T(8,128)(2,1)S(1)}, bf16[1024,896]{1,0:T(8,128)(2,1)}, u32[]{:S(2)}) copy-start(bf16[1024,896]{1,0:T(8,128)(2,1)} %param.17) | copy-start | bytes 5505028
  267.9 2.4 copy-start.11
  267.9 2.4 copy-start.21
  272.6 1.9 copy-start.2
  286.9 51.0 %copy-start.15 = (bf16[8,64,1024]{2,1,0:T(8,128)(2,1)S(1)}, bf16[8,64,1024]{2,1,0:T(8,128)(2,1)}, u32[]{:S(2)}) copy-start(bf16[8,64,1024]{2,1,0:T(8,128)(2,1)} %get-tuple-element.16) | copy-start | bytes 3145732
  337.9 3.1 copy-start.5
  341.0 7.4 %copy-start.8 = (bf16[128,1024]{1,0:T(8,128)(2,1)S(1)}, bf16[128,1024]{1,0:T(8,128)(2,1)}, u32[]{:S(2)}) copy-start(bf16[128,1024]{1,0:T(8,128)(2,1)} %param.10) | copy-start | bytes 786436
  341.0 7.4 %copy-start.18 = (f32[1024]{0:T(1024)S(1)}, f32[1024]{0:T(1024)}, u32[]{:S(2)}) copy-start(f32[1024]{0:T(1024)} %param.16) | copy-start | bytes 12292
  341.0 22.9 %copy-start.16 = (bf16[128,1024]{1,0:T(8,128)(2,1)S(1)}, bf16[128,1024]{1,0:T(8,128)(2,1)}, u32[]{:S(2)}) copy-start(bf16[128,1024]{1,0:T(8,128)(2,1)} %refs_0_.1) | copy-start | bytes 786436
  341.0 23.8 %copy-start.1 = (bf16[896,1024]{1,0:T(8,128)(2,1)S(1)}, bf16[896,1024]{1,0:T(8,128)(2,1)}, u32[]{:S(2)}) copy-start(bf16[896,1024]{1,0:T(8,128)(2,1)} %param.19) | copy-start | bytes 5505028

commit v14 on v11

--- a/solution.py
+++ b/solution.py
@@ -339,7 +339,7 @@
         jnp.float32
     )
     stats = jnp.concatenate([jnp.sum(xs * xs, axis=1), jnp.sum(onehot, axis=0)])[None, :]
-    (stats_all,) = exchange([(stats, "row", "gather")], 0)
+    stats_all, cot_full = exchange([(stats, "row", "gather"), (grad_out, "col", PG)], 1)
     stats_sum = jnp.sum(stats_all, axis=(0, 1))
     squares, counts = stats_sum[:tok_col], stats_sum[tok_col:]
     weights = jnp.sum(onehot * (total / (SEGS * counts))[None, :], axis=1)
@@ -350,12 +350,11 @@
     sig = jax.nn.sigmoid(gate_f)
     keep_f = keep_mask.astype(jnp.float32) * keep_scale
     dropped = (gate_f * sig * up_f * keep_f * weights[:, None]).astype(jnp.bfloat16)
-    cot_full, dropped_full = exchange([(grad_out, "col", PG), (dropped, "row", RG)], 1)
     cot_full = pair_order(cot_full)
+    back, normed_full, dropped_full = reduce_scatter(
+        over_width(cot_full, w_down), "row", 2, [(normed, "col", PG), (dropped, "row", RG)]
+    )
     dropped_full = dropped_full.reshape(total, ff_loc)
-    back, normed_full = reduce_scatter(
-        over_width(cot_full, w_down), "row", 2, [(normed, "col", PG)]
-    )
     normed_full = pair_order(normed_full)
     grad_act = back * weights[:, None] * keep_f
     grad_gpre = (grad_act * up_f * sig * (1.0 + gate_f * (1.0 - sig))).astype(jnp.bfloat16)

time: 361 us -> 372 us (1.030)
  Pallas kernels: 275 us -> 289 us
  other arithmetic: 36.1 us -> 31.1 us
    pallas_call x9 -> x8, Pallas kernels: 275 us -> 289 us  [exchange(): pl.pallas_call(functools.partial(_exchange_kernel, modes, axes), out_shap...]
where the time goes in v14:
time: 372 us
  Pallas kernels  289 us (78%)
  matrix products  38.9 us (10%)
  other arithmetic  31.1 us (8%)
  local copies, waits for them, and re-layouts  12.2 us (3%)
    pallas_call x8, Pallas kernels, exchange(): pl.pallas_call(functools.partial(_exchange_kernel, modes, axes), out_shap...  289 us
    dot_general x3, matrix products, over_tokens(): lax.dot_general(left, right, (((0,), (0,)), ((), ())), preferred_element_...  20.1 us
    dot_general x5, matrix products, over_width(): lax.dot_general(left, right, (((1,), (1,)), ((), ())), preferred_element_...  18.8 us
    convert_element_type x2, other arithmetic, pair_reduce_scatter(): pair.astype(WIRE)  11.1 us

profile of v14, /device:TPU:64, one launch (start us, length us, event | category | flops | bytes accessed | tf_op | source)
XLA Modules:
  0.0 371.7 jit_solution(12517420752837957354)
XLA Ops:
  1.6 1.1 fusion.12
  3.3 34.8 %shard_map.129 = (f32[8,1,144]{2,1,0:T(1,128)}, bf16[2,8,128,1024]{3,2,1,0:T(8,128)(2,1)}) custom-call(f32[1,144]{1,0:T(1,128)} %bitcast.125, bf16[128,1024]{1,0:T(8,128)(2,1)} %refs_1_.1), custom_call_target="tpu_custom_call" | custom-call | tf_op jit(solution)/shard_map/pallas_call | solution.py:279
  38.9 2.8 copy.32
  41.8 1.2 fusion.14.refs_1_
  43.0 1.2 fusion.2.refs_2_
  44.2 7.2 %fusion.24 = (bf16[2048,896]{1,0:T(8,128)(2,1)}, f32[2048,896]{1,0:T(8,128)}) fusion(bf16[2048,1024]{1,0:T(8,128)(2,1)S(1)} %bitcast.105, bf16[896,1024]{1,0:T(8,128)(2,1)S(1)} %copy-done), kind=kOutput, calls=%fused_computation.66 | convolution fusion | flops 3759931392 | bytes 17039360 | tf_op jit(solution)/shard_map/dot_general | solution.py:26
  51.3 101.8 %shard_map.130 = (bf16[8,256,896]{2,1,0:T(8,128)(2,1)}, bf16[2,8,128,1024]{3,2,1,0:T(8,128)(2,1)}, bf16[8,256,896]{2,1,0:T(8,128)(2,1)}) custom-call(bf16[2048,896]{1,0:T(8,128)(2,1)} %get-tuple-element.36.refs_0_, bf16[128,1024]{1,0:T(8,128)(2,1)} %fusion.14.refs_1_, bf16[256,896]{1,0:T(8,128)(2,1)} %fusion.2.refs_2_), custom_call_target="tpu_custom_call" | custom-call | tf_op jit(solution)/shard_map/pallas_call | solution.py:279
  153.2 8.7 %convolution_convert_fusion = bf16[896,1024]{1,0:T(8,128)(2,1)} fusion(bf16[2048,896]{1,0:T(8,128)(2,1)} %bitcast.127, bf16[2048,1024]{1,0:T(8,128)(2,1)} %bitcast.106), kind=kOutput, calls=%fused_computation.15 | convolution fusion | flops 3759013888 | bytes 9699328 | tf_op jit(solution)/shard_map/dot_general | solution.py:20
  162.7 1.8 fusion.11
  165.1 2.4 copy.41
  169.5 49.8 %shard_map.131 = (bf16[8,128,896]{2,1,0:T(8,128)(2,1)}, bf16[8,128,896]{2,1,0:T(8,128)(2,1)}) custom-call(bf16[128,896]{1,0:T(8,128)(2,1)} %bitcast.122, bf16[128,896]{1,0:T(8,128)(2,1)} %bitcast.121), custom_call_target="tpu_custom_call" | custom-call | tf_op jit(solution)/shard_map/pallas_call | solution.py:279
  219.4 4.6 %fusion.25 = f32[1024,1024]{1,0:T(8,128)S(1)} fusion(bf16[1024,896]{1,0:T(8,128)(2,1)} %bitcast.111, bf16[1024,896]{1,0:T(8,128)(2,1)} %param.17), kind=kOutput, calls=%fused_computation.67 | convolution fusion | flops 1879048192 | bytes 7864320 | tf_op jit(solution)/shard_map/dot_general | solution.py:26
  224.0 2.4 convolution_add_fusion.1
  226.3 2.0 copy-done.3
  228.3 1.8 select_bitcast_fusion.1.refs_0_
  230.1 5.1 %shard_map.132 = f32[8,64,1024]{2,1,0:T(8,128)} custom-call(f32[8,64,1024]{2,1,0:T(8,128)} %select_bitcast_fusion.1.refs_0_), custom_call_target="tpu_custom_call" | custom-call | tf_op jit(solution)/shard_map/pallas_call | solution.py:279
  235.1 5.5 %fusion.21 = (bf16[8,64,1024]{2,1,0:T(8,128)(2,1)}, f32[8,64,1024]{2,1,0:T(8,128)}) fusion(f32[8,64,1024]{2,1,0:T(8,128)} %shard_map.132, f32[8,2,64,1024]{3,2,1,0:T(8,128)} %bitcast.102, pred[]{:T(512)S(6)} %eq.25), kind=kLoop, calls=%fused_computation.63 | loop fusion | flops 1572864 | bytes 9437185 | tf_op jit(solution)/shard_map/convert_element_type | solution.py:319
  240.7 61.2 %shard_map.133 = (bf16[8,64,1024]{2,1,0:T(8,128)(2,1)}, bf16[8,128,896]{2,1,0:T(8,128)(2,1)}, bf16[8,128,896]{2,1,0:T(8,128)(2,1)}) custom-call(bf16[8,64,1024]{2,1,0:T(8,128)(2,1)} %get-tuple-element.28.refs_0_, bf16[128,896]{1,0:T(8,128)(2,1)} %bitcast.124, bf16[128,896]{1,0:T(8,128)(2,1)} %bitcast.123), custom_call_target="tpu_custom_call" | custom-call | tf_op jit(solution)/shard_map/pallas_call | solution.py:279
  301.9 2.0 pad_maximum_fusion.1
  304.7 5.7 %convolution_convert_fusion.1 = bf16[1024,896]{1,0:T(8,128)(2,1)} fusion(bf16[2048,1024]{1,0:T(8,128)(2,1)S(1)} %bitcast.103, bf16[2048,896]{1,0:T(8,128)(2,1)S(1)} %bitcast.110), kind=kOutput, calls=%fused_computation.16 | convolution fusion | flops 3759013888 | bytes 9699328 | tf_op jit(solution)/shard_map/dot_general | solution.py:20
  310.7 5.7 %convolution_convert_fusion.2 = bf16[1024,896]{1,0:T(8,128)(2,1)} fusion(bf16[2048,1024]{1,0:T(8,128)(2,1)S(1)} %bitcast.104, bf16[2048,896]{1,0:T(8,128)(2,1)S(1)} %bitcast.109), kind=kOutput, calls=%fused_computation.17 | convolution fusion | flops 3759013888 | bytes 9699328 | tf_op jit(solution)/shard_map/dot_general | solution.py:20
  316.4 2.4 fusion.26
  318.8 2.4 convolution_add_fusion
  321.2 1.9 copy-done.2
  323.2 1.7 select_bitcast_fusion.refs_0_
  324.9 5.1 %shard_map.134 = f32[8,64,1024]{2,1,0:T(8,128)} custom-call(f32[8,64,1024]{2,1,0:T(8,128)} %select_bitcast_fusion.refs_0_), custom_call_target="tpu_custom_call" | custom-call | tf_op jit(solution)/shard_map/pallas_call | solution.py:279
  330.0 5.6 %fusion.20 = (bf16[8,64,1024]{2,1,0:T(8,128)(2,1)}, f32[8,64,1024]{2,1,0:T(8,128)}) fusion(f32[8,64,1024]{2,1,0:T(8,128)} %shard_map.134, f32[8,2,64,1024]{3,2,1,0:T(8,128)} %bitcast.100, pred[]{:T(512)S(6)} %eq.25), kind=kLoop, calls=%fused_computation.62 | loop fusion | flops 1572864 | bytes 9437185 | tf_op jit(solution)/shard_map/convert_element_type | solution.py:319
  335.5 21.0 %shard_map.135 = bf16[8,64,1024]{2,1,0:T(8,128)(2,1)} custom-call(bf16[8,64,1024]{2,1,0:T(8,128)(2,1)} %get-tuple-element.26.refs_0_), custom_call_target="tpu_custom_call" | custom-call | tf_op jit(solution)/shard_map/pallas_call | solution.py:279
  356.6 2.0 select_reduce_fusion.2
  358.5 1.1 bitcast_add_fusion.2
  360.3 9.7 %shard_map.136 = f32[8,1,128]{2,1,0:T(1,128)} custom-call(f32[1,128]{1,0:T(1,128)} %bitcast.126), custom_call_target="tpu_custom_call" | custom-call | tf_op jit(solution)/shard_map/pallas_call | solution.py:279
  370.8 0.9 fusion.19
  (62 shorter events, 8.4 us)
Async XLA Ops:
  0.6 43.5 %copy-start = (bf16[896,1024]{1,0:T(8,128)(2,1)S(1)}, bf16[896,1024]{1,0:T(8,128)(2,1)}, u32[]{:S(2)}) copy-start(bf16[896,1024]{1,0:T(8,128)(2,1)} %param.19) | copy-start | bytes 5505028
  38.8 2.9 copy-start.20
  38.8 3.0 copy-start.7
  38.8 3.0 copy-start.19
  38.9 4.1 %copy-start.8 = (bf16[256,896]{1,0:T(8,128)(2,1)S(1)}, bf16[256,896]{1,0:T(8,128)(2,1)}, u32[]{:S(2)}) copy-start(bf16[256,896]{1,0:T(8,128)(2,1)} %param.12) | copy-start | bytes 1376260
  38.9 4.1 %copy-start.10 = (s32[256,896]{1,0:T(8,128)S(1)}, s32[256,896]{1,0:T(8,128)}, u32[]{:S(2)}) copy-start(s32[256,896]{1,0:T(8,128)} %param.14) | copy-start | bytes 2752516
  38.9 4.1 %copy-start.15 = (bf16[256,896]{1,0:T(8,128)(2,1)S(1)}, bf16[256,896]{1,0:T(8,128)(2,1)}, u32[]{:S(2)}) copy-start(bf16[256,896]{1,0:T(8,128)(2,1)} %param.13) | copy-start | bytes 1376260
  41.7 9.7 %copy-start.5 = (bf16[8,2,128,1024]{3,2,1,0:T(8,128)(2,1)}, bf16[8,2,128,1024]{3,2,1,0:T(8,128)(2,1)S(1)}, u32[]{:S(2)}) copy-start(bf16[8,2,128,1024]{3,2,1,0:T(8,128)(2,1)S(1)} %copy.32) | copy-start | bytes 12582916
  153.2 8.7 %copy-start.9 = (bf16[8,256,896]{2,1,0:T(8,128)(2,1)S(1)}, bf16[8,256,896]{2,1,0:T(8,128)(2,1)}, u32[]{:S(2)}) copy-start(bf16[8,256,896]{2,1,0:T(8,128)(2,1)} %get-tuple-element.16) | copy-start | bytes 11010052
  162.7 2.5 copy-start.6
  165.1 3.2 copy-start.16
  219.3 4.6 %copy-start.12 = (bf16[8,128,896]{2,1,0:T(8,128)(2,1)S(1)}, bf16[8,128,896]{2,1,0:T(8,128)(2,1)}, u32[]{:S(2)}) copy-start(bf16[8,128,896]{2,1,0:T(8,128)(2,1)} %get-tuple-element.18) | copy-start | bytes 5505028
  219.4 4.6 %copy-start.22 = (bf16[1024,896]{1,0:T(8,128)(2,1)S(1)}, bf16[1024,896]{1,0:T(8,128)(2,1)}, u32[]{:S(2)}) copy-start(bf16[1024,896]{1,0:T(8,128)(2,1)} %param.18) | copy-start | bytes 5505028
  226.3 2.0 copy-start.3
  301.9 2.7 copy-start.4
  304.7 5.7 %copy-start.11 = (bf16[8,128,896]{2,1,0:T(8,128)(2,1)S(1)}, bf16[8,128,896]{2,1,0:T(8,128)(2,1)}, u32[]{:S(2)}) copy-start(bf16[8,128,896]{2,1,0:T(8,128)(2,1)} %get-tuple-element.17) | copy-start | bytes 5505028
  304.7 5.7 %copy-start.14 = (bf16[8,128,896]{2,1,0:T(8,128)(2,1)S(1)}, bf16[8,128,896]{2,1,0:T(8,128)(2,1)}, u32[]{:S(2)}) copy-start(bf16[8,128,896]{2,1,0:T(8,128)(2,1)} %get-tuple-element.20) | copy-start | bytes 5505028
  310.7 5.7 %copy-start.21 = (bf16[1024,896]{1,0:T(8,128)(2,1)S(1)}, bf16[1024,896]{1,0:T(8,128)(2,1)}, u32[]{:S(2)}) copy-start(bf16[1024,896]{1,0:T(8,128)(2,1)} %param.17) | copy-start | bytes 5505028
  316.4 2.4 copy-start.13
  316.4 2.4 copy-start.23
  321.2 1.9 copy-start.2
  335.5 21.0 %copy-start.17 = (bf16[8,64,1024]{2,1,0:T(8,128)(2,1)S(1)}, bf16[8,64,1024]{2,1,0:T(8,128)(2,1)}, u32[]{:S(2)}) copy-start(bf16[8,64,1024]{2,1,0:T(8,128)(2,1)} %get-tuple-element.19) | copy-start | bytes 3145732
  356.5 14.2 %copy-start.18 = (bf16[128,1024]{1,0:T(8,128)(2,1)S(1)}, bf16[128,1024]{1,0:T(8,128)(2,1)}, u32[]{:S(2)}) copy-start(bf16[128,1024]{1,0:T(8,128)(2,1)} %refs_1_.1) | copy-start | bytes 786436
  356.5 15.1 %copy-start.1 = (bf16[896,1024]{1,0:T(8,128)(2,1)S(1)}, bf16[896,1024]{1,0:T(8,128)(2,1)}, u32[]{:S(2)}) copy-start(bf16[896,1024]{1,0:T(8,128)(2,1)} %param.19) | copy-start | bytes 5505028

commit v15 on v11

--- a/solution.py
+++ b/solution.py
@@ -356,7 +356,7 @@
     back, normed_full = reduce_scatter(
         over_width(cot_full, w_down), "row", 2, [(normed, "col", PG)]
     )
-    normed_full = pair_order(normed_full)
+    normed_full = normed_full.reshape(total, feat_loc)
     grad_act = back * weights[:, None] * keep_f
     grad_gpre = (grad_act * up_f * sig * (1.0 + gate_f * (1.0 - sig))).astype(jnp.bfloat16)
     grad_upre = (grad_act * gate_f * sig).astype(jnp.bfloat16)
@@ -370,7 +370,8 @@
     def joined(a, b):
         a = a.reshape(n_row, n_chunk, 1, half, ff_loc)
         b = b.reshape(n_row, n_chunk, 1, half, ff_loc)
-        return jnp.concatenate([a, b], axis=2).reshape(total, ff_loc)
+        both = jnp.concatenate([a, b], axis=2)
+        return jnp.swapaxes(both, 0, 1).reshape(total, ff_loc)
 
     gpre_a, gpre_b = split(grad_gpre)
     upre_a, upre_b = split(grad_upre)

time: 361 us -> 359 us (level)
  no operation moved by 1% of the time
where the time goes in v15:
time: 359 us
  Pallas kernels  275 us (77%)
  other arithmetic  35.7 us (10%)
  matrix products  35.5 us (10%)
  local copies, waits for them, and re-layouts  11.4 us (3%)
    pallas_call x9, Pallas kernels, exchange(): pl.pallas_call(functools.partial(_exchange_kernel, modes, axes), out_shap...  275 us
    dot_general x5, matrix products, over_width(): lax.dot_general(left, right, (((1,), (1,)), ((), ())), preferred_element_...  18.8 us
    dot_general x3, matrix products, over_tokens(): lax.dot_general(left, right, (((0,), (0,)), ((), ())), preferred_element_...  16.7 us
    convert_element_type x2, other arithmetic, pair_reduce_scatter(): pair.astype(WIRE)  11 us

profile of v15, /device:TPU:64, one launch (start us, length us, event | category | flops | bytes accessed | tf_op | source)
XLA Modules:
  0.0 358.7 jit_solution(5196368730543364225)
XLA Ops:
  3.3 7.8 %shard_map.129 = f32[8,1,144]{2,1,0:T(1,128)} custom-call(f32[1,144]{1,0:T(1,128)} %bitcast.117), custom_call_target="tpu_custom_call" | custom-call | tf_op jit(solution)/shard_map/pallas_call | solution.py:279
  12.6 1.8 fusion.14.refs_1_
  14.4 2.6 fusion.2.refs_1_
  17.0 55.2 %shard_map.130 = (bf16[2,8,128,1024]{3,2,1,0:T(8,128)(2,1)}, bf16[8,256,896]{2,1,0:T(8,128)(2,1)}) custom-call(bf16[128,1024]{1,0:T(8,128)(2,1)} %refs_0_.1, bf16[256,896]{1,0:T(8,128)(2,1)} %fusion.2.refs_1_), custom_call_target="tpu_custom_call" | custom-call | tf_op jit(solution)/shard_map/pallas_call | solution.py:279
  72.2 2.8 copy.31
  75.5 5.1 %convolution_convert_fusion = bf16[896,1024]{1,0:T(8,128)(2,1)} fusion(bf16[2048,896]{1,0:T(8,128)(2,1)S(1)} %bitcast.121, bf16[2048,1024]{1,0:T(8,128)(2,1)S(1)} %bitcast.98), kind=kOutput, calls=%fused_computation.15 | convolution fusion | flops 3759013888 | bytes 9699328 | tf_op jit(solution)/shard_map/dot_general | solution.py:20
  80.6 7.1 %fusion.24 = (bf16[2048,896]{1,0:T(8,128)(2,1)}, f32[2048,896]{1,0:T(8,128)}) fusion(bf16[2048,1024]{1,0:T(8,128)(2,1)S(1)} %bitcast.99, bf16[896,1024]{1,0:T(8,128)(2,1)S(1)} %copy-done), kind=kOutput, calls=%fused_computation.66 | convolution fusion | flops 3759931392 | bytes 17039360 | tf_op jit(solution)/shard_map/dot_general | solution.py:26
  87.8 73.5 %shard_map.131 = (bf16[8,256,896]{2,1,0:T(8,128)(2,1)}, bf16[2,8,128,1024]{3,2,1,0:T(8,128)(2,1)}) custom-call(bf16[2048,896]{1,0:T(8,128)(2,1)} %get-tuple-element.34.refs_0_, bf16[128,1024]{1,0:T(8,128)(2,1)} %fusion.14.refs_1_), custom_call_target="tpu_custom_call" | custom-call | tf_op jit(solution)/shard_map/pallas_call | solution.py:279
  161.3 3.0 select_reduce_fusion
  164.4 1.7 fusion.11
  168.0 45.2 %shard_map.132 = (bf16[8,128,896]{2,1,0:T(8,128)(2,1)}, bf16[8,128,896]{2,1,0:T(8,128)(2,1)}) custom-call(bf16[128,896]{1,0:T(8,128)(2,1)} %bitcast.114, bf16[128,896]{1,0:T(8,128)(2,1)} %bitcast.113), custom_call_target="tpu_custom_call" | custom-call | tf_op jit(solution)/shard_map/pallas_call | solution.py:279
  213.2 4.6 %fusion.25 = f32[1024,1024]{1,0:T(8,128)S(1)} fusion(bf16[1024,896]{1,0:T(8,128)(2,1)} %bitcast.103, bf16[1024,896]{1,0:T(8,128)(2,1)} %param.17), kind=kOutput, calls=%fused_computation.67 | convolution fusion | flops 1879048192 | bytes 7864320 | tf_op jit(solution)/shard_map/dot_general | solution.py:26
  217.8 2.4 convolution_add_fusion.1
  220.2 1.9 copy-done.3
  222.1 1.7 select_bitcast_fusion.1.refs_0_
  223.8 5.1 %shard_map.133 = f32[8,64,1024]{2,1,0:T(8,128)} custom-call(f32[8,64,1024]{2,1,0:T(8,128)} %select_bitcast_fusion.1.refs_0_), custom_call_target="tpu_custom_call" | custom-call | tf_op jit(solution)/shard_map/pallas_call | solution.py:279
  228.9 5.5 %fusion.21 = (bf16[8,64,1024]{2,1,0:T(8,128)(2,1)}, f32[8,64,1024]{2,1,0:T(8,128)}) fusion(f32[8,64,1024]{2,1,0:T(8,128)} %shard_map.133, f32[8,2,64,1024]{3,2,1,0:T(8,128)} %bitcast.97, pred[]{:T(512)S(6)} %eq.25), kind=kLoop, calls=%fused_computation.63 | loop fusion | flops 1572864 | bytes 9437185 | tf_op jit(solution)/shard_map/convert_element_type | solution.py:319
  234.4 53.9 %shard_map.134 = (bf16[8,64,1024]{2,1,0:T(8,128)(2,1)}, bf16[8,128,896]{2,1,0:T(8,128)(2,1)}, bf16[8,128,896]{2,1,0:T(8,128)(2,1)}) custom-call(bf16[8,64,1024]{2,1,0:T(8,128)(2,1)} %get-tuple-element.26.refs_0_, bf16[128,896]{1,0:T(8,128)(2,1)} %bitcast.116, bf16[128,896]{1,0:T(8,128)(2,1)} %bitcast.115), custom_call_target="tpu_custom_call" | custom-call | tf_op jit(solution)/shard_map/pallas_call | solution.py:279
  288.3 1.9 pad_maximum_fusion.1
  290.6 1.8 copy-done.15
  292.4 5.7 %convolution_convert_fusion.1 = bf16[1024,896]{1,0:T(8,128)(2,1)} fusion(bf16[2048,1024]{1,0:T(8,128)(2,1)S(1)} %bitcast.119, bf16[2048,896]{1,0:T(8,128)(2,1)S(1)} %bitcast.102), kind=kOutput, calls=%fused_computation.16 | convolution fusion | flops 3759013888 | bytes 9699328 | tf_op jit(solution)/shard_map/dot_general | solution.py:20
  298.9 5.9 %convolution_convert_fusion.2 = bf16[1024,896]{1,0:T(8,128)(2,1)} fusion(bf16[2048,1024]{1,0:T(8,128)(2,1)S(1)} %bitcast.120, bf16[2048,896]{1,0:T(8,128)(2,1)S(1)} %bitcast.101), kind=kOutput, calls=%fused_computation.17 | convolution fusion | flops 3759013888 | bytes 9699328 | tf_op jit(solution)/shard_map/dot_general | solution.py:20
  304.8 2.4 fusion.26
  307.2 2.4 convolution_add_fusion
  309.6 1.9 copy-done.2
  311.5 1.7 select_bitcast_fusion.refs_0_
  313.2 5.1 %shard_map.135 = f32[8,64,1024]{2,1,0:T(8,128)} custom-call(f32[8,64,1024]{2,1,0:T(8,128)} %select_bitcast_fusion.refs_0_), custom_call_target="tpu_custom_call" | custom-call | tf_op jit(solution)/shard_map/pallas_call | solution.py:279
  318.3 5.5 %fusion.20 = (bf16[8,64,1024]{2,1,0:T(8,128)(2,1)}, f32[8,64,1024]{2,1,0:T(8,128)}) fusion(f32[8,64,1024]{2,1,0:T(8,128)} %shard_map.135, f32[8,2,64,1024]{3,2,1,0:T(8,128)} %bitcast.95, pred[]{:T(512)S(6)} %eq.25), kind=kLoop, calls=%fused_computation.62 | loop fusion | flops 1572864 | bytes 9437185 | tf_op jit(solution)/shard_map/convert_element_type | solution.py:319
  323.8 20.1 %shard_map.136 = bf16[8,64,1024]{2,1,0:T(8,128)(2,1)} custom-call(bf16[8,64,1024]{2,1,0:T(8,128)(2,1)} %get-tuple-element.24.refs_0_), custom_call_target="tpu_custom_call" | custom-call | tf_op jit(solution)/shard_map/pallas_call | solution.py:279
  344.0 2.0 select_reduce_fusion.2
  346.0 1.1 bitcast_add_fusion.2
  347.8 9.3 %shard_map.137 = f32[8,1,128]{2,1,0:T(1,128)} custom-call(f32[1,128]{1,0:T(1,128)} %bitcast.118), custom_call_target="tpu_custom_call" | custom-call | tf_op jit(solution)/shard_map/pallas_call | solution.py:279
  (56 shorter events, 10.2 us)
Async XLA Ops:
  0.6 80.0 %copy-start = (bf16[896,1024]{1,0:T(8,128)(2,1)S(1)}, bf16[896,1024]{1,0:T(8,128)(2,1)}, u32[]{:S(2)}) copy-start(bf16[896,1024]{1,0:T(8,128)(2,1)} %param.19) | copy-start | bytes 5505028
  72.2 3.3 copy-start.16
  161.3 3.0 copy-start.5
  161.3 3.0 copy-start.6
  164.3 2.5 copy-start.11
  213.2 4.6 %copy-start.8 = (bf16[8,128,896]{2,1,0:T(8,128)(2,1)S(1)}, bf16[8,128,896]{2,1,0:T(8,128)(2,1)}, u32[]{:S(2)}) copy-start(bf16[8,128,896]{2,1,0:T(8,128)(2,1)} %get-tuple-element.16) | copy-start | bytes 5505028
  213.2 4.6 %copy-start.18 = (bf16[1024,896]{1,0:T(8,128)(2,1)S(1)}, bf16[1024,896]{1,0:T(8,128)(2,1)}, u32[]{:S(2)}) copy-start(bf16[1024,896]{1,0:T(8,128)(2,1)} %param.18) | copy-start | bytes 5505028
  220.2 1.9 copy-start.3
  290.2 2.2 copy-start.15
  292.4 5.7 %copy-start.7 = (bf16[8,128,896]{2,1,0:T(8,128)(2,1)S(1)}, bf16[8,128,896]{2,1,0:T(8,128)(2,1)}, u32[]{:S(2)}) copy-start(bf16[8,128,896]{2,1,0:T(8,128)(2,1)} %get-tuple-element.15) | copy-start | bytes 5505028
  292.4 5.7 %copy-start.10 = (bf16[8,128,896]{2,1,0:T(8,128)(2,1)S(1)}, bf16[8,128,896]{2,1,0:T(8,128)(2,1)}, u32[]{:S(2)}) copy-start(bf16[8,128,896]{2,1,0:T(8,128)(2,1)} %get-tuple-element.18) | copy-start | bytes 5505028
  298.8 5.9 %copy-start.17 = (bf16[1024,896]{1,0:T(8,128)(2,1)S(1)}, bf16[1024,896]{1,0:T(8,128)(2,1)}, u32[]{:S(2)}) copy-start(bf16[1024,896]{1,0:T(8,128)(2,1)} %param.17) | copy-start | bytes 5505028
  304.8 2.4 copy-start.9
  304.8 2.4 copy-start.19
  309.5 1.9 copy-start.2
  323.8 20.1 %copy-start.12 = (bf16[8,64,1024]{2,1,0:T(8,128)(2,1)S(1)}, bf16[8,64,1024]{2,1,0:T(8,128)(2,1)}, u32[]{:S(2)}) copy-start(bf16[8,64,1024]{2,1,0:T(8,128)(2,1)} %get-tuple-element.17) | copy-start | bytes 3145732
  343.9 3.1 copy-start.4
  344.0 3.1 copy-start.14
  344.0 13.8 %copy-start.13 = (bf16[128,1024]{1,0:T(8,128)(2,1)S(1)}, bf16[128,1024]{1,0:T(8,128)(2,1)}, u32[]{:S(2)}) copy-start(bf16[128,1024]{1,0:T(8,128)(2,1)} %refs_0_.1) | copy-start | bytes 786436
  344.0 14.7 %copy-start.1 = (bf16[896,1024]{1,0:T(8,128)(2,1)S(1)}, bf16[896,1024]{1,0:T(8,128)(2,1)}, u32[]{:S(2)}) copy-start(bf16[896,1024]{1,0:T(8,128)(2,1)} %param.19) | copy-start | bytes 5505028

commit v16 on v15

--- a/solution.py
+++ b/solution.py
@@ -137,7 +137,7 @@
             continue
         if mode == "pswap":
             c = pltpu.make_async_remote_copy(
-                ins[i], outs[i], send_sem.at[i, 0], recv_sem.at[i, me],
+                ins[i].at[:, 1 - me % 2], outs[i], send_sem.at[i, 0], recv_sem.at[i, me],
                 device_id=_dev(axis, me + 1 - 2 * (me % 2)),
                 device_id_type=pl.DeviceIdType.MESH,
             )
@@ -226,7 +226,7 @@
         if mode == "pswap":
             partner = me + 1 - 2 * (me % 2)
             pltpu.make_async_remote_copy(
-                ins[i], outs[i], send_sem.at[i, 0], recv_sem.at[i, partner],
+                outs[i], outs[i], send_sem.at[i, 0], recv_sem.at[i, partner],
                 device_id=_dev(axis, partner), device_id_type=pl.DeviceIdType.MESH,
             ).wait_recv()
             continue
@@ -267,7 +267,9 @@
         kmax = max(kmax, k)
         if mode in ("gather", "rgather"):
             out_shapes.append(jax.ShapeDtypeStruct((k,) + x.shape, x.dtype))
-        elif mode in ("pswap", "pscatter"):
+        elif mode == "pswap":
+            out_shapes.append(jax.ShapeDtypeStruct((x.shape[0],) + x.shape[2:], x.dtype))
+        elif mode == "pscatter":
             out_shapes.append(jax.ShapeDtypeStruct(x.shape, x.dtype))
         elif mode in ("pgather", "prgather"):
             out_shapes.append(jax.ShapeDtypeStruct((2, k // 2) + x.shape, x.dtype))
@@ -312,10 +314,8 @@
     p = me % 2
     m = parts.shape[0] // k
     quad = parts.reshape((k // 2, 2, m) + parts.shape[1:])
-    mine_half = jnp.where(p == 0, quad[:, 0], quad[:, 1])
-    theirs_half = jnp.where(p == 0, quad[:, 1], quad[:, 0])
-    (got,) = exchange([(theirs_half, axis, "pswap")], cid)
-    pair = mine_half + got
+    (got,) = exchange([(quad, axis, "pswap")], cid)
+    pair = lax.dynamic_index_in_dim(quad, p, axis=1, keepdims=False) + got
     outs = exchange([(pair.astype(WIRE), axis, "pscatter")] + list(extra), cid + 1)
     slots = outs[0]
     own = lax.dynamic_index_in_dim(pair, me // 2, axis=0, keepdims=False)

time: 359 us -> 354 us (0.986)
  other arithmetic: 35.7 us -> 30.3 us
  local copies, waits for them, and re-layouts: 11.4 us -> 7.54 us
  matrix products: 35.5 us -> 39.2 us
    dot_general x5, matrix products: 18.8 us -> 22.7 us  [over_width(): lax.dot_general(left, right, (((1,), (1,)), ((), ())), preferred_element_...]
    unnamed x40 -> x36, local copies, waits for them, and re-layouts: 6.21 us -> 2.34 us
where the time goes in v16:
time: 354 us; the launch traced here: 353 us
  Pallas kernels  275 us (78%)
  matrix products  39.2 us (11%)
  other arithmetic  30.3 us (9%)
  local copies, waits for them, and re-layouts  7.54 us (2%)
    pallas_call x9, Pallas kernels, exchange(): pl.pallas_call(functools.partial(_exchange_kernel, modes, axes), out_shap...  275 us
    dot_general x5, matrix products, over_width(): lax.dot_general(left, right, (((1,), (1,)), ((), ())), preferred_element_...  22.7 us
    dot_general x3, matrix products, over_tokens(): lax.dot_general(left, right, (((0,), (0,)), ((), ())), preferred_element_...  16.5 us
    convert_element_type x2, other arithmetic, pair_reduce_scatter(): pair.astype(WIRE)  9.35 us

profile of v16, /device:TPU:64, one launch (start us, length us, event | category | flops | bytes accessed | tf_op | source)
XLA Modules:
  0.0 353.3 jit_solution(16832599816460641671)
XLA Ops:
  0.7 0.9 convert_reduce_fusion
  1.6 1.1 fusion.12
  3.3 7.8 %shard_map.129 = f32[8,1,144]{2,1,0:T(1,128)} custom-call(f32[1,144]{1,0:T(1,128)} %bitcast.85), custom_call_target="tpu_custom_call" | custom-call | tf_op jit(solution)/shard_map/pallas_call | solution.py:281
  12.6 1.8 fusion.14.refs_1_
  14.4 2.6 fusion.2.refs_1_
  17.0 55.2 %shard_map.130 = (bf16[2,8,128,1024]{3,2,1,0:T(8,128)(2,1)}, bf16[8,256,896]{2,1,0:T(8,128)(2,1)}) custom-call(bf16[128,1024]{1,0:T(8,128)(2,1)} %refs_0_.1, bf16[256,896]{1,0:T(8,128)(2,1)} %fusion.2.refs_1_), custom_call_target="tpu_custom_call" | custom-call | tf_op jit(solution)/shard_map/pallas_call | solution.py:281
  72.2 2.8 copy.27
  75.5 5.1 %convolution_convert_fusion = bf16[896,1024]{1,0:T(8,128)(2,1)} fusion(bf16[2048,896]{1,0:T(8,128)(2,1)S(1)} %bitcast.89, bf16[2048,1024]{1,0:T(8,128)(2,1)S(1)} %bitcast.66), kind=kOutput, calls=%fused_computation.9 | convolution fusion | flops 3759013888 | bytes 9699328 | tf_op jit(solution)/shard_map/dot_general | solution.py:20
  80.6 7.2 %fusion.24 = (bf16[2048,896]{1,0:T(8,128)(2,1)}, f32[2048,896]{1,0:T(8,128)}) fusion(bf16[2048,1024]{1,0:T(8,128)(2,1)S(1)} %bitcast.67, bf16[896,1024]{1,0:T(8,128)(2,1)S(1)} %copy-done), kind=kOutput, calls=%fused_computation.60 | convolution fusion | flops 3759931392 | bytes 17039360 | tf_op jit(solution)/shard_map/dot_general | solution.py:26
  87.8 73.5 %shard_map.131 = (bf16[8,256,896]{2,1,0:T(8,128)(2,1)}, bf16[2,8,128,1024]{3,2,1,0:T(8,128)(2,1)}) custom-call(bf16[2048,896]{1,0:T(8,128)(2,1)} %get-tuple-element.34.refs_0_, bf16[128,1024]{1,0:T(8,128)(2,1)} %fusion.14.refs_1_), custom_call_target="tpu_custom_call" | custom-call | tf_op jit(solution)/shard_map/pallas_call | solution.py:281
  161.3 2.9 select_reduce_fusion
  164.3 1.7 fusion.11
  166.0 0.8 fusion.22
  168.0 45.1 %shard_map.132 = (bf16[8,128,896]{2,1,0:T(8,128)(2,1)}, bf16[8,128,896]{2,1,0:T(8,128)(2,1)}) custom-call(bf16[128,896]{1,0:T(8,128)(2,1)} %bitcast.82, bf16[128,896]{1,0:T(8,128)(2,1)} %bitcast.81), custom_call_target="tpu_custom_call" | custom-call | tf_op jit(solution)/shard_map/pallas_call | solution.py:281
  213.1 4.6 %fusion.25 = f32[1024,1024]{1,0:T(8,128)S(1)} fusion(bf16[1024,896]{1,0:T(8,128)(2,1)} %bitcast.71, bf16[1024,896]{1,0:T(8,128)(2,1)} %param.17), kind=kOutput, calls=%fused_computation.61 | convolution fusion | flops 1879048192 | bytes 7864320 | tf_op jit(solution)/shard_map/dot_general | solution.py:26
  217.7 4.3 %convolution_add_fusion.1 = f32[1024,1024]{1,0:T(8,128)} fusion(f32[1024,1024]{1,0:T(8,128)S(1)} %fusion.25, bf16[1024,896]{1,0:T(8,128)(2,1)S(1)} %bitcast.73, bf16[1024,896]{1,0:T(8,128)(2,1)S(1)} %copy-done.16), kind=kOutput, calls=%fused_computation.8 | convolution fusion | flops 1880096768 | bytes 12058624 | tf_op jit(solution)/shard_map/dot_general | solution.py:26
  222.0 5.1 %shard_map.133 = f32[8,64,1024]{2,1,0:T(8,128)} custom-call(f32[8,2,64,1024]{3,2,1,0:T(8,128)} %bitcast.64), custom_call_target="tpu_custom_call" | custom-call | tf_op jit(solution)/shard_map/pallas_call | solution.py:281
  227.1 4.6 %fusion.21 = (bf16[8,64,1024]{2,1,0:T(8,128)(2,1)}, f32[8,64,1024]{2,1,0:T(8,128)}) fusion(f32[8,64,1024]{2,1,0:T(8,128)} %shard_map.133, f32[8,2,64,1024]{3,2,1,0:T(8,128)} %bitcast.65, s32[]{:T(128)S(6)} %select_n.43), kind=kLoop, calls=%fused_computation.57 | loop fusion | flops 1048576 | bytes 7340036 | tf_op jit(solution)/shard_map/convert_element_type | solution.py:319
  231.7 53.9 %shard_map.134 = (bf16[8,64,1024]{2,1,0:T(8,128)(2,1)}, bf16[8,128,896]{2,1,0:T(8,128)(2,1)}, bf16[8,128,896]{2,1,0:T(8,128)(2,1)}) custom-call(bf16[8,64,1024]{2,1,0:T(8,128)(2,1)} %get-tuple-element.26.refs_0_, bf16[128,896]{1,0:T(8,128)(2,1)} %bitcast.84, bf16[128,896]{1,0:T(8,128)(2,1)} %bitcast.83), custom_call_target="tpu_custom_call" | custom-call | tf_op jit(solution)/shard_map/pallas_call | solution.py:281
  285.7 1.9 pad_maximum_fusion.1
  287.9 1.8 copy-done.13
  289.7 5.7 %convolution_convert_fusion.1 = bf16[1024,896]{1,0:T(8,128)(2,1)} fusion(bf16[2048,1024]{1,0:T(8,128)(2,1)S(1)} %bitcast.87, bf16[2048,896]{1,0:T(8,128)(2,1)S(1)} %bitcast.70), kind=kOutput, calls=%fused_computation.10 | convolution fusion | flops 3759013888 | bytes 9699328 | tf_op jit(solution)/shard_map/dot_general | solution.py:20
  296.2 5.7 %convolution_convert_fusion.2 = bf16[1024,896]{1,0:T(8,128)(2,1)} fusion(bf16[2048,1024]{1,0:T(8,128)(2,1)S(1)} %bitcast.88, bf16[2048,896]{1,0:T(8,128)(2,1)S(1)} %bitcast.69), kind=kOutput, calls=%fused_computation.11 | convolution fusion | flops 3759013888 | bytes 9699328 | tf_op jit(solution)/shard_map/dot_general | solution.py:20
  301.9 2.4 fusion.26
  304.3 4.4 %convolution_add_fusion = f32[1024,1024]{1,0:T(8,128)} fusion(f32[1024,1024]{1,0:T(8,128)S(1)} %fusion.26, bf16[1024,896]{1,0:T(8,128)(2,1)S(1)} %bitcast.76, bf16[1024,896]{1,0:T(8,128)(2,1)S(1)} %copy-done.17), kind=kOutput, calls=%fused_computation.7 | convolution fusion | flops 1880096768 | bytes 12058624 | tf_op jit(solution)/shard_map/dot_general | solution.py:26
  308.7 5.1 %shard_map.135 = f32[8,64,1024]{2,1,0:T(8,128)} custom-call(f32[8,2,64,1024]{3,2,1,0:T(8,128)} %bitcast.62), custom_call_target="tpu_custom_call" | custom-call | tf_op jit(solution)/shard_map/pallas_call | solution.py:281
  313.8 4.7 %fusion.20 = (bf16[8,64,1024]{2,1,0:T(8,128)(2,1)}, f32[8,64,1024]{2,1,0:T(8,128)}) fusion(f32[8,64,1024]{2,1,0:T(8,128)} %shard_map.135, f32[8,2,64,1024]{3,2,1,0:T(8,128)} %bitcast.63, s32[]{:T(128)S(6)} %select_n.43), kind=kLoop, calls=%fused_computation.56 | loop fusion | flops 1048576 | bytes 7340036 | tf_op jit(solution)/shard_map/convert_element_type | solution.py:319
  318.5 20.2 %shard_map.136 = bf16[8,64,1024]{2,1,0:T(8,128)(2,1)} custom-call(bf16[8,64,1024]{2,1,0:T(8,128)(2,1)} %get-tuple-element.24.refs_0_), custom_call_target="tpu_custom_call" | custom-call | tf_op jit(solution)/shard_map/pallas_call | solution.py:281
  338.7 1.8 select_reduce_fusion.2
  340.6 1.1 bitcast_add_fusion.2
  342.3 9.2 %shard_map.137 = f32[8,1,128]{2,1,0:T(1,128)} custom-call(f32[1,128]{1,0:T(1,128)} %bitcast.86), custom_call_target="tpu_custom_call" | custom-call | tf_op jit(solution)/shard_map/pallas_call | solution.py:281
  352.3 0.9 fusion.19
  (50 shorter events, 6.4 us)
Async XLA Ops:
  0.6 80.0 %copy-start = (bf16[896,1024]{1,0:T(8,128)(2,1)S(1)}, bf16[896,1024]{1,0:T(8,128)(2,1)}, u32[]{:S(2)}) copy-start(bf16[896,1024]{1,0:T(8,128)(2,1)} %param.19) | copy-start | bytes 5505028
  72.2 3.3 copy-start.14
  87.8 76.5 %copy-start.3 = (bf16[256,896]{1,0:T(8,128)(2,1)S(1)}, bf16[256,896]{1,0:T(8,128)(2,1)}, u32[]{:S(2)}) copy-start(bf16[256,896]{1,0:T(8,128)(2,1)} %param.12) | copy-start | bytes 1376260
  87.8 76.5 %copy-start.4 = (s32[256,896]{1,0:T(8,128)S(1)}, s32[256,896]{1,0:T(8,128)}, u32[]{:S(2)}) copy-start(s32[256,896]{1,0:T(8,128)} %param.14) | copy-start | bytes 2752516
  164.3 2.5 copy-start.9
  213.1 4.6 %copy-start.6 = (bf16[8,128,896]{2,1,0:T(8,128)(2,1)S(1)}, bf16[8,128,896]{2,1,0:T(8,128)(2,1)}, u32[]{:S(2)}) copy-start(bf16[8,128,896]{2,1,0:T(8,128)(2,1)} %get-tuple-element.16) | copy-start | bytes 5505028
  213.1 4.6 %copy-start.16 = (bf16[1024,896]{1,0:T(8,128)(2,1)S(1)}, bf16[1024,896]{1,0:T(8,128)(2,1)}, u32[]{:S(2)}) copy-start(bf16[1024,896]{1,0:T(8,128)(2,1)} %param.18) | copy-start | bytes 5505028
  287.5 2.2 copy-start.13
  289.7 5.7 %copy-start.5 = (bf16[8,128,896]{2,1,0:T(8,128)(2,1)S(1)}, bf16[8,128,896]{2,1,0:T(8,128)(2,1)}, u32[]{:S(2)}) copy-start(bf16[8,128,896]{2,1,0:T(8,128)(2,1)} %get-tuple-element.15) | copy-start | bytes 5505028
  289.7 5.7 %copy-start.8 = (bf16[8,128,896]{2,1,0:T(8,128)(2,1)S(1)}, bf16[8,128,896]{2,1,0:T(8,128)(2,1)}, u32[]{:S(2)}) copy-start(bf16[8,128,896]{2,1,0:T(8,128)(2,1)} %get-tuple-element.18) | copy-start | bytes 5505028
  296.2 5.7 %copy-start.15 = (bf16[1024,896]{1,0:T(8,128)(2,1)S(1)}, bf16[1024,896]{1,0:T(8,128)(2,1)}, u32[]{:S(2)}) copy-start(bf16[1024,896]{1,0:T(8,128)(2,1)} %param.17) | copy-start | bytes 5505028
  301.9 2.4 copy-start.7
  301.9 2.4 copy-start.17
  313.7 25.0 %copy-start.10 = (bf16[8,64,1024]{2,1,0:T(8,128)(2,1)S(1)}, bf16[8,64,1024]{2,1,0:T(8,128)(2,1)}, u32[]{:S(2)}) copy-start(bf16[8,64,1024]{2,1,0:T(8,128)(2,1)} %get-tuple-element.17) | copy-start | bytes 3145732
  318.5 23.2 %copy-start.2 = (bf16[128,1024]{1,0:T(8,128)(2,1)S(1)}, bf16[128,1024]{1,0:T(8,128)(2,1)}, u32[]{:S(2)}) copy-start(bf16[128,1024]{1,0:T(8,128)(2,1)} %param.10) | copy-start | bytes 786436
  318.5 23.2 %copy-start.12 = (f32[1024]{0:T(1024)S(1)}, f32[1024]{0:T(1024)}, u32[]{:S(2)}) copy-start(f32[1024]{0:T(1024)} %param.16) | copy-start | bytes 12292
  318.5 33.8 %copy-start.11 = (bf16[128,1024]{1,0:T(8,128)(2,1)S(1)}, bf16[128,1024]{1,0:T(8,128)(2,1)}, u32[]{:S(2)}) copy-start(bf16[128,1024]{1,0:T(8,128)(2,1)} %refs_0_.1) | copy-start | bytes 786436
  318.5 34.8 %copy-start.1 = (bf16[896,1024]{1,0:T(8,128)(2,1)S(1)}, bf16[896,1024]{1,0:T(8,128)(2,1)}, u32[]{:S(2)}) copy-start(bf16[896,1024]{1,0:T(8,128)(2,1)} %param.19) | copy-start | bytes 5505028

commit v17 on v16

--- a/solution.py
+++ b/solution.py
@@ -54,17 +54,19 @@
     pl.semaphore_wait(barrier, count)
 
 
-def _ring_pair_send(i, src_ref, slot, dev, me_g, ng, send_sem, recv_sem, sends, axis):
+def _ring_pair_send(i, src_ref, slot, dev, me_g, ng, send_sem, recv_sem, sends, axis, part):
     ny = ng // 2
     ym, zm = me_g // 2, me_g % 2
     direct = [ym * 2 + 1 - zm] + [((ym + dy) % ny) * 2 + z for dy in (1, ny - 1) for z in (0, 1)]
-    for d, tgt in enumerate(direct):
-        c = pltpu.make_async_remote_copy(
-            src_ref, slot(me_g), send_sem.at[i, d], recv_sem.at[i, me_g],
-            device_id=_dev(axis, dev(tgt)), device_id_type=pl.DeviceIdType.MESH,
-        )
-        c.start()
-        sends.append(c)
+    if part == "direct":
+        for d, tgt in enumerate(direct):
+            c = pltpu.make_async_remote_copy(
+                src_ref, slot(me_g), send_sem.at[i, d], recv_sem.at[i, me_g],
+                device_id=_dev(axis, dev(tgt)), device_id_type=pl.DeviceIdType.MESH,
+            )
+            c.start()
+            sends.append(c)
+        return
     h = src_ref.shape[0] // 2
     for e, (dy, lo, off) in enumerate([(ny - 1, 0, 0), (1, h, ng)]):
         for z in (0, 1):
@@ -107,7 +109,7 @@
     ins, outs = refs[:n], refs[n:2 * n]
     send_sem, recv_sem, local_sem = refs[2 * n:]
     _barrier(modes, axes)
-    sends, relays = [], []
+    sends, relays, locals_ = [], [], {}
     for i, (mode, axis) in enumerate(zip(modes, axes)):
         k = lax.axis_size(axis)
         me = lax.axis_index(axis)
@@ -116,24 +118,15 @@
             loc.start()
             sends.append(loc)
             _ring_pair_send(i, ins[i], lambda g: outs[i].at[g], lambda g: g, me, k,
-                            send_sem, recv_sem, sends, axis)
+                            send_sem, recv_sem, sends, axis, "direct")
             continue
         if mode == "prgather":
             p = me % 2
-            partner = me + 1 - 2 * p
-            slot = lambda g: outs[i].at[p, g]
-            dev = lambda g: g * 2 + p
-            loc = pltpu.make_async_copy(ins[i], slot(me // 2), local_sem.at[i])
+            loc = pltpu.make_async_copy(ins[i], outs[i].at[p, me // 2], local_sem.at[i])
             loc.start()
-            _ring_pair_send(i, ins[i], slot, dev, me // 2, k // 2, send_sem, recv_sem, sends, axis)
-            _ring_pair_wait(i, ins[i], slot, dev, me // 2, k // 2, send_sem, recv_sem, axis)
-            loc.wait()
-            c = pltpu.make_async_remote_copy(
-                outs[i].at[p], outs[i].at[p], send_sem.at[i, 2 * k - 1], recv_sem.at[i, 2 * k - 1],
-                device_id=_dev(axis, partner), device_id_type=pl.DeviceIdType.MESH,
-            )
-            c.start()
-            sends.append(c)
+            locals_[i] = loc
+            _ring_pair_send(i, ins[i], lambda g: outs[i].at[p, g], lambda g: g * 2 + p,
+                            me // 2, k // 2, send_sem, recv_sem, sends, axis, "direct")
             continue
         if mode == "pswap":
             c = pltpu.make_async_remote_copy(
@@ -183,6 +176,32 @@
             loc = pltpu.make_async_copy(ins[i], outs[i].at[me], local_sem.at[i])
             loc.start()
             sends.append(loc)
+    for i, (mode, axis) in enumerate(zip(modes, axes)):
+        k = lax.axis_size(axis)
+        me = lax.axis_index(axis)
+        if mode == "rgather":
+            _ring_pair_send(i, ins[i], lambda g: outs[i].at[g], lambda g: g, me, k,
+                            send_sem, recv_sem, sends, axis, "relay")
+        elif mode == "prgather":
+            p = me % 2
+            _ring_pair_send(i, ins[i], lambda g: outs[i].at[p, g], lambda g: g * 2 + p,
+                            me // 2, k // 2, send_sem, recv_sem, sends, axis, "relay")
+    for i, (mode, axis) in enumerate(zip(modes, axes)):
+        if mode != "prgather":
+            continue
+        k = lax.axis_size(axis)
+        me = lax.axis_index(axis)
+        p = me % 2
+        partner = me + 1 - 2 * p
+        _ring_pair_wait(i, ins[i], lambda g: outs[i].at[p, g], lambda g: g * 2 + p,
+                        me // 2, k // 2, send_sem, recv_sem, axis)
+        locals_[i].wait()
+        c = pltpu.make_async_remote_copy(
+            outs[i].at[p], outs[i].at[p], send_sem.at[i, 2 * k - 1], recv_sem.at[i, 2 * k - 1],
+            device_id=_dev(axis, partner), device_id_type=pl.DeviceIdType.MESH,
+        )
+        c.start()
+        sends.append(c)
     for i, loc in relays:
         axis = axes[i]
         k = lax.axis_size(axis)

time: 354 us -> 340 us (0.960)
  Pallas kernels: 275 us -> 262 us
    pallas_call x9, Pallas kernels: 275 us -> 262 us  [exchange(): pl.pallas_call(functools.partial(_exchange_kernel, modes, axes), out_shap...]
where the time goes in v17:
time: 340 us
  Pallas kernels  262 us (77%)
  matrix products  39.2 us (12%)
  other arithmetic  30.3 us (9%)
  local copies, waits for them, and re-layouts  7.54 us (2%)
    pallas_call x9, Pallas kernels, exchange(): pl.pallas_call(functools.partial(_exchange_kernel, modes, axes), out_shap...  262 us
    dot_general x5, matrix products, over_width(): lax.dot_general(left, right, (((1,), (1,)), ((), ())), preferred_element_...  22.7 us
    dot_general x3, matrix products, over_tokens(): lax.dot_general(left, right, (((0,), (0,)), ((), ())), preferred_element_...  16.5 us
    convert_element_type x2, other arithmetic, pair_reduce_scatter(): pair.astype(WIRE)  9.35 us

profile of v17, /device:TPU:64, one launch (start us, length us, event | category | flops | bytes accessed | tf_op | source)
XLA Modules:
  0.0 339.8 jit_solution(784027827823472599)
XLA Ops:
  0.7 0.9 convert_reduce_fusion
  1.6 1.1 fusion.12
  3.3 7.8 %shard_map.129 = f32[8,1,144]{2,1,0:T(1,128)} custom-call(f32[1,144]{1,0:T(1,128)} %bitcast.85), custom_call_target="tpu_custom_call" | custom-call | tf_op jit(solution)/shard_map/pallas_call | solution.py:300
  12.6 1.8 fusion.14.refs_1_
  14.4 2.6 fusion.2.refs_1_
  17.0 51.6 %shard_map.130 = (bf16[2,8,128,1024]{3,2,1,0:T(8,128)(2,1)}, bf16[8,256,896]{2,1,0:T(8,128)(2,1)}) custom-call(bf16[128,1024]{1,0:T(8,128)(2,1)} %refs_0_.1, bf16[256,896]{1,0:T(8,128)(2,1)} %fusion.2.refs_1_), custom_call_target="tpu_custom_call" | custom-call | tf_op jit(solution)/shard_map/pallas_call | solution.py:300
  68.6 2.8 copy.27
  71.9 5.1 %convolution_convert_fusion = bf16[896,1024]{1,0:T(8,128)(2,1)} fusion(bf16[2048,896]{1,0:T(8,128)(2,1)S(1)} %bitcast.89, bf16[2048,1024]{1,0:T(8,128)(2,1)S(1)} %bitcast.66), kind=kOutput, calls=%fused_computation.9 | convolution fusion | flops 3759013888 | bytes 9699328 | tf_op jit(solution)/shard_map/dot_general | solution.py:20
  77.0 7.2 %fusion.24 = (bf16[2048,896]{1,0:T(8,128)(2,1)}, f32[2048,896]{1,0:T(8,128)}) fusion(bf16[2048,1024]{1,0:T(8,128)(2,1)S(1)} %bitcast.67, bf16[896,1024]{1,0:T(8,128)(2,1)S(1)} %copy-done), kind=kOutput, calls=%fused_computation.60 | convolution fusion | flops 3759931392 | bytes 17039360 | tf_op jit(solution)/shard_map/dot_general | solution.py:26
  84.2 68.8 %shard_map.131 = (bf16[8,256,896]{2,1,0:T(8,128)(2,1)}, bf16[2,8,128,1024]{3,2,1,0:T(8,128)(2,1)}) custom-call(bf16[2048,896]{1,0:T(8,128)(2,1)} %get-tuple-element.34.refs_0_, bf16[128,1024]{1,0:T(8,128)(2,1)} %fusion.14.refs_1_), custom_call_target="tpu_custom_call" | custom-call | tf_op jit(solution)/shard_map/pallas_call | solution.py:300
  153.0 2.9 select_reduce_fusion
  155.9 1.7 fusion.11
  157.6 0.8 fusion.22
  159.6 41.0 %shard_map.132 = (bf16[8,128,896]{2,1,0:T(8,128)(2,1)}, bf16[8,128,896]{2,1,0:T(8,128)(2,1)}) custom-call(bf16[128,896]{1,0:T(8,128)(2,1)} %bitcast.82, bf16[128,896]{1,0:T(8,128)(2,1)} %bitcast.81), custom_call_target="tpu_custom_call" | custom-call | tf_op jit(solution)/shard_map/pallas_call | solution.py:300
  200.7 4.6 %fusion.25 = f32[1024,1024]{1,0:T(8,128)S(1)} fusion(bf16[1024,896]{1,0:T(8,128)(2,1)} %bitcast.71, bf16[1024,896]{1,0:T(8,128)(2,1)} %param.17), kind=kOutput, calls=%fused_computation.61 | convolution fusion | flops 1879048192 | bytes 7864320 | tf_op jit(solution)/shard_map/dot_general | solution.py:26
  205.3 4.3 %convolution_add_fusion.1 = f32[1024,1024]{1,0:T(8,128)} fusion(f32[1024,1024]{1,0:T(8,128)S(1)} %fusion.25, bf16[1024,896]{1,0:T(8,128)(2,1)S(1)} %bitcast.73, bf16[1024,896]{1,0:T(8,128)(2,1)S(1)} %copy-done.16), kind=kOutput, calls=%fused_computation.8 | convolution fusion | flops 1880096768 | bytes 12058624 | tf_op jit(solution)/shard_map/dot_general | solution.py:26
  209.6 5.1 %shard_map.133 = f32[8,64,1024]{2,1,0:T(8,128)} custom-call(f32[8,2,64,1024]{3,2,1,0:T(8,128)} %bitcast.64), custom_call_target="tpu_custom_call" | custom-call | tf_op jit(solution)/shard_map/pallas_call | solution.py:300
  214.7 4.6 %fusion.21 = (bf16[8,64,1024]{2,1,0:T(8,128)(2,1)}, f32[8,64,1024]{2,1,0:T(8,128)}) fusion(f32[8,64,1024]{2,1,0:T(8,128)} %shard_map.133, f32[8,2,64,1024]{3,2,1,0:T(8,128)} %bitcast.65, s32[]{:T(128)S(6)} %select_n.43), kind=kLoop, calls=%fused_computation.57 | loop fusion | flops 1048576 | bytes 7340036 | tf_op jit(solution)/shard_map/convert_element_type | solution.py:338
  219.3 52.8 %shard_map.134 = (bf16[8,64,1024]{2,1,0:T(8,128)(2,1)}, bf16[8,128,896]{2,1,0:T(8,128)(2,1)}, bf16[8,128,896]{2,1,0:T(8,128)(2,1)}) custom-call(bf16[8,64,1024]{2,1,0:T(8,128)(2,1)} %get-tuple-element.26.refs_0_, bf16[128,896]{1,0:T(8,128)(2,1)} %bitcast.84, bf16[128,896]{1,0:T(8,128)(2,1)} %bitcast.83), custom_call_target="tpu_custom_call" | custom-call | tf_op jit(solution)/shard_map/pallas_call | solution.py:300
  272.0 1.9 pad_maximum_fusion.1
  274.3 1.8 copy-done.13
  276.1 5.7 %convolution_convert_fusion.1 = bf16[1024,896]{1,0:T(8,128)(2,1)} fusion(bf16[2048,1024]{1,0:T(8,128)(2,1)S(1)} %bitcast.87, bf16[2048,896]{1,0:T(8,128)(2,1)S(1)} %bitcast.70), kind=kOutput, calls=%fused_computation.10 | convolution fusion | flops 3759013888 | bytes 9699328 | tf_op jit(solution)/shard_map/dot_general | solution.py:20
  282.6 5.7 %convolution_convert_fusion.2 = bf16[1024,896]{1,0:T(8,128)(2,1)} fusion(bf16[2048,1024]{1,0:T(8,128)(2,1)S(1)} %bitcast.88, bf16[2048,896]{1,0:T(8,128)(2,1)S(1)} %bitcast.69), kind=kOutput, calls=%fused_computation.11 | convolution fusion | flops 3759013888 | bytes 9699328 | tf_op jit(solution)/shard_map/dot_general | solution.py:20
  288.3 2.4 fusion.26
  290.7 4.3 %convolution_add_fusion = f32[1024,1024]{1,0:T(8,128)} fusion(f32[1024,1024]{1,0:T(8,128)S(1)} %fusion.26, bf16[1024,896]{1,0:T(8,128)(2,1)S(1)} %bitcast.76, bf16[1024,896]{1,0:T(8,128)(2,1)S(1)} %copy-done.17), kind=kOutput, calls=%fused_computation.7 | convolution fusion | flops 1880096768 | bytes 12058624 | tf_op jit(solution)/shard_map/dot_general | solution.py:26
  295.0 5.1 %shard_map.135 = f32[8,64,1024]{2,1,0:T(8,128)} custom-call(f32[8,2,64,1024]{3,2,1,0:T(8,128)} %bitcast.62), custom_call_target="tpu_custom_call" | custom-call | tf_op jit(solution)/shard_map/pallas_call | solution.py:300
  300.1 4.7 %fusion.20 = (bf16[8,64,1024]{2,1,0:T(8,128)(2,1)}, f32[8,64,1024]{2,1,0:T(8,128)}) fusion(f32[8,64,1024]{2,1,0:T(8,128)} %shard_map.135, f32[8,2,64,1024]{3,2,1,0:T(8,128)} %bitcast.63, s32[]{:T(128)S(6)} %select_n.43), kind=kLoop, calls=%fused_computation.56 | loop fusion | flops 1048576 | bytes 7340036 | tf_op jit(solution)/shard_map/convert_element_type | solution.py:338
  304.9 20.3 %shard_map.136 = bf16[8,64,1024]{2,1,0:T(8,128)(2,1)} custom-call(bf16[8,64,1024]{2,1,0:T(8,128)(2,1)} %get-tuple-element.24.refs_0_), custom_call_target="tpu_custom_call" | custom-call | tf_op jit(solution)/shard_map/pallas_call | solution.py:300
  325.2 1.8 select_reduce_fusion.2
  327.1 1.1 bitcast_add_fusion.2
  328.9 9.3 %shard_map.137 = f32[8,1,128]{2,1,0:T(1,128)} custom-call(f32[1,128]{1,0:T(1,128)} %bitcast.86), custom_call_target="tpu_custom_call" | custom-call | tf_op jit(solution)/shard_map/pallas_call | solution.py:300
  338.9 0.9 fusion.19
  (50 shorter events, 6.4 us)
Async XLA Ops:
  0.6 76.4 %copy-start = (bf16[896,1024]{1,0:T(8,128)(2,1)S(1)}, bf16[896,1024]{1,0:T(8,128)(2,1)}, u32[]{:S(2)}) copy-start(bf16[896,1024]{1,0:T(8,128)(2,1)} %param.19) | copy-start | bytes 5505028
  68.6 3.3 copy-start.14
  84.2 71.7 %copy-start.3 = (bf16[256,896]{1,0:T(8,128)(2,1)S(1)}, bf16[256,896]{1,0:T(8,128)(2,1)}, u32[]{:S(2)}) copy-start(bf16[256,896]{1,0:T(8,128)(2,1)} %param.12) | copy-start | bytes 1376260
  84.2 71.7 %copy-start.4 = (s32[256,896]{1,0:T(8,128)S(1)}, s32[256,896]{1,0:T(8,128)}, u32[]{:S(2)}) copy-start(s32[256,896]{1,0:T(8,128)} %param.14) | copy-start | bytes 2752516
  155.9 2.5 copy-start.9
  200.7 4.6 %copy-start.6 = (bf16[8,128,896]{2,1,0:T(8,128)(2,1)S(1)}, bf16[8,128,896]{2,1,0:T(8,128)(2,1)}, u32[]{:S(2)}) copy-start(bf16[8,128,896]{2,1,0:T(8,128)(2,1)} %get-tuple-element.16) | copy-start | bytes 5505028
  200.7 4.6 %copy-start.16 = (bf16[1024,896]{1,0:T(8,128)(2,1)S(1)}, bf16[1024,896]{1,0:T(8,128)(2,1)}, u32[]{:S(2)}) copy-start(bf16[1024,896]{1,0:T(8,128)(2,1)} %param.18) | copy-start | bytes 5505028
  273.9 2.2 copy-start.13
  276.1 5.7 %copy-start.5 = (bf16[8,128,896]{2,1,0:T(8,128)(2,1)S(1)}, bf16[8,128,896]{2,1,0:T(8,128)(2,1)}, u32[]{:S(2)}) copy-start(bf16[8,128,896]{2,1,0:T(8,128)(2,1)} %get-tuple-element.15) | copy-start | bytes 5505028
  276.1 5.7 %copy-start.8 = (bf16[8,128,896]{2,1,0:T(8,128)(2,1)S(1)}, bf16[8,128,896]{2,1,0:T(8,128)(2,1)}, u32[]{:S(2)}) copy-start(bf16[8,128,896]{2,1,0:T(8,128)(2,1)} %get-tuple-element.18) | copy-start | bytes 5505028
  282.6 5.7 %copy-start.15 = (bf16[1024,896]{1,0:T(8,128)(2,1)S(1)}, bf16[1024,896]{1,0:T(8,128)(2,1)}, u32[]{:S(2)}) copy-start(bf16[1024,896]{1,0:T(8,128)(2,1)} %param.17) | copy-start | bytes 5505028
  288.3 2.4 copy-start.7
  288.3 2.4 copy-start.17
  300.1 25.1 %copy-start.10 = (bf16[8,64,1024]{2,1,0:T(8,128)(2,1)S(1)}, bf16[8,64,1024]{2,1,0:T(8,128)(2,1)}, u32[]{:S(2)}) copy-start(bf16[8,64,1024]{2,1,0:T(8,128)(2,1)} %get-tuple-element.17) | copy-start | bytes 3145732
  304.9 23.3 %copy-start.2 = (bf16[128,1024]{1,0:T(8,128)(2,1)S(1)}, bf16[128,1024]{1,0:T(8,128)(2,1)}, u32[]{:S(2)}) copy-start(bf16[128,1024]{1,0:T(8,128)(2,1)} %param.10) | copy-start | bytes 786436
  304.9 23.3 %copy-start.12 = (f32[1024]{0:T(1024)S(1)}, f32[1024]{0:T(1024)}, u32[]{:S(2)}) copy-start(f32[1024]{0:T(1024)} %param.16) | copy-start | bytes 12292
  304.9 34.0 %copy-start.11 = (bf16[128,1024]{1,0:T(8,128)(2,1)S(1)}, bf16[128,1024]{1,0:T(8,128)(2,1)}, u32[]{:S(2)}) copy-start(bf16[128,1024]{1,0:T(8,128)(2,1)} %refs_0_.1) | copy-start | bytes 786436
  304.9 34.9 %copy-start.1 = (bf16[896,1024]{1,0:T(8,128)(2,1)S(1)}, bf16[896,1024]{1,0:T(8,128)(2,1)}, u32[]{:S(2)}) copy-start(bf16[896,1024]{1,0:T(8,128)(2,1)} %param.19) | copy-start | bytes 5505028

commit v18 on v17

--- a/solution.py
+++ b/solution.py
@@ -394,15 +394,13 @@
 
     gpre_a, gpre_b = split(grad_gpre)
     upre_a, upre_b = split(grad_upre)
-    ga_full, ua_full = exchange([(gpre_a, "row", RG), (upre_a, "row", RG)], 3)
-    ga_full = ga_full.reshape(total // 2, ff_loc)
-    ua_full = ua_full.reshape(total // 2, ff_loc)
+    (gu_a,) = exchange([(jnp.stack([gpre_a, upre_a]), "row", RG)], 3)
+    ga_full = gu_a[:, 0].reshape(total // 2, ff_loc)
+    ua_full = gu_a[:, 1].reshape(total // 2, ff_loc)
     part_a = over_width(ga_full, w_gate) + over_width(ua_full, w_up)
-    gn_a, gb_full, ub_full = pair_reduce_scatter(
-        part_a, "col", 4, [(gpre_b, "row", RG), (upre_b, "row", RG)]
-    )
-    gb_full = gb_full.reshape(total // 2, ff_loc)
-    ub_full = ub_full.reshape(total // 2, ff_loc)
+    gn_a, gu_b = pair_reduce_scatter(part_a, "col", 4, [(jnp.stack([gpre_b, upre_b]), "row", RG)])
+    gb_full = gu_b[:, 0].reshape(total // 2, ff_loc)
+    ub_full = gu_b[:, 1].reshape(total // 2, ff_loc)
     part_b = over_width(gb_full, w_gate) + over_width(ub_full, w_up)
     (gn_b,) = pair_reduce_scatter(part_b, "col", 6)
     grad_normed = jnp.concatenate([gn_a, gn_b], axis=0)

time: 340 us -> 351 us (1.032)
  Pallas kernels: 262 us -> 271 us
  local copies, waits for them, and re-layouts: 7.54 us -> 11.2 us
    pallas_call x9, Pallas kernels: 262 us -> 271 us  [exchange(): pl.pallas_call(functools.partial(_exchange_kernel, modes, axes), out_shap...]
    slice x0 -> x2, local copies, waits for them, and re-layouts: none -> 5.13 us  [the longest x1 2.58 us: per_device(): ua_full = gu_a[:, 1].reshape(total // 2, ff_loc)]
where the time goes in v18:
time: 351 us
  Pallas kernels  271 us (77%)
  matrix products  37.3 us (11%)
  other arithmetic  30.4 us (9%)
  local copies, waits for them, and re-layouts  11.2 us (3%)
    pallas_call x9, Pallas kernels, exchange(): pl.pallas_call(functools.partial(_exchange_kernel, modes, axes), out_shap...  271 us
    dot_general x5, matrix products, over_width(): lax.dot_general(left, right, (((1,), (1,)), ((), ())), preferred_element_...  20.5 us
    dot_general x3, matrix products, over_tokens(): lax.dot_general(left, right, (((0,), (0,)), ((), ())), preferred_element_...  16.7 us
    convert_element_type x2, other arithmetic, pair_reduce_scatter(): pair.astype(WIRE)  9.35 us

profile of v18, /device:TPU:64, one launch (start us, length us, event | category | flops | bytes accessed | tf_op | source)
XLA Modules:
  0.0 350.5 jit_solution(7721761980906643409)
XLA Ops:
  0.7 0.9 convert_reduce_fusion
  1.6 1.1 fusion.12
  3.3 7.8 %shard_map.129 = f32[8,1,144]{2,1,0:T(1,128)} custom-call(f32[1,144]{1,0:T(1,128)} %bitcast.85), custom_call_target="tpu_custom_call" | custom-call | tf_op jit(solution)/shard_map/pallas_call | solution.py:300
  12.6 1.8 fusion.14.refs_1_
  14.4 2.6 fusion.2.refs_1_
  17.0 51.6 %shard_map.130 = (bf16[2,8,128,1024]{3,2,1,0:T(8,128)(2,1)}, bf16[8,256,896]{2,1,0:T(8,128)(2,1)}) custom-call(bf16[128,1024]{1,0:T(8,128)(2,1)} %refs_0_.1, bf16[256,896]{1,0:T(8,128)(2,1)} %fusion.2.refs_1_), custom_call_target="tpu_custom_call" | custom-call | tf_op jit(solution)/shard_map/pallas_call | solution.py:300
  68.6 2.8 copy.27
  71.9 5.1 %convolution_convert_fusion = bf16[896,1024]{1,0:T(8,128)(2,1)} fusion(bf16[2048,896]{1,0:T(8,128)(2,1)S(1)} %bitcast.89, bf16[2048,1024]{1,0:T(8,128)(2,1)S(1)} %bitcast.74), kind=kOutput, calls=%fused_computation.9 | convolution fusion | flops 3759013888 | bytes 9699328 | tf_op jit(solution)/shard_map/dot_general | solution.py:20
  77.0 7.2 %fusion.26 = (bf16[2048,896]{1,0:T(8,128)(2,1)}, f32[2048,896]{1,0:T(8,128)}) fusion(bf16[2048,1024]{1,0:T(8,128)(2,1)S(1)} %bitcast.75, bf16[896,1024]{1,0:T(8,128)(2,1)S(1)} %copy-done), kind=kOutput, calls=%fused_computation.64 | convolution fusion | flops 3759931392 | bytes 17039360 | tf_op jit(solution)/shard_map/dot_general | solution.py:26
  84.2 68.9 %shard_map.131 = (bf16[8,256,896]{2,1,0:T(8,128)(2,1)}, bf16[2,8,128,1024]{3,2,1,0:T(8,128)(2,1)}) custom-call(bf16[2048,896]{1,0:T(8,128)(2,1)} %get-tuple-element.32.refs_0_, bf16[128,1024]{1,0:T(8,128)(2,1)} %fusion.14.refs_1_), custom_call_target="tpu_custom_call" | custom-call | tf_op jit(solution)/shard_map/pallas_call | solution.py:300
  153.1 2.9 select_reduce_fusion
  156.1 1.8 fusion.5
  159.9 44.5 %shard_map.132 = bf16[8,2,128,896]{3,2,1,0:T(8,128)(2,1)} custom-call(bf16[2,128,896]{2,1,0:T(8,128)(2,1)} %pad_maximum_fusion.2.refs_0_), custom_call_target="tpu_custom_call" | custom-call | tf_op jit(solution)/shard_map/pallas_call | solution.py:300
  204.4 2.6 fusion.23
  207.1 2.4 fusion.27
  209.4 4.3 %convolution_add_fusion.1 = f32[1024,1024]{1,0:T(8,128)} fusion(f32[1024,1024]{1,0:T(8,128)S(1)} %fusion.27, bf16[1024,896]{1,0:T(8,128)(2,1)S(1)} %bitcast.66, bf16[1024,896]{1,0:T(8,128)(2,1)S(1)} %copy-done.15), kind=kOutput, calls=%fused_computation.8 | convolution fusion | flops 1880096768 | bytes 12058624 | tf_op jit(solution)/shard_map/dot_general | solution.py:26
  213.7 5.1 %shard_map.133 = f32[8,64,1024]{2,1,0:T(8,128)} custom-call(f32[8,2,64,1024]{3,2,1,0:T(8,128)} %bitcast.64), custom_call_target="tpu_custom_call" | custom-call | tf_op jit(solution)/shard_map/pallas_call | solution.py:300
  218.8 4.6 %fusion.21 = (bf16[8,64,1024]{2,1,0:T(8,128)(2,1)}, f32[8,64,1024]{2,1,0:T(8,128)}) fusion(f32[8,64,1024]{2,1,0:T(8,128)} %shard_map.133, f32[8,2,64,1024]{3,2,1,0:T(8,128)} %bitcast.65, s32[]{:T(128)S(6)} %select_n.43), kind=kLoop, calls=%fused_computation.59 | loop fusion | flops 1048576 | bytes 7340036 | tf_op jit(solution)/shard_map/convert_element_type | solution.py:338
  223.4 53.9 %shard_map.134 = (bf16[8,64,1024]{2,1,0:T(8,128)(2,1)}, bf16[8,2,128,896]{3,2,1,0:T(8,128)(2,1)}) custom-call(bf16[8,64,1024]{2,1,0:T(8,128)(2,1)} %get-tuple-element.20.refs_0_, bf16[2,128,896]{2,1,0:T(8,128)(2,1)} %pad_maximum_fusion.3.refs_1_), custom_call_target="tpu_custom_call" | custom-call | tf_op jit(solution)/shard_map/pallas_call | solution.py:300
  277.3 2.6 fusion.22
  280.7 1.8 copy-done.11
  282.5 5.7 %convolution_convert_fusion.2 = bf16[1024,896]{1,0:T(8,128)(2,1)} fusion(bf16[2048,1024]{1,0:T(8,128)(2,1)S(1)} %bitcast.87, bf16[2048,896]{1,0:T(8,128)(2,1)S(1)} %bitcast.78), kind=kOutput, calls=%fused_computation.11 | convolution fusion | flops 3759013888 | bytes 9699328 | tf_op jit(solution)/shard_map/dot_general | solution.py:20
  289.0 5.9 %convolution_convert_fusion.1 = bf16[1024,896]{1,0:T(8,128)(2,1)} fusion(bf16[2048,1024]{1,0:T(8,128)(2,1)S(1)} %bitcast.88, bf16[2048,896]{1,0:T(8,128)(2,1)S(1)} %bitcast.77), kind=kOutput, calls=%fused_computation.10 | convolution fusion | flops 3759013888 | bytes 9699328 | tf_op jit(solution)/shard_map/dot_general | solution.py:20
  294.9 2.4 fusion.28
  297.3 4.4 %convolution_add_fusion = f32[1024,1024]{1,0:T(8,128)} fusion(f32[1024,1024]{1,0:T(8,128)S(1)} %fusion.28, bf16[1024,896]{1,0:T(8,128)(2,1)S(1)} %bitcast.71, bf16[1024,896]{1,0:T(8,128)(2,1)S(1)} %copy-done.16), kind=kOutput, calls=%fused_computation.7 | convolution fusion | flops 1880096768 | bytes 12058624 | tf_op jit(solution)/shard_map/dot_general | solution.py:26
  301.6 5.1 %shard_map.135 = f32[8,64,1024]{2,1,0:T(8,128)} custom-call(f32[8,2,64,1024]{3,2,1,0:T(8,128)} %bitcast.62), custom_call_target="tpu_custom_call" | custom-call | tf_op jit(solution)/shard_map/pallas_call | solution.py:300
  306.7 4.7 %fusion.20 = (bf16[8,64,1024]{2,1,0:T(8,128)(2,1)}, f32[8,64,1024]{2,1,0:T(8,128)}) fusion(f32[8,64,1024]{2,1,0:T(8,128)} %shard_map.135, f32[8,2,64,1024]{3,2,1,0:T(8,128)} %bitcast.63, s32[]{:T(128)S(6)} %select_n.43), kind=kLoop, calls=%fused_computation.58 | loop fusion | flops 1048576 | bytes 7340036 | tf_op jit(solution)/shard_map/convert_element_type | solution.py:338
  311.5 20.6 %shard_map.136 = bf16[8,64,1024]{2,1,0:T(8,128)(2,1)} custom-call(bf16[8,64,1024]{2,1,0:T(8,128)(2,1)} %get-tuple-element.18.refs_0_), custom_call_target="tpu_custom_call" | custom-call | tf_op jit(solution)/shard_map/pallas_call | solution.py:300
  332.1 1.8 select_reduce_fusion.2
  333.9 1.1 bitcast_add_fusion.2
  335.7 13.2 %shard_map.137 = f32[8,1,128]{2,1,0:T(1,128)} custom-call(f32[1,128]{1,0:T(1,128)} %bitcast.86), custom_call_target="tpu_custom_call" | custom-call | tf_op jit(solution)/shard_map/pallas_call | solution.py:300
  349.6 0.9 fusion.19
  (52 shorter events, 7.6 us)
Async XLA Ops:
  0.6 76.4 %copy-start = (bf16[896,1024]{1,0:T(8,128)(2,1)S(1)}, bf16[896,1024]{1,0:T(8,128)(2,1)}, u32[]{:S(2)}) copy-start(bf16[896,1024]{1,0:T(8,128)(2,1)} %param.19) | copy-start | bytes 5505028
  68.6 3.3 copy-start.12
  84.2 71.9 %copy-start.5 = (bf16[256,896]{1,0:T(8,128)(2,1)S(1)}, bf16[256,896]{1,0:T(8,128)(2,1)}, u32[]{:S(2)}) copy-start(bf16[256,896]{1,0:T(8,128)(2,1)} %param.12) | copy-start | bytes 1376260
  84.2 71.9 %copy-start.6 = (s32[256,896]{1,0:T(8,128)S(1)}, s32[256,896]{1,0:T(8,128)}, u32[]{:S(2)}) copy-start(s32[256,896]{1,0:T(8,128)} %param.14) | copy-start | bytes 2752516
  84.2 71.9 %copy-start.7 = (bf16[256,896]{1,0:T(8,128)(2,1)S(1)}, bf16[256,896]{1,0:T(8,128)(2,1)}, u32[]{:S(2)}) copy-start(bf16[256,896]{1,0:T(8,128)(2,1)} %param.13) | copy-start | bytes 1376260
  204.4 2.6 copy-start.13
  207.0 2.4 copy-start.2
  207.0 2.4 copy-start.15
  277.3 2.6 copy-start.3
  280.3 2.2 copy-start.11
  289.0 5.9 %copy-start.14 = (bf16[1024,896]{1,0:T(8,128)(2,1)S(1)}, bf16[1024,896]{1,0:T(8,128)(2,1)}, u32[]{:S(2)}) copy-start(bf16[1024,896]{1,0:T(8,128)(2,1)} %param.17) | copy-start | bytes 5505028
  294.9 2.4 copy-start.16
  306.7 25.4 %copy-start.8 = (bf16[8,64,1024]{2,1,0:T(8,128)(2,1)S(1)}, bf16[8,64,1024]{2,1,0:T(8,128)(2,1)}, u32[]{:S(2)}) copy-start(bf16[8,64,1024]{2,1,0:T(8,128)(2,1)} %get-tuple-element.12) | copy-start | bytes 3145732
  311.5 23.6 %copy-start.4 = (bf16[128,1024]{1,0:T(8,128)(2,1)S(1)}, bf16[128,1024]{1,0:T(8,128)(2,1)}, u32[]{:S(2)}) copy-start(bf16[128,1024]{1,0:T(8,128)(2,1)} %param.10) | copy-start | bytes 786436
  311.5 23.6 %copy-start.10 = (f32[1024]{0:T(1024)S(1)}, f32[1024]{0:T(1024)}, u32[]{:S(2)}) copy-start(f32[1024]{0:T(1024)} %param.16) | copy-start | bytes 12292
  311.5 38.1 %copy-start.9 = (bf16[128,1024]{1,0:T(8,128)(2,1)S(1)}, bf16[128,1024]{1,0:T(8,128)(2,1)}, u32[]{:S(2)}) copy-start(bf16[128,1024]{1,0:T(8,128)(2,1)} %refs_0_.1) | copy-start | bytes 786436
  311.5 39.1 %copy-start.1 = (bf16[896,1024]{1,0:T(8,128)(2,1)S(1)}, bf16[896,1024]{1,0:T(8,128)(2,1)}, u32[]{:S(2)}) copy-start(bf16[896,1024]{1,0:T(8,128)(2,1)} %param.19) | copy-start | bytes 5505028
